TPU v7x, 256 devices: a whole 4x4x8 slice. The times are simulated.
256 devices in a mesh: chan: 64 (over x, y_hi, z), stn: 4 (over y_lo, core).
Axes of the slice: x: 4, y: 4 (y_hi: 2, y_lo: 2; y = y_hi * 2 + y_lo), z: 8, core: 2. Of those that a mesh axis runs over, the one named last changes fastest.
Arguments:
- gains: float32 [128, 2, 2, 2, 16, 512], P('chan', None, None, None, None, 'stn'), may hold values from -2.1 to 2.1
- coherency: bfloat16 [128, 16, 2, 512, 512], P('chan', None, None, 'stn'), may hold values from -1.5 to 1.5
- vis_data: bfloat16 [128, 2, 2, 2, 512, 512], P('chan', None, None, None, 'stn'), may hold values from -6 to 6
- flags: int32 [128, 32, 32], P('chan', 'stn'), may hold values 0 or 1
- beam: float32 [8, 16], replicated, may hold values from 0.5 to 2
- group_of: int32 [512], replicated, may hold values from 0 to 7
Outputs:
- gain_step: float32 [128, 2, 2, 2, 16, 512], P('chan', None, None, None, None, 'stn')
- loss_value: float32 [], replicated
All inputs are finite; a program needn't handle non-finite values. No bound on the sum of `flags` on one device may be relied on, other than what follows from the above.
Results may differ from a plain program's by a relative error of at most 0.0003.
Values sent between devices are 32-bit elements; how exact they have to be, the bound alone decides.
No kernel may reach another device: no remote copies, remote signals or barrier semaphores. Data moves between devices by JAX's collectives and lax.ppermute only.
A program may use at most 128 MiB of HBM per device.

v0:
```python
import jax
import jax.numpy as jnp
from jax import lax
from jax.sharding import Mesh
from jax.sharding import PartitionSpec as P

BLK = 16
STN = ("stn_0", "stn_1")
CHAN = ("chan_0", "chan_1", "chan_2")
CHAN_STN = ("chan_0", "chan_1", "chan_2", "stn_0", "stn_1")


smooth_weight = 0.05
damping = 0.3


def in_order(parts, dim):
    shape = list(parts.shape[1:])
    shape[dim] *= parts.shape[0]
    return jnp.moveaxis(parts, 0, dim).reshape(shape)


def copy_for_each(shard, axis):
    copies = jnp.broadcast_to(shard, (lax.axis_size(axis), *shard.shape))
    return lax.all_to_all(copies, axis, split_axis=0, concat_axis=0, tiled=True)


def collect(shard, axis, dim):
    return in_order(copy_for_each(shard, axis), dim)


def cut_along(shard, dim, peers):
    shape = shard.shape
    parts = shard.reshape(*shape[:dim], peers, shape[dim] // peers, *shape[dim + 1 :])
    return jnp.moveaxis(parts, dim, 0)


def summed_on_arrival(shard, axis, dim):
    peers = lax.axis_size(axis)
    parts = lax.all_to_all(cut_along(shard, dim, peers), axis, 0, 0, tiled=True)
    return jnp.sum(parts, axis=0)


def padded(cells, sides, width):
    for axis, dim in sides:
        count = lax.axis_size(axis)
        ends = count - 1
        head = lax.slice_in_dim(cells, 0, width, axis=dim)
        tail = lax.slice_in_dim(cells, cells.shape[dim] - width, cells.shape[dim], axis=dim)
        cells = jnp.concatenate(
            [
                lax.ppermute(tail, axis, [(i, (i + 1) % count) for i in range(ends)]),
                cells,
                lax.ppermute(head, axis, [((i + 1) % count, i) for i in range(ends)]),
            ],
            axis=dim,
        )
    return cells


def over_axes(shard, axes):
    for axis in axes:
        shard = lax.psum(shard, axis)
    return shard


def beam_factor(beam, group_of):
    groups = beam.shape[0]
    onehot = (group_of[None, :] == jnp.arange(groups, dtype=jnp.int32)[:, None]).astype(jnp.float32)
    return jnp.sum(beam[:, :, None] * onehot[:, None, :], axis=0)


def expand_flags(flags):
    chans, first, second = flags.shape
    wide = jnp.broadcast_to(
        flags.astype(jnp.float32)[:, :, None, :, None], (chans, first, BLK, second, BLK)
    )
    return wide.reshape(chans, first * BLK, second * BLK)


def outer_product(row_dir, col_dir):
    row_real = row_dir[:, 0][:, :, None, :, :, None]
    row_imag = row_dir[:, 1][:, :, None, :, :, None]
    col_real = col_dir[:, 0][:, None, :, :, None, :]
    col_imag = col_dir[:, 1][:, None, :, :, None, :]
    real_part = jnp.sum(row_real * col_real + row_imag * col_imag, axis=3)
    imag_part = jnp.sum(row_imag * col_real - row_real * col_imag, axis=3)
    return (real_part, imag_part)


def block_terms(coherency, vis_data, weight, row_gains, col_gains):
    count_dirs = row_gains.shape[4]
    chans, row_total, col_total = weight.shape
    empty = jnp.zeros((chans, 2, 2, row_total, col_total), jnp.float32)

    def model_turn(state_pair, dir_index):
        coh_dir = lax.dynamic_index_in_dim(coherency, dir_index, 1, False).astype(jnp.float32)
        coh_real = coh_dir[:, 0][:, None, None]
        coh_imag = coh_dir[:, 1][:, None, None]
        row_dir = lax.dynamic_index_in_dim(row_gains, dir_index, 4, False)
        col_dir = lax.dynamic_index_in_dim(col_gains, dir_index, 4, False)
        outer_real, outer_imag = outer_product(row_dir, col_dir)
        model_real = state_pair[0] + coh_real * outer_real - coh_imag * outer_imag
        model_imag = state_pair[1] + coh_real * outer_imag + coh_imag * outer_real
        return ((model_real, model_imag), None)

    dir_list = jnp.arange(count_dirs, dtype=jnp.int32)
    (model_real, model_imag), _ = lax.scan(model_turn, (empty, empty), dir_list)
    observed = vis_data.astype(jnp.float32)
    res_real = weight[:, None, None] * (observed[:, 0] - model_real)
    res_imag = weight[:, None, None] * (observed[:, 1] - model_imag)
    total_sq = jnp.sum(res_real * res_real + res_imag * res_imag)
    wide_real = res_real[:, :, :, None]
    wide_imag = res_imag[:, :, :, None]

    def gradient_turn(state_dummy, dir_index):
        coh_dir = lax.dynamic_index_in_dim(coherency, dir_index, 1, False).astype(jnp.float32)
        coh_real = coh_dir[:, 0][:, None, None]
        coh_imag = coh_dir[:, 1][:, None, None]
        row_dir = lax.dynamic_index_in_dim(row_gains, dir_index, 4, False)
        col_dir = lax.dynamic_index_in_dim(col_gains, dir_index, 4, False)
        col_real = col_dir[:, 0][:, None, :, :, None, :]
        col_imag = col_dir[:, 1][:, None, :, :, None, :]
        prod_real = jnp.sum(wide_real * col_real - wide_imag * col_imag, axis=2)
        prod_imag = jnp.sum(wide_real * col_imag + wide_imag * col_real, axis=2)
        row_grad_real = -jnp.sum(coh_real * prod_real + coh_imag * prod_imag, axis=-1)
        row_grad_imag = -jnp.sum(coh_real * prod_imag - coh_imag * prod_real, axis=-1)
        row_real = row_dir[:, 0][:, :, None, :, :, None]
        row_imag = row_dir[:, 1][:, :, None, :, :, None]
        herm_real = jnp.sum(wide_real * row_real + wide_imag * row_imag, axis=1)
        herm_imag = jnp.sum(wide_real * row_imag - wide_imag * row_real, axis=1)
        col_grad_real = -jnp.sum(coh_real * herm_real - coh_imag * herm_imag, axis=-2)
        col_grad_imag = -jnp.sum(coh_real * herm_imag + coh_imag * herm_real, axis=-2)
        power = weight * (coh_dir[:, 0] * coh_dir[:, 0] + coh_dir[:, 1] * coh_dir[:, 1])
        col_norm = jnp.sum(col_dir * col_dir, axis=(1, 2, 3))
        row_norm = jnp.sum(row_dir * row_dir, axis=(1, 2, 3))
        row_curv = jnp.sum(power * col_norm[:, None, :], axis=-1)
        col_curv = jnp.sum(power * row_norm[:, :, None], axis=-2)
        row_grad = jnp.stack([row_grad_real, row_grad_imag], axis=1)
        col_grad = jnp.stack([col_grad_real, col_grad_imag], axis=1)
        return (state_dummy, (row_grad, row_curv, col_grad, col_curv))

    _, stacked = lax.scan(gradient_turn, jnp.float32(0.0), dir_list)
    row_grad = jnp.moveaxis(stacked[0], 0, 4)
    row_curv = jnp.moveaxis(stacked[1], 0, 1)
    col_grad = jnp.moveaxis(stacked[2], 0, 4)
    col_curv = jnp.moveaxis(stacked[3], 0, 1)
    return (total_sq, row_grad, row_curv, col_grad, col_curv)


def on_device(gains, coherency, vis_data, flags, beam, group_of):
    chan_dev = gains.shape[0]
    row_count = gains.shape[5]
    stn_count = lax.axis_size(STN)
    stn_index = lax.axis_index(STN)
    all_stations = row_count * stn_count
    all_channels = chan_dev * lax.axis_size(CHAN)
    factor = beam_factor(beam, group_of)
    row_factor = lax.dynamic_slice_in_dim(factor, stn_index * row_count, row_count, 1)
    row_gains = gains * row_factor
    row_ids = stn_index * row_count + jnp.arange(row_count, dtype=jnp.int32)
    col_ids = jnp.arange(all_stations, dtype=jnp.int32)
    weight = expand_flags(flags) * (row_ids[:, None] != col_ids[None, :]).astype(jnp.float32)[None]
    local_count = jnp.sum(weight)
    all_gains = collect(row_gains, STN, 5)
    total_sq, row_grad, row_curv, col_grad, col_curv = block_terms(
        coherency, vis_data, weight, row_gains, all_gains
    )
    own_grad, own_curv = (summed_on_arrival(col_grad, STN, 5), summed_on_arrival(col_curv, STN, 2))
    extended = padded(gains, ((CHAN, 0),), 2)
    second = extended[2:] - 2.0 * extended[1:-1] + extended[:-2]
    first_chan = lax.axis_index(CHAN) * chan_dev
    positions = first_chan - 1 + jnp.arange(chan_dev + 2, dtype=jnp.int32)
    inside = ((positions >= 1) & (positions <= all_channels - 2)).astype(jnp.float32)
    second = second * inside[:, None, None, None, None, None]
    smooth_grad = second[:-2] - 2.0 * second[1:-1] + second[2:]
    own_second = second[1:-1]
    smooth_local = jnp.sum(own_second * own_second)
    count_total, sq_total, smooth_total = (
        over_axes(local_count, CHAN_STN),
        over_axes(total_sq, CHAN_STN),
        over_axes(smooth_local, CHAN_STN),
    )
    norm_scale = all_channels * all_stations / count_total
    gradient = norm_scale * row_factor * (row_grad + own_grad) + smooth_weight * smooth_grad
    curvature = norm_scale * row_factor * row_factor * (row_curv + own_curv) + damping
    gain_step = gradient / curvature[:, None, None, None]
    loss_value = (norm_scale * sq_total + smooth_weight * smooth_total) / (
        all_channels * all_stations
    )
    return (gain_step, loss_value)


def solution(mesh):
    split = Mesh(
        mesh.devices.reshape(4, 2, 8, 2, 2), ("chan_0", "chan_1", "chan_2", "stn_0", "stn_1")
    )
    in_specs = (
        P(CHAN, None, None, None, None, STN),
        P(CHAN, None, None, STN, None),
        P(CHAN, None, None, None, STN, None),
        P(CHAN, STN, None),
        P(),
        P(),
    )
    out_specs = (P(CHAN, None, None, None, None, STN), P())
    return jax.shard_map(
        on_device, mesh=split, in_specs=in_specs, out_specs=out_specs, check_vma=False
    )
```

profile of v0, /device:TPU:1, one launch (start us, length us, event | category | flops | bytes accessed | tf_op | source)
XLA Modules:
  0.0 684.5 jit_solution(3169094442952550494)
XLA Ops:
  3.6 5.6 collective-permute-start.1
  13.1 6.2 all-to-all-start
  30.0 7.7 %copy.57 = bf16[2,16,2,128,512]{4,3,0,2,1:T(8,128)(2,1)} copy(bf16[2,16,2,128,512]{4,3,2,1,0:T(8,128)(2,1)} %param.11) | data formatting | bytes 16777216
  41.8 215.3 %while.31 = (s32[]{:T(128)}, f32[2,2,2,128,512]{4,3,2,1,0:T(8,128)}, f32[2,2,2,128,512]{4,3,2,1,0:T(8,128)}, s32[16]{0:T(128)S(1)}, bf16[2,16,2,128,512]{4,3,0,2...) while((s32[]{:T(128)}, ...), condition=%wide.region_10.11_spmd.clone, body=%wide.region_7.10_spmd.clone.sunk | while | flops 12845062 | bytes 21700776 | solution.py:108
  61.6 6.0 fusion.27
  75.1 6.0 fusion.27
  88.7 6.0 fusion.27
  102.2 6.0 fusion.27
  115.7 6.0 fusion.27
  129.3 6.0 fusion.27
  142.8 6.0 fusion.27
  156.3 6.0 fusion.27
  169.9 6.0 fusion.27
  183.4 6.0 fusion.27
  196.9 6.0 fusion.27
  210.5 6.0 fusion.27
  224.0 6.0 fusion.27
  237.5 6.0 fusion.27
  251.0 6.0 fusion.27
  257.1 6.7 add_reduce_fusion.5
  264.3 353.1 %while.30 = (s32[]{:T(128)}, f32[16,2,2,2,2,128]{5,4,3,2,1,0:T(2,128)}, f32[16,2,128]{2,1,0:T(2,128)}, f32[16,2,2,2,2,512]{5,4,3,1,2,0:T(2,128)}, f32[16,2,512]{...) while((s32[]{:T(128)}, ...), condition=%wide.region_24.25_spmd.clone, body=%wide.region_11.24_spmd.clone.sunk | while | flops 24538628 | bytes 29537488 | solution.py:143
  278.8 5.1 reshape.150
  300.9 5.1 reshape.150
  323.0 5.1 reshape.150
  345.0 5.1 reshape.150
  389.2 5.1 reshape.150
  411.2 5.1 reshape.150
  433.3 5.1 reshape.150
  630.9 13.5 %all-reduce.1 = (f32[]{:T(128)}, f32[]{:T(128)}, f32[]{:T(128)}) all-reduce(f32[]{:T(128)} %multiply_reduce_fusion.4, f32[]{:T(128)} %get-tuple-element.364, f32[]{:T(128)} %multiply_reduce_fusion.6), channel_id=1, replica_groups=mesh['chan_0'=4,'chan_1'=2,'chan_2'=8,'stn_0'=2,'stn_1'=2] {'chan_0'}, use_global_device_ids=true, to_apply=%region_1.0 | all-reduce | flops 3 | bytes 24 | tf_op jit(solution)/shard_map/psum | solution.py:63
  644.4 6.0 all-reduce.4
  650.3 13.9 %all-reduce = (f32[]{:T(128)}, f32[]{:T(128)}, f32[]{:T(128)}) all-reduce(f32[]{:T(128)} %get-tuple-element.339, f32[]{:T(128)} %get-tuple-element.340, f32[]{:T(128)} %get-tuple-element.341), channel_id=1, replica_groups=mesh['chan_0'=4,'chan_1'=2,'chan_2'=8,'stn_0'=2,'stn_1'=2] {'chan_2'}, use_global_device_ids=true, to_apply=%region_3.4 | all-reduce | flops 3 | bytes 24 | tf_op jit(solution)/shard_map/psum | solution.py:63
  668.7 10.7 %all-reduce.2 = (f32[]{:T(128)}, f32[]{:T(128)}, f32[]{:T(128)}) all-reduce(f32[]{:T(128)} %get-tuple-element.336, f32[]{:T(128)} %get-tuple-element.337, f32[]{:T(128)} %get-tuple-element.338), channel_id=1, replica_groups=mesh['chan_0'=4,'chan_1'=2,'chan_2'=8,'stn_0'=2,'stn_1'=2] {'stn_1'}, use_global_device_ids=true, to_apply=%region_5.6 | all-reduce | flops 3 | bytes 24 | tf_op jit(solution)/shard_map/psum | solution.py:63
  (470 shorter events, 427.6 us)
Async XLA Ops:
  0.6 18.8 %copy-start.4 = (s32[2,8,32]{2,1,0:T(8,128)S(1)}, s32[2,8,32]{2,1,0:T(8,128)}, u32[]{:S(2)}) copy-start(s32[2,8,32]{2,1,0:T(8,128)} %param.13) | copy-start | bytes 6148
  2.3 620.2 %collective-permute-start = (f32[2,2,2,2,16,128]{5,3,2,1,0,4:T(2,128)}, f32[2,2,2,2,16,128]{5,3,2,1,0,4:T(2,128)}, u32[]{:S(2)}, u32[]{:S(2)}) collective-permute-start(f32[2,2,2,2,16,128]{5,3,2,1,0,4:T(2,128)} %copy.64), channel_id=1, source_target_pairs={{4,0},{8,4},{12,8},{16,12},{20,16},{24,20},{28,24},{32,28},{36,32}... | collective-permute-start | bytes 393224 | tf_op jit(solution)/shard_map/ppermute | solution.py:54
  3.6 618.9 %collective-permute-start.1 = (f32[2,2,2,2,16,128]{5,3,2,1,0,4:T(2,128)}, f32[2,2,2,2,16,128]{5,3,2,1,0,4:T(2,128)}, u32[]{:S(2)}, u32[]{:S(2)}) collective-permute-start(f32[2,2,2,2,16,128]{5,3,2,1,0,4:T(2,128)} %copy.64), channel_id=1, source_target_pairs={{0,4},{4,8},{8,12},{12,16},{16,20},{20,24},{24,28},{28,32},{32,36}... | collective-permute-start | bytes 393224 | tf_op jit(solution)/shard_map/ppermute | solution.py:52
  10.7 0.6 copy-start.2
  13.1 27.2 %all-to-all-start = ((f32[4,2,2,2,2,16,128]{6,5,4,3,2,1,0:T(8,128)}), f32[4,2,2,2,2,16,128]{6,5,4,3,2,1,0:T(8,128)S(1)}, u32[]{:S(2)}, u32[]{:S(2)}) async-start(f32[4,2,2,2,2,16,128]{6,5,4,3,2,1,0:T(8,128)} %broadcast_in_dim.68), calls=%async_computation | async-start | bytes 1048576 | tf_op jit(solution)/shard_map/all_to_all | solution.py:25
  30.0 7.8 %copy-start = (bf16[2,2,2,2,128,512]{5,4,3,2,1,0:T(8,128)(2,1)S(1)}, bf16[2,2,2,2,128,512]{5,4,3,2,1,0:T(8,128)(2,1)}, u32[]{:S(2)}) copy-start(bf16[2,2,2,2,128,512]{5,4,3,2,1,0:T(8,128)(2,1)} %param.12) | copy-start | bytes 6291460
  619.0 63.1 %copy-start.3 = (f32[16,2,128]{2,1,0:T(2,128)S(1)}, f32[16,2,128]{2,1,0:T(2,128)}, u32[]{:S(2)}) copy-start(f32[16,2,128]{2,1,0:T(2,128)} %get-tuple-element.109) | copy-start | bytes 49156
  619.0 7.6 %all-to-all-start.2 = ((f32[4,2,16,128]{3,1,2,0:T(2,128)}), f32[4,2,16,128]{3,1,2,0:T(2,128)S(1)}, u32[]{:S(2)}, u32[]{:S(2)}) async-start(f32[4,2,16,128]{3,1,2,0:T(2,128)} %copy.69), calls=%async_computation.2 | async-start | bytes 131072 | tf_op jit(solution)/shard_map/all_to_all | solution.py:40
  624.0 58.5 %copy-start.1 = (f32[16,2,2,2,2,128]{5,4,3,2,1,0:T(2,128)S(1)}, f32[16,2,2,2,2,128]{5,4,3,2,1,0:T(2,128)}, u32[]{:S(2)}) copy-start(f32[16,2,2,2,2,128]{5,4,3,2,1,0:T(2,128)} %get-tuple-element.107) | copy-start | bytes 393220
  626.6 55.5 %all-to-all-start.1 = ((f32[4,2,2,2,2,16,128]{6,4,3,2,1,5,0:T(2,128)}), f32[4,2,2,2,2,16,128]{6,4,3,2,1,5,0:T(2,128)S(1)}, u32[]{:S(2)}, u32[]{:S(2)}) async-start(f32[4,2,2,2,2,16,128]{6,4,3,2,1,5,0:T(2,128)} %copy.61), calls=%async_computation.1 | async-start | bytes 1048576 | tf_op jit(solution)/shard_map/all_to_all | solution.py:40
where the time goes:
time: 691 us; the launch traced here: 684 us
  other arithmetic  346 us (50%)
  local copies, waits for them, and re-layouts  209 us (30%)
  loops' own time  56.6 us (8%)
  blocking collectives  48.6 us (7%)
  starting transfers between devices  20 us (3%)
    add x16, other arithmetic, model_turn(): model_imag = state_pair[1] + coh_real * outer_imag + coh_imag * outer_real  94.9 us
    reshape x17, local copies, waits for them, and re-layouts, expand_flags(): return wide.reshape(chans, first * BLK, second * BLK)  86.2 us
    reduce_sum x16, other arithmetic, gradient_turn(): herm_imag = jnp.sum(wide_real * row_imag - wide_imag * row_real, axis=1)  71.3 us
    reduce_sum x16, other arithmetic, outer_product(): real_part = jnp.sum(row_real * col_real + row_imag * col_imag, axis=3)  48.9 us
    psum x5, blocking collectives, over_axes(): shard = lax.psum(shard, axis)  48.6 us
    broadcast_in_dim x17, local copies, waits for them, and re-layouts, expand_flags(): jnp.broadcast_to(flags.astype(jnp.float32)[:, :, None, :, None], (chans,...  43.7 us
    another operation x1, loops' own time, block_terms(): (model_real, model_imag), _ = lax.scan(model_turn, (empty, empty), dir_list)  29.5 us
    dynamic_slice x32, local copies, waits for them, and re-layouts, block_terms(): (model_real, model_imag), _ = lax.scan(model_turn, (empty, empty), dir_list)  28.3 us
  transfers between devices with their start and end apart: 5, of which 0 were waited for; matrix products, arithmetic and copies ran while one was open for 81% of the time, Pallas kernels for 0%

commit v1 on v0

v1 whole, which is shorter than its diff:
```python
import jax
import jax.numpy as jnp
import numpy as np
from jax import lax
from jax.experimental import pallas as pl
from jax.experimental.pallas import tpu as pltpu
from jax.sharding import PartitionSpec as P


BF = jnp.bfloat16
F32 = jnp.float32
BLK = 16
CHAN = "chan"
STN = "stn"
ALL = ("chan", "stn")
smooth_weight = 0.05
damping = 0.3


def selections():
    sel_w = np.zeros((64, 16), np.float32)
    sel_l = np.zeros((2, 16, 16), np.float32)
    for s in range(2):
        for t in range(2):
            for i in range(2):
                for r in range(2):
                    kk = ((s * 2 + t) * 2 + i) * 2 + r
                    for a in range(2):
                        sel_l[a, s * 8 + r * 4 + a * 2 + i, kk] = 1.0
                        sel_w[a * 16 + kk, t * 8 + r * 4 + a * 2 + i] = 1.0
                        sel_w[32 + a * 16 + kk, t * 8 + (1 - r) * 4 + a * 2 + i] = -1.0 if r == 0 else 1.0
    sel_c = np.zeros((2, 16, 16), np.float32)
    sel_q = np.zeros((4, 16, 16), np.float32)
    for s in range(2):
        for a in range(2):
            for i in range(2):
                re, im = s * 8 + a * 2 + i, s * 8 + 4 + a * 2 + i
                sel_c[a, s * 8 + i, re] = -1.0
                sel_c[a, s * 8 + 2 + i, im] = -1.0
                sel_c[a, s * 8 + 4 + i, im] = -1.0
                sel_c[a, s * 8 + 6 + i, re] = 1.0
                for half in range(2):
                    row = s * 8 + half * 4 + i
                    sel_q[a * 2, row, re] = -1.0
                    sel_q[a * 2, row + 2, im] = -1.0
                    sel_q[a * 2 + 1, row, im] = 1.0
                    sel_q[a * 2 + 1, row + 2, re] = -1.0
    w2 = np.concatenate([sel_w, sel_q.reshape(64, 16)], axis=0)
    return w2, sel_l, sel_c.reshape(32, 16)


def dot(a, b):
    return jnp.dot(a, b, preferred_element_type=F32)


def dot_t(a, b):
    return lax.dot_general(a, b, (((1,), (1,)), ((), ())), preferred_element_type=F32)


def dot_l(a, b):
    return lax.dot_general(a, b, (((0,), (0,)), ((), ())), preferred_element_type=F32)


def split(x):
    high = x.astype(BF)
    return high, (x - high.astype(F32)).astype(BF)


def parts_of(x):
    high = x.astype(BF).astype(F32)
    return jnp.concatenate([high, x - high], axis=0).astype(BF)


K = 16
ROWS = 128
LANES = 128
TILES = ROWS // 16


def weights_of(first, flags, wgt, groups):
    blocks, cols = flags.shape
    rows8 = lax.broadcasted_iota(jnp.int32, (ROWS, blocks), 0) // 16 == lax.broadcasted_iota(jnp.int32, (ROWS, blocks), 1)
    wide = dot(rows8.astype(F32).astype(BF), flags.astype(F32).astype(BF)).astype(BF)
    for g in range(groups):
        at = (lax.broadcasted_iota(jnp.int32, (cols, LANES), 1) + g * LANES) // 16
        at = at == lax.broadcasted_iota(jnp.int32, (cols, LANES), 0)
        full = dot(wide, at.astype(F32).astype(BF))
        row_id = lax.broadcasted_iota(jnp.int32, (ROWS, LANES), 0) + first
        col_id = lax.broadcasted_iota(jnp.int32, (ROWS, LANES), 1) + g * LANES
        wgt[:, g * LANES:(g + 1) * LANES] = jnp.where(row_id == col_id, 0.0, full)


def model_operands(f, jall, jrow, w2, sell, wr, wi, lr):
    groups = jall.shape[0]

    def turn(k, _):
        for g in range(groups):
            w = dot(w2[0:64], parts_of(jall[g, f, pl.ds(k, 8, stride=16), :])).astype(BF)
            for b in range(2):
                wr[k, g, :, b * 128:(b + 1) * 128] = w[b * 16:(b + 1) * 16]
                wi[k, g, :, b * 128:(b + 1) * 128] = w[32 + b * 16:48 + b * 16]
        hm = parts_of(jrow[f, pl.ds(k, 8, stride=16), :])
        for a in range(2):
            l = dot_l(hm, sell[a]).astype(BF)
            for t in range(TILES):
                lr[k, t, a * 16:(a + 1) * 16, :] = l[t * 16:(t + 1) * 16]
        return 0

    lax.fori_loop(0, K, turn, 0)


def model(f, coh, vis, wgt, res, wr, wi, lr, groups):
    def turn(t, sq):
        rows = pl.ds(pl.multiple_of(t * 16, 16), 16)
        for g in range(groups):
            cols = slice(g * 128, (g + 1) * 128)
            acc = [[[jnp.zeros((16, 128), F32)] * 2 for _ in range(2)] for _ in range(2)]
            for k in range(K):
                o_re = dot(lr[k, t], wr[k, g])
                o_im = dot(lr[k, t], wi[k, g])
                c_re = coh[f, k, 0, rows, cols].astype(F32)
                c_im = coh[f, k, 1, rows, cols].astype(F32)
                for a in range(2):
                    for b in range(2):
                        re = o_re[a * 16:(a + 1) * 16, b * 128:(b + 1) * 128]
                        im = o_im[a * 16:(a + 1) * 16, b * 128:(b + 1) * 128]
                        acc[a][b] = [acc[a][b][0] + c_re * re - c_im * im,
                                     acc[a][b][1] + c_re * im + c_im * re]
            w = wgt[rows, cols]
            for a in range(2):
                for b in range(2):
                    for r in range(2):
                        v = w * (vis[f, r, a, b, rows, cols].astype(F32) - acc[a][b][r])
                        res[b, r, pl.ds(pl.multiple_of(a * ROWS + t * 16, 16), 16), cols] = v
                        sq = sq + v * v
        return sq

    sq = lax.fori_loop(0, TILES, turn, jnp.zeros((16, 128), F32))
    return sq[:8] + sq[8:]


def norms(x):
    return parts_of(jnp.broadcast_to(jnp.sum(x * x, axis=0, keepdims=True), (8, LANES)))


def gradient_operands(f, jall, jrow, w2, selc, lq, lc, nq, nr):
    groups = jall.shape[0]
    span = groups * LANES

    def turn(k, _):
        for g in range(groups):
            x = jall[g, f, pl.ds(k, 8, stride=16), :]
            w = dot(w2[64:128], parts_of(x)).astype(BF)
            for j in range(4):
                lq[k, :, j * span + g * 128:j * span + (g + 1) * 128] = w[j * 16:j * 16 + 16]
            nq[k, :, g * 128:(g + 1) * 128] = norms(x)
        x = jrow[f, pl.ds(k, 8, stride=16), :]
        c = dot(selc[...], parts_of(x)).astype(BF)
        for a in range(2):
            lc[k, :, a * 128:(a + 1) * 128] = c[a * 16:(a + 1) * 16]
        nr[k] = norms(x)
        return 0

    lax.fori_loop(0, K, turn, 0)


def gradient(f, coh, wgt, res, lq, lc, nq, nr, bufs, row, col, groups):
    span = groups * LANES
    halves = groups // 2

    def fill(k, t, h, y, am):
        cols = slice(h * 256, (h + 1) * 256)
        rows = slice(t * 16, (t + 1) * 16)
        c_re = coh[f, k, 0, rows, cols].astype(F32)
        c_im = coh[f, k, 1, rows, cols].astype(F32)
        for a in range(2):
            at = slice(a * ROWS + t * 16, a * ROWS + t * 16 + 16)
            for b in range(2):
                r_re = res[b, 0, at, cols]
                r_im = res[b, 1, at, cols]
                for r, v in ((0, c_re * r_re + c_im * r_im), (1, c_re * r_im - c_im * r_re)):
                    high, low = split(v)
                    y[b * 2 + r, h, 0, at, :] = high
                    y[b * 2 + r, h, 1, at, :] = low
        high, low = split(wgt[rows, cols] * (c_re * c_re + c_im * c_im))
        am[h, rows, :] = high
        am[h, ROWS + t * 16:ROWS + t * 16 + 16, :] = low

    top = lax.broadcasted_iota(jnp.int32, (8, 128), 0) < 4

    def reduce_part(k, j, h, s, y, cell):
        tile = y[j, h, s]
        c = dot(lc[k], tile)
        r = dot_t(lq[k, :, j * span + h * 256:j * span + (h + 1) * 256], tile)
        c = c[:8] + c[8:]
        cell[0][j, h] = c if s == 0 else cell[0][j, h] + c
        cell[1] = r if cell[1] is None else cell[1] + r

    def reduce_end(k, am, cell):
        r = cell[1][:8] + cell[1][8:]
        row[pl.ds(k, 8, stride=16), :] = jnp.where(top, r[:, :ROWS], r[:, ROWS:])
        for g in range(groups):
            h, cols = g // 2, slice(g % 2 * 128, g % 2 * 128 + 128)
            c = [cell[0][j, h][:, cols] for j in range(4)]
            t0 = c[0] + pltpu.roll(c[1], 4, 0)
            t1 = pltpu.roll(c[2], 4, 0) + c[3]
            col[g, pl.ds(k, 8, stride=16), :] = jnp.where(top, t0, t1)
        total = None
        n_row = jnp.concatenate([nr[k], nr[k]], axis=1)
        for h in range(halves):
            tile = am[h]
            cc = dot(n_row, tile)
            cc = cc[0:1] + cc[8:9]
            for g in range(2):
                col[h * 2 + g, pl.ds(128 + k, 1), :] = cc[:, g * 128:(g + 1) * 128]
            cr = dot_t(nq[k, :, h * 256:(h + 1) * 256], tile)
            cr = cr[0:1] + cr[8:9]
            cr = cr[:, :ROWS] + cr[:, ROWS:]
            total = cr if total is None else total + cr
        row[pl.ds(128 + k, 1), :] = total

    fills = [(t, h) for t in range(TILES) for h in range(halves)]
    dots = [(j, h, s) for j in range(4) for h in range(halves) for s in range(2)]
    (y0, a0), (y1, a1) = bufs
    for t, h in fills:
        fill(0, t, h, y0, a0)

    def pair(i, _):
        for step, (y, am, y_next, am_next) in enumerate(((y0, a0, y1, a1), (y1, a1, y0, a0))):
            k = 2 * i + step
            k_next = jnp.minimum(k + 1, K - 1)
            cell = [{}, None]
            for (t, h), part in zip(fills, dots):
                reduce_part(k, *part, y, cell)
                fill(k_next, t, h, y_next, am_next)
            reduce_end(k, am, cell)
        return 0

    lax.fori_loop(0, K // 2, pair, 0)


def operand_scratch(G):
    S = G * 128
    return dict(
        model=[pltpu.VMEM((K, G, 16, 256), BF), pltpu.VMEM((K, G, 16, 256), BF), pltpu.VMEM((K, TILES, 32, 16), BF)],
        grad=[pltpu.VMEM((K, 16, 4 * S), BF), pltpu.VMEM((K, 16, 2 * ROWS), BF), pltpu.VMEM((K, 16, S), BF), pltpu.VMEM((K, 16, ROWS), BF)],
        bufs=[pltpu.VMEM((4, G // 2, 2, 2 * ROWS, 256), BF), pltpu.VMEM((G // 2, 2 * ROWS, 256), BF)] * 2,
    )


def front(first, jall, jrow, coh, vis, flags, w2, sell, selc, row, col, res1, wgt1, sq, res0, wgt0, wr, wi, lr, lq, lc, nq, nr, y0, a0, y1, a1):
    G = jall.shape[0]
    total = None
    for f, (res, wgt) in enumerate(((res0, wgt0), (res1, wgt1))):
        weights_of(first[0], flags[f], wgt, G)
        model_operands(f, jall, jrow, w2, sell, wr, wi, lr)
        part = model(f, coh, vis, wgt, res, wr, wi, lr, G)
        total = part if total is None else total + part
    sq[...] = total
    gradient_operands(0, jall, jrow, w2, selc, lq, lc, nq, nr)
    gradient(0, coh, wgt0, res0, lq, lc, nq, nr, ((y0, a0), (y1, a1)), row, col, G)


def back(jall, jrow, coh, res, wgt, w2, selc, row, col, lq, lc, nq, nr, y0, a0, y1, a1):
    G = jall.shape[0]
    gradient_operands(1, jall, jrow, w2, selc, lq, lc, nq, nr)
    gradient(0, coh, wgt, res, lq, lc, nq, nr, ((y0, a0), (y1, a1)), row, col, G)


def whole(x):
    return pl.BlockSpec(x.shape, lambda i: (0,) * x.ndim)


def spec(shape):
    return pl.BlockSpec(shape, lambda i: (0,) * len(shape))


def call_front(first, jall, jrow, coh, vis, flags, sels):
    G = jall.shape[0]
    S = G * 128
    sc = operand_scratch(G)
    outs = [(144, ROWS), (G, 144, ROWS), (2, 2, 2 * ROWS, S), (ROWS, S), (8, 128)]
    return pl.pallas_call(
        front, grid=(1,),
        out_shape=[jax.ShapeDtypeStruct(s, F32) for s in outs],
        in_specs=[pl.BlockSpec(memory_space=pltpu.SMEM)] + [whole(x) for x in (jall, jrow, coh, vis, flags, *sels)],
        out_specs=[spec(s) for s in outs],
        scratch_shapes=[pltpu.VMEM((2, 2, 2 * ROWS, S), F32), pltpu.VMEM((ROWS, S), F32), *sc["model"], *sc["grad"], *sc["bufs"]],
        cost_estimate=pl.CostEstimate(flops=40_000_000_000, bytes_accessed=20_000_000, transcendentals=0),
        name="front",
    )(first, jall, jrow, coh, vis, flags, *sels)


def call_back(jall, jrow, coh, res, wgt, sels):
    G = jall.shape[0]
    sc = operand_scratch(G)
    outs = [(144, ROWS), (G, 144, ROWS)]
    sels = (sels[0], sels[2])
    return pl.pallas_call(
        back, grid=(1,),
        out_shape=[jax.ShapeDtypeStruct(s, F32) for s in outs],
        in_specs=[whole(jall), whole(jrow), pl.BlockSpec((1, *coh.shape[1:]), lambda i: (1, 0, 0, 0, 0))] + [whole(x) for x in (res, wgt, *sels)],
        out_specs=[spec(s) for s in outs],
        scratch_shapes=[*sc["grad"], *sc["bufs"]],
        cost_estimate=pl.CostEstimate(flops=20_000_000_000, bytes_accessed=10_000_000, transcendentals=0),
        name="back",
    )(jall, jrow, coh, res, wgt, *sels)


def beam_factor(beam, group_of):
    groups = beam.shape[0]
    onehot = (group_of[None, :] == jnp.arange(groups, dtype=jnp.int32)[:, None]).astype(F32)
    return jnp.sum(beam[:, :, None] * onehot[:, None, :], axis=0)


def exchange(parts, axis):
    return lax.all_to_all(parts, axis, 0, 0, tiled=True)


def owned_sum(parts):
    count = parts.shape[0]
    me = lax.axis_index(STN)
    total = lax.dynamic_index_in_dim(parts, me, 0, False)
    for hop in range(1, count):
        part = lax.dynamic_index_in_dim(parts, lax.rem(me + hop, count), 0, False)
        total = total + lax.ppermute(part, STN, [(i, (i + hop) % count) for i in range(count)])
    return total


def on_device(gains, coherency, vis_data, flags, beam, group_of):
    chan_dev = gains.shape[0]
    row_count = gains.shape[5]
    stn_count = lax.axis_size(STN)
    chan_count = lax.axis_size(CHAN)
    first_row = lax.axis_index(STN) * row_count
    all_channels = chan_dev * chan_count
    all_stations = row_count * stn_count

    row_factor = lax.dynamic_slice_in_dim(beam_factor(beam, group_of), first_row, row_count, 1)
    own = (gains * row_factor).reshape(chan_dev, 8 * K, row_count)
    every = exchange(jnp.broadcast_to(own, (stn_count, *own.shape)), STN)

    up = [(i, i + 1) for i in range(chan_count - 1)]
    down = [(i + 1, i) for i in range(chan_count - 1)]
    extended = jnp.concatenate([lax.ppermute(gains, CHAN, up), gains, lax.ppermute(gains, CHAN, down)], axis=0)
    second = extended[2:] - 2.0 * extended[1:-1] + extended[:-2]
    positions = lax.axis_index(CHAN) * chan_dev - 1 + jnp.arange(chan_dev + 2, dtype=jnp.int32)
    inside = ((positions >= 1) & (positions <= all_channels - 2)).astype(F32)
    second = second * inside[:, None, None, None, None, None]
    smooth_grad = second[:-2] - 2.0 * second[1:-1] + second[2:]
    own_second = second[1:-1]
    smooth_local = jnp.sum(own_second * own_second)

    blocks = jnp.arange(flags.shape[1], dtype=jnp.int32) + first_row // BLK
    selves = blocks[:, None] == jnp.arange(flags.shape[2], dtype=jnp.int32)[None, :]
    local_count = jnp.sum(flags * jnp.where(selves, BLK * (BLK - 1), BLK * BLK)[None]).astype(F32)

    sels = tuple(jnp.asarray(x, BF) for x in selections())
    row0, col0, res, wgt, sq = call_front(first_row[None].astype(jnp.int32), every, own, coherency, vis_data, flags, sels)
    lane = jnp.arange(row_count)
    packed = jnp.where(lane == 0, local_count, jnp.where(lane == 1, jnp.sum(sq), jnp.where(lane == 2, smooth_local, 0.0)))
    devices = chan_count * stn_count
    packed, own_back = lax.optimization_barrier((packed, own))
    arrived = exchange(jnp.broadcast_to(packed, (devices, row_count)), ALL)
    got0 = owned_sum(col0)
    row1, col1 = call_back(every, own_back, coherency, res, wgt, sels)
    col1, arrived = lax.optimization_barrier((col1, arrived))
    got1 = jnp.sum(exchange(col1, STN), axis=0)
    totals = jnp.sum(arrived, axis=0)

    norm_scale = all_channels * all_stations / totals[0]
    steps = []
    for f, (row, got) in enumerate(((row0, got0), (row1, got1))):
        both = row + got
        grad = both[:8 * K].reshape(2, 2, 2, K, row_count).swapaxes(0, 1)
        curv = both[8 * K:]
        gradient = norm_scale * row_factor * grad + smooth_weight * smooth_grad[f]
        curvature = norm_scale * row_factor * row_factor * curv + damping
        steps.append(gradient / curvature)
    gain_step = jnp.stack(steps)
    loss_value = (norm_scale * totals[1] + smooth_weight * totals[2]) / (all_channels * all_stations)
    return gain_step, loss_value


def solution(mesh):
    in_specs = (
        P(CHAN, None, None, None, None, STN),
        P(CHAN, None, None, STN, None),
        P(CHAN, None, None, None, STN, None),
        P(CHAN, STN, None),
        P(),
        P(),
    )
    out_specs = (P(CHAN, None, None, None, None, STN), P())

    return jax.shard_map(on_device, mesh=mesh, in_specs=in_specs, out_specs=out_specs, check_vma=False)
```

time: 691 us -> 134 us (0.19)
  other arithmetic: 346 us -> 8.97 us
  local copies, waits for them, and re-layouts: 209 us -> 3.93 us
  Pallas kernels: 0 us -> 71.5 us
  loops' own time: 56.6 us -> 0 us
  blocking collectives: 48.6 us -> 0 us
  starting transfers between devices: 20 us -> 34.2 us
  waiting for transfers between devices: 0.01 us -> 10.1 us
    reduce_sum x100 -> x4, other arithmetic: 184 us -> 1.99 us  [the longest x1 1.29 us: on_device(): jnp.sum(sq)]
    add x19 -> x4, other arithmetic: 95 us -> 1.83 us  [the longest x2 1.81 us: on_device(): both = row + got]
    reshape x19 -> x0, local copies, waits for them, and re-layouts: 88.7 us -> none  [the longest x17 86.2 us: expand_flags(): return wide.reshape(chans, first * BLK, second * BLK)]
    pallas_call x0 -> x2, Pallas kernels: none -> 71.5 us  [the longest x1 46.4 us: call_front(): pl.pallas_call(front, grid=(1,), out_shape=[jax.ShapeDtypeStruct(s, F32)...]
    another operation x2 -> x0, loops' own time: 56.6 us -> none  [the longest x1 29.5 us: block_terms(): (model_real, model_imag), _ = lax.scan(model_turn, (empty, empty), dir_list)]
    psum x5 -> x0, blocking collectives: 48.6 us -> none  [over_axes(): shard = lax.psum(shard, axis)]
    broadcast_in_dim x18 -> x2, local copies, waits for them, and re-layouts: 44.5 us -> 1.53 us  [the longest x1 0.83 us: on_device(): every = exchange(jnp.broadcast_to(own, (stn_count, *own.shape)), STN)]
    convert_element_type x37 -> x1, other arithmetic: 40.6 us -> 0.01 us  [on_device(): inside = ((positions >= 1) & (positions <= all_channels - 2)).astype(F32)]
  transfers between devices with their start and end apart: 5 -> 8, of which waited for: 0 -> 2; matrix products, arithmetic and copies ran while one was open for 81% -> 7% of each run, Pallas kernels for 0% -> 19%
where the time goes in v1:
time: 134 us; the launch traced here: 133 us
  Pallas kernels  71.5 us (53%)
  starting transfers between devices  34.2 us (26%)
  waiting for transfers between devices  10.1 us (8%)
  other arithmetic  8.97 us (7%)
  between operations  4.51 us (3%)
  local copies, waits for them, and re-layouts  3.93 us (3%)
    pallas_call x1, Pallas kernels, call_front(): pl.pallas_call(front, grid=(1,), out_shape=[jax.ShapeDtypeStruct(s, F32)...  46.4 us
    all_to_all x3, starting transfers between devices, exchange(): return lax.all_to_all(parts, axis, 0, 0, tiled=True)  25.4 us
    pallas_call x1, Pallas kernels, call_back(): pl.pallas_call(back, grid=(1,), out_shape=[jax.ShapeDtypeStruct(s, F32) f...  25.1 us
    all_to_all x3, waiting for transfers between devices, exchange(): return lax.all_to_all(parts, axis, 0, 0, tiled=True)  10.1 us
    ppermute x1, starting transfers between devices, on_device(): lax.ppermute(gains, CHAN, up)  5 us
  transfers between devices with their start and end apart: 8, of which 2 were waited for; matrix products, arithmetic and copies ran while one was open for 7% of the time, Pallas kernels for 19%

profile of v1, /device:TPU:1, one launch (start us, length us, event | category | flops | bytes accessed | tf_op | source)
XLA Modules:
  0.0 133.3 jit_solution(1737088202897840417)
XLA Ops:
  0.6 0.0 copy-start.2
  0.6 0.0 copy-start.4
  0.7 1.4 %collective-permute-start = (f32[2,2,2,2,16,128]{5,4,3,2,1,0:T(8,128)}, f32[2,2,2,2,16,128]{5,4,3,2,1,0:T(8,128)S(1)}, u32[]{:S(2)}, u32[]{:S(2)}) collective-permute-start(f32[2,2,2,2,16,128]{5,4,3,2,1,0:T(8,128)} %param.9), channel_id=1, source_target_pairs={{4,0},{8,4},{12,8},{16,12},{20,16},{24,20},{28,24},{32,28},{36,32}... | collective-permute-start | bytes 393224 | tf_op jit(solution)/shard_map/ppermute | solution.py:345
  2.1 5.0 %collective-permute-start.1 = (f32[2,2,2,2,16,128]{5,4,3,2,1,0:T(8,128)}, f32[2,2,2,2,16,128]{5,4,3,2,1,0:T(8,128)S(1)}, u32[]{:S(2)}, u32[]{:S(2)}) collective-permute-start(f32[2,2,2,2,16,128]{5,4,3,2,1,0:T(8,128)} %param.9), channel_id=1, source_target_pairs={{0,4},{4,8},{8,12},{12,16},{16,20},{20,24},{24,28},{28,32},{32,36}... | collective-permute-start | bytes 393224 | tf_op jit(solution)/shard_map/ppermute | solution.py:345
  7.1 0.7 fusion.15
  7.8 0.8 multiply_reduce_fusion
  8.6 0.9 broadcast_multiply_fusion
  9.5 0.0 copy-start
  9.5 0.8 broadcast_in_dim.45
  10.3 6.2 %all-to-all-start = ((f32[4,2,128,128]{3,2,1,0:T(8,128)}), f32[4,2,128,128]{3,2,1,0:T(8,128)S(1)}, u32[]{:S(2)}, u32[]{:S(2)}) async-start(f32[4,2,128,128]{3,2,1,0:T(8,128)} %broadcast_in_dim.45), calls=%async_computation | async-start | bytes 1048576 | tf_op jit(solution)/shard_map/all_to_all | solution.py:317
  16.5 0.1 fusion.18
  16.6 0.6 multiply_reduce_fusion.2
  18.0 0.1 fusion.3
  18.1 0.6 multiply_reduce_fusion.1
  18.7 8.2 %all-to-all-done.jall = f32[4,2,128,128]{3,2,1,0:T(8,128)S(1)} async-done(((f32[4,2,128,128]{3,2,1,0:T(8,128)}), f32[4,2,128,128]{3,2,1,0:T(8,128)S(1)}, u32[]{:S(2)}, u32[]{:S(2)}) %all-to-all-start) | async-done | bytes 524320 | tf_op jit(solution)/shard_map/all_to_all | solution.py:317
  26.9 0.8 copy-done.1
  27.7 46.4 %front.1 = (f32[144,128]{1,0:T(8,128)}, f32[4,144,128]{2,1,0:T(8,128)}, f32[2,2,256,512]{3,2,1,0:T(8,128)}, f32[128,512]{1,0:T(8,128)}, f32[8,128]{1,0:T(8,128)}) custom-call(s32[1]{0:T(128)} %bitcast.1.first, f32[4,2,128,128]{3,2,1,0:T(8,128)} %copy-done.1, f32[2,128,128]{2,1,0:T(8,128)} %bitcast.47, bf16[2,16,2,128,512]{4,3,2,1,0:T(8,128)(2,1)} %coh.3, ...), custom_call_target="tpu_custom_call" | custom-call | flops 40000000000 | bytes 20000000 | tf_op jit(solution)/shard_map/front/pallas_call | solution.py:283
  74.1 1.0 dynamic-slice_bitcast_fusion.2
  75.1 0.5 collective-permute-start.4
  75.6 0.2 collective-permute-start.3
  75.8 1.6 %collective-permute-start.2 = (f32[144,128]{1,0:T(8,128)S(1)}, f32[144,128]{1,0:T(8,128)S(1)}, u32[]{:S(2)}, u32[]{:S(2)}) collective-permute-start(f32[144,128]{1,0:T(8,128)S(1)} %get-tuple-element.24), channel_id=1, source_target_pairs={{0,1},{1,2},{2,3},{3,0},{4,5},{5,6},{6,7},{7,4},{8,9},{9,10},{10,1... | collective-permute-start | bytes 221192 | tf_op jit(solution)/shard_map/ppermute | solution.py:326
  77.4 1.3 reduce_sum.56
  78.7 1.3 compare_select_fusion.2
  80.0 0.7 broadcast_in_dim.53
  80.7 13.7 %all-to-all-start.1 = ((f32[256,1,128]{2,1,0:T(1,128)}), f32[256,1,128]{2,1,0:T(1,128)S(1)}, u32[]{:S(2)}, u32[]{:S(2)}) async-start(f32[256,1,128]{2,1,0:T(1,128)} %broadcast_in_dim.53), calls=%async_computation.1 | async-start | bytes 262144 | tf_op jit(solution)/shard_map/all_to_all | solution.py:317
  94.4 25.1 %back.1 = (f32[144,128]{1,0:T(8,128)}, f32[4,144,128]{2,1,0:T(8,128)}) custom-call(f32[4,2,128,128]{3,2,1,0:T(8,128)} %copy-done.1, f32[2,128,128]{2,1,0:T(8,128)} %bitcast.48, bf16[2,16,2,128,512]{4,3,2,1,0:T(8,128)(2,1)} %coh.3, f32[2,2,256,512]{3,2,1,0:T(8,128)} %get-tuple-element.15.res, f32[128,512]{1,0:T(8,128)} %get-tuple-element.16.wgt, ...), custom_call_target="tpu_custom_call" | custom-call | flops 20000000000 | bytes 10000000 | tf_op jit(solution)/shard_map/back/pallas_call | solution.py:299
  119.5 5.6 %all-to-all-start.2 = ((f32[4,144,128]{2,1,0:T(8,128)}), f32[4,144,128]{2,1,0:T(8,128)S(1)}, u32[]{:S(2)}, u32[]{:S(2)}) async-start(f32[4,144,128]{2,1,0:T(8,128)} %get-tuple-element.23), calls=%async_computation.2 | async-start | bytes 589824 | tf_op jit(solution)/shard_map/all_to_all | solution.py:317
  125.1 0.9 fusion.6
  126.1 0.6 fusion.19
  128.6 1.9 %all-to-all-done.2 = f32[4,144,128]{2,1,0:T(8,128)S(1)} async-done(((f32[4,144,128]{2,1,0:T(8,128)}), f32[4,144,128]{2,1,0:T(8,128)S(1)}, u32[]{:S(2)}, u32[]{:S(2)}) %all-to-all-start.2) | async-done | bytes 294944 | tf_op jit(solution)/shard_map/all_to_all | solution.py:317
  130.5 0.9 add.103
  131.5 0.7 pad_maximum_fusion.2
  (21 shorter events, 0.2 us)
Async XLA Ops:
  0.6 17.3 %copy-start.2 = (f32[2,2,2,2,16,128]{5,4,3,2,1,0:T(8,128)S(1)}, f32[2,2,2,2,16,128]{5,4,3,2,1,0:T(8,128)}, u32[]{:S(2)}) copy-start(f32[2,2,2,2,16,128]{5,4,3,2,1,0:T(8,128)} %param.9) | copy-start | bytes 393220
  0.6 16.0 %copy-start.4 = (s32[2,8,32]{2,1,0:T(8,128)S(1)}, s32[2,8,32]{2,1,0:T(8,128)}, u32[]{:S(2)}) copy-start(s32[2,8,32]{2,1,0:T(8,128)} %flags.1) | copy-start | bytes 6148
  0.7 17.3 %collective-permute-start = (f32[2,2,2,2,16,128]{5,4,3,2,1,0:T(8,128)}, f32[2,2,2,2,16,128]{5,4,3,2,1,0:T(8,128)S(1)}, u32[]{:S(2)}, u32[]{:S(2)}) collective-permute-start(f32[2,2,2,2,16,128]{5,4,3,2,1,0:T(8,128)} %param.9), channel_id=1, source_target_pairs={{4,0},{8,4},{12,8},{16,12},{20,16},{24,20},{28,24},{32,28},{36,32}... | collective-permute-start | bytes 393224 | tf_op jit(solution)/shard_map/ppermute | solution.py:345
  2.1 15.9 %collective-permute-start.1 = (f32[2,2,2,2,16,128]{5,4,3,2,1,0:T(8,128)}, f32[2,2,2,2,16,128]{5,4,3,2,1,0:T(8,128)S(1)}, u32[]{:S(2)}, u32[]{:S(2)}) collective-permute-start(f32[2,2,2,2,16,128]{5,4,3,2,1,0:T(8,128)} %param.9), channel_id=1, source_target_pairs={{0,4},{4,8},{8,12},{12,16},{16,20},{20,24},{24,28},{28,32},{32,36}... | collective-permute-start | bytes 393224 | tf_op jit(solution)/shard_map/ppermute | solution.py:345
  9.5 17.4 %copy-start = (f32[2,2,2,2,16,128]{5,4,3,2,1,0:T(8,128)}, f32[2,2,2,2,16,128]{5,4,3,2,1,0:T(8,128)S(1)}, u32[]{:S(2)}) copy-start(f32[2,2,2,2,16,128]{5,4,3,2,1,0:T(8,128)S(1)} %broadcast_multiply_fusion) | copy-start | bytes 393220
  10.3 16.6 %all-to-all-start = ((f32[4,2,128,128]{3,2,1,0:T(8,128)}), f32[4,2,128,128]{3,2,1,0:T(8,128)S(1)}, u32[]{:S(2)}, u32[]{:S(2)}) async-start(f32[4,2,128,128]{3,2,1,0:T(8,128)} %broadcast_in_dim.45), calls=%async_computation | async-start | bytes 1048576 | tf_op jit(solution)/shard_map/all_to_all | solution.py:317
  26.9 0.8 copy-start.1
  75.1 50.0 %collective-permute-start.4 = (f32[144,128]{1,0:T(8,128)S(1)}, f32[144,128]{1,0:T(8,128)S(1)}, u32[]{:S(2)}, u32[]{:S(2)}) collective-permute-start(f32[144,128]{1,0:T(8,128)S(1)} %get-tuple-element.25), channel_id=1, source_target_pairs={{0,3},{1,0},{2,1},{3,2},{4,7},{5,4},{6,5},{7,6},{8,11},{9,8},{10,9... | collective-permute-start | bytes 221192 | tf_op jit(solution)/shard_map/ppermute | solution.py:326
  75.6 49.4 %collective-permute-start.3 = (f32[144,128]{1,0:T(8,128)S(1)}, f32[144,128]{1,0:T(8,128)S(1)}, u32[]{:S(2)}, u32[]{:S(2)}) collective-permute-start(f32[144,128]{1,0:T(8,128)S(1)} %get-tuple-element.26), channel_id=1, source_target_pairs={{0,2},{1,3},{2,0},{3,1},{4,6},{5,7},{6,4},{7,5},{8,10},{9,11},{10,... | collective-permute-start | bytes 221192 | tf_op jit(solution)/shard_map/ppermute | solution.py:326
  75.8 49.3 %collective-permute-start.2 = (f32[144,128]{1,0:T(8,128)S(1)}, f32[144,128]{1,0:T(8,128)S(1)}, u32[]{:S(2)}, u32[]{:S(2)}) collective-permute-start(f32[144,128]{1,0:T(8,128)S(1)} %get-tuple-element.24), channel_id=1, source_target_pairs={{0,1},{1,2},{2,3},{3,0},{4,5},{5,6},{6,7},{7,4},{8,9},{9,10},{10,1... | collective-permute-start | bytes 221192 | tf_op jit(solution)/shard_map/ppermute | solution.py:326
  80.7 38.8 %all-to-all-start.1 = ((f32[256,1,128]{2,1,0:T(1,128)}), f32[256,1,128]{2,1,0:T(1,128)S(1)}, u32[]{:S(2)}, u32[]{:S(2)}) async-start(f32[256,1,128]{2,1,0:T(1,128)} %broadcast_in_dim.53), calls=%async_computation.1 | async-start | bytes 262144 | tf_op jit(solution)/shard_map/all_to_all | solution.py:317
  94.4 30.7 %copy-start.3 = (f32[144,128]{1,0:T(8,128)S(1)}, f32[144,128]{1,0:T(8,128)}, u32[]{:S(2)}) copy-start(f32[144,128]{1,0:T(8,128)} %get-tuple-element.20) | copy-start | bytes 221188
  119.5 11.0 %all-to-all-start.2 = ((f32[4,144,128]{2,1,0:T(8,128)}), f32[4,144,128]{2,1,0:T(8,128)S(1)}, u32[]{:S(2)}, u32[]{:S(2)}) async-start(f32[4,144,128]{2,1,0:T(8,128)} %get-tuple-element.23), calls=%async_computation.2 | async-start | bytes 589824 | tf_op jit(solution)/shard_map/all_to_all | solution.py:317

commit v2 on v1

v2 whole, which is shorter than its diff:
```python
import functools

import jax
import jax.numpy as jnp
import numpy as np
from jax import lax
from jax.experimental import pallas as pl
from jax.experimental.pallas import tpu as pltpu
from jax.sharding import Mesh
from jax.sharding import PartitionSpec as P


BF = jnp.bfloat16
F32 = jnp.float32
BLK = 16
CHAN = ("chan_x", "chan_y", "chan_z")
STN = "stn"
NEAR = ("chan_x", "stn")
OUTER = ("chan_y", "chan_z")
smooth_weight = 0.05
damping = 0.3


def selections():
    sel_w = np.zeros((64, 16), np.float32)
    sel_l = np.zeros((2, 16, 16), np.float32)
    for s in range(2):
        for t in range(2):
            for i in range(2):
                for r in range(2):
                    kk = ((s * 2 + t) * 2 + i) * 2 + r
                    for a in range(2):
                        sel_l[a, s * 8 + r * 4 + a * 2 + i, kk] = 1.0
                        sel_w[a * 16 + kk, t * 8 + r * 4 + a * 2 + i] = 1.0
                        sel_w[32 + a * 16 + kk, t * 8 + (1 - r) * 4 + a * 2 + i] = -1.0 if r == 0 else 1.0
    sel_c = np.zeros((2, 16, 16), np.float32)
    sel_q = np.zeros((4, 16, 16), np.float32)
    for s in range(2):
        for a in range(2):
            for i in range(2):
                re, im = s * 8 + a * 2 + i, s * 8 + 4 + a * 2 + i
                sel_c[a, s * 8 + i, re] = -1.0
                sel_c[a, s * 8 + 2 + i, im] = -1.0
                sel_c[a, s * 8 + 4 + i, im] = -1.0
                sel_c[a, s * 8 + 6 + i, re] = 1.0
                for half in range(2):
                    row = s * 8 + half * 4 + i
                    sel_q[a * 2, row, re] = -1.0
                    sel_q[a * 2, row + 2, im] = -1.0
                    sel_q[a * 2 + 1, row, im] = 1.0
                    sel_q[a * 2 + 1, row + 2, re] = -1.0
    w2 = np.concatenate([sel_w, sel_q.reshape(64, 16)], axis=0)
    return w2, sel_l, sel_c.reshape(32, 16)


def dot(a, b):
    return jnp.dot(a, b, preferred_element_type=F32)


def dot_t(a, b):
    return lax.dot_general(a, b, (((1,), (1,)), ((), ())), preferred_element_type=F32)


def dot_l(a, b):
    return lax.dot_general(a, b, (((0,), (0,)), ((), ())), preferred_element_type=F32)


def split(x):
    high = x.astype(BF)
    return high, (x - high.astype(F32)).astype(BF)


def parts_of(x):
    high = x.astype(BF).astype(F32)
    return jnp.concatenate([high, x - high], axis=0).astype(BF)


K = 16
ROWS = 128
LANES = 128
TILES = ROWS // 16


def weights_of(first, flags, wgt, groups):
    blocks, cols = flags.shape
    rows8 = lax.broadcasted_iota(jnp.int32, (ROWS, blocks), 0) // 16 == lax.broadcasted_iota(jnp.int32, (ROWS, blocks), 1)
    wide = dot(rows8.astype(F32).astype(BF), flags.astype(F32).astype(BF)).astype(BF)
    for g in range(groups):
        at = (lax.broadcasted_iota(jnp.int32, (cols, LANES), 1) + g * LANES) // 16
        at = at == lax.broadcasted_iota(jnp.int32, (cols, LANES), 0)
        full = dot(wide, at.astype(F32).astype(BF))
        row_id = lax.broadcasted_iota(jnp.int32, (ROWS, LANES), 0) + first
        col_id = lax.broadcasted_iota(jnp.int32, (ROWS, LANES), 1) + g * LANES
        wgt[:, g * LANES:(g + 1) * LANES] = jnp.where(row_id == col_id, 0.0, full)


def model_operands(jall, me, w2, sell, wr, wi, lr):
    groups = jall.shape[0]

    def turn(k, _):
        for g in range(groups):
            w = dot(w2[0:64], parts_of(jall[g, pl.ds(k, 8, stride=16), :])).astype(BF)
            for b in range(2):
                wr[k, g, :, b * 128:(b + 1) * 128] = w[b * 16:(b + 1) * 16]
                wi[k, g, :, b * 128:(b + 1) * 128] = w[32 + b * 16:48 + b * 16]
        hm = parts_of(jall[me, pl.ds(k, 8, stride=16), :])
        for a in range(2):
            l = dot_l(hm, sell[a]).astype(BF)
            for t in range(TILES):
                lr[k, t, a * 16:(a + 1) * 16, :] = l[t * 16:(t + 1) * 16]
        return 0

    lax.fori_loop(0, K, turn, 0)


def model(me_ref, own, mate, over, far, factor, coh, vis, flags, w2, sell, jall, res, wgt, sq, w_all, wr, wi, lr):
    groups = jall.shape[0]
    t = pl.program_id(0)
    me = me_ref[0]

    @pl.when(t == 0)
    def _():
        for hop, piece in enumerate((own, mate, over, far)):
            g = me ^ hop
            scale = factor[g]
            for plane in range(8):
                at = slice(plane * K, (plane + 1) * K)
                jall[g, at, :] = piece[0, at, :] * scale
        weights_of(me * ROWS, flags[0], w_all, groups)
        model_operands(jall, me, w2, sell, wr, wi, lr)
        sq[...] = jnp.zeros_like(sq)

    w_rows = w_all[pl.ds(pl.multiple_of(t * 16, 16), 16), :]
    wgt[...] = w_rows
    total = jnp.zeros((16, 128), F32)
    for g in range(groups):
        cols = slice(g * 128, (g + 1) * 128)
        acc = [[[jnp.zeros((16, 128), F32)] * 2 for _ in range(2)] for _ in range(2)]
        for k in range(K):
            o_re = dot(lr[k, t], wr[k, g])
            o_im = dot(lr[k, t], wi[k, g])
            c_re = coh[0, k, 0, :, cols].astype(F32)
            c_im = coh[0, k, 1, :, cols].astype(F32)
            for a in range(2):
                for b in range(2):
                    re = o_re[a * 16:(a + 1) * 16, b * 128:(b + 1) * 128]
                    im = o_im[a * 16:(a + 1) * 16, b * 128:(b + 1) * 128]
                    acc[a][b] = [acc[a][b][0] + c_re * re - c_im * im,
                                 acc[a][b][1] + c_re * im + c_im * re]
        w = w_rows[:, cols]
        for a in range(2):
            for b in range(2):
                for r in range(2):
                    v = w * (vis[0, r, a, b, :, cols].astype(F32) - acc[a][b][r])
                    res[b, r, a, :, cols] = v
                    total = total + v * v
    sq[...] += total[:8] + total[8:]


def norms(x):
    return parts_of(jnp.broadcast_to(jnp.sum(x * x, axis=0, keepdims=True), (8, LANES)))


def gradient_operands(jall, me, w2, selc, lq, lc, nq, nr):
    groups = jall.shape[0]
    span = groups * LANES

    def turn(k, _):
        for g in range(groups):
            x = jall[g, pl.ds(k, 8, stride=16), :]
            w = dot(w2[64:128], parts_of(x)).astype(BF)
            for j in range(4):
                lq[k, :, j * span + g * 128:j * span + (g + 1) * 128] = w[j * 16:j * 16 + 16]
            nq[k, :, g * 128:(g + 1) * 128] = norms(x)
        x = jall[me, pl.ds(k, 8, stride=16), :]
        c = dot(selc[...], parts_of(x)).astype(BF)
        for a in range(2):
            lc[k, :, a * 128:(a + 1) * 128] = c[a * 16:(a + 1) * 16]
        nr[k] = norms(x)
        return 0

    lax.fori_loop(0, K, turn, 0)


def gradient(coh, wgt, res, lq, lc, nq, nr, bufs, row, col, groups, rest):
    span = groups * LANES
    halves = groups // 2

    def fill(k, t, h, y, am):
        cols = slice(h * 256, (h + 1) * 256)
        rows = slice(t * 16, (t + 1) * 16)
        c_re = coh[k, 0, rows, cols].astype(F32)
        c_im = coh[k, 1, rows, cols].astype(F32)
        for a in range(2):
            at = slice(a * ROWS + t * 16, a * ROWS + t * 16 + 16)
            for b in range(2):
                r_re = res[b, 0, a, rows, cols]
                r_im = res[b, 1, a, rows, cols]
                for r, v in ((0, c_re * r_re + c_im * r_im), (1, c_re * r_im - c_im * r_re)):
                    high, low = split(v)
                    y[b * 2 + r, h, 0, at, :] = high
                    y[b * 2 + r, h, 1, at, :] = low
        high, low = split(wgt[rows, cols] * (c_re * c_re + c_im * c_im))
        am[h, rows, :] = high
        am[h, ROWS + t * 16:ROWS + t * 16 + 16, :] = low

    top = lax.broadcasted_iota(jnp.int32, (8, 128), 0) < 4

    def reduce_part(k, j, h, s, y, cell):
        tile = y[j, h, s]
        c = dot(lc[k], tile)
        r = dot_t(lq[k, :, j * span + h * 256:j * span + (h + 1) * 256], tile)
        c = c[:8] + c[8:]
        cell[0][j, h] = c if s == 0 else cell[0][j, h] + c
        cell[1] = r if cell[1] is None else cell[1] + r

    def reduce_end(k, am, cell):
        r = cell[1][:8] + cell[1][8:]
        row[pl.ds(k, 8, stride=16), :] = jnp.where(top, r[:, :ROWS], r[:, ROWS:])
        for g in range(groups):
            h, cols = g // 2, slice(g % 2 * 128, g % 2 * 128 + 128)
            c = [cell[0][j, h][:, cols] for j in range(4)]
            t0 = c[0] + pltpu.roll(c[1], 4, 0)
            t1 = pltpu.roll(c[2], 4, 0) + c[3]
            col[g, pl.ds(k, 8, stride=16), :] = jnp.where(top, t0, t1)
        total = None
        n_row = jnp.concatenate([nr[k], nr[k]], axis=1)
        for h in range(halves):
            tile = am[h]
            cc = dot(n_row, tile)
            cc = cc[0:1] + cc[8:9]
            for g in range(2):
                col[h * 2 + g, pl.ds(128 + k, 1), :] = cc[:, g * 128:(g + 1) * 128]
            cr = dot_t(nq[k, :, h * 256:(h + 1) * 256], tile)
            cr = cr[0:1] + cr[8:9]
            cr = cr[:, :ROWS] + cr[:, ROWS:]
            total = cr if total is None else total + cr
        row[pl.ds(128 + k, 1), :] = total

    fills = [(t, h) for t in range(TILES) for h in range(halves)]
    dots = [(j, h, s) for j in range(4) for h in range(halves) for s in range(2)]
    (y0, a0), (y1, a1) = bufs
    for t, h in fills:
        fill(0, t, h, y0, a0)
    rest()

    def pair(i, _):
        for step, (y, am, y_next, am_next) in enumerate(((y0, a0, y1, a1), (y1, a1, y0, a0))):
            k = 2 * i + step
            k_next = jnp.minimum(k + 1, K - 1)
            cell = [{}, None]
            for (t, h), part in zip(fills, dots):
                reduce_part(k, *part, y, cell)
                fill(k_next, t, h, y_next, am_next)
            reduce_end(k, am, cell)
        return 0

    lax.fori_loop(0, K // 2, pair, 0)


def operand_scratch(G):
    S = G * 128
    return dict(
        model=[pltpu.VMEM((K, G, 16, 256), BF), pltpu.VMEM((K, G, 16, 256), BF), pltpu.VMEM((K, TILES, 32, 16), BF)],
        grad=[pltpu.VMEM((K, 16, 4 * S), BF), pltpu.VMEM((K, 16, 2 * ROWS), BF), pltpu.VMEM((K, 16, S), BF), pltpu.VMEM((K, 16, ROWS), BF)],
        bufs=[pltpu.VMEM((4, G // 2, 2, 2 * ROWS, 256), BF), pltpu.VMEM((G // 2, 2 * ROWS, 256), BF)] * 2,
    )


def grad_kernel(f, me_ref, jall, coh_hbm, res_hbm, wgt, w2, selc, row, col0, col1, col2, col3,
                coh, res, sems, col, lq, lc, nq, nr, y0, a0, y1, a1):
    groups = jall.shape[0]
    me = me_ref[0]
    load_res = pltpu.make_async_copy(res_hbm, res, sems.at[0])
    load_first = pltpu.make_async_copy(coh_hbm.at[f, pl.ds(0, 2)], coh.at[pl.ds(0, 2)], sems.at[1])
    load_rest = pltpu.make_async_copy(coh_hbm.at[f, pl.ds(2, K - 2)], coh.at[pl.ds(2, K - 2)], sems.at[2])
    load_res.start()
    load_first.start()
    load_rest.start()
    gradient_operands(jall, me, w2, selc, lq, lc, nq, nr)
    load_res.wait()
    load_first.wait()
    gradient(coh, wgt, res, lq, lc, nq, nr, ((y0, a0), (y1, a1)), row, col, groups, load_rest.wait)
    for hop, out in enumerate((col0, col1, col2, col3)):
        out[...] = col[me ^ hop]


def whole(x):
    return pl.BlockSpec(x.shape, lambda i: (0,) * x.ndim)


def spec(shape):
    return pl.BlockSpec(shape, lambda i: (0,) * len(shape))


def call_model(f, me, pieces, factor, coh, vis, flags, sels):
    G = factor.shape[0]
    S = G * LANES
    sc = operand_scratch(G)
    outs = [((G, 8 * K, LANES), None), ((2, 2, 2, ROWS, S), 3), ((ROWS, S), 0), ((8, 128), None)]

    def piece_spec(x):
        at = f if x.shape[0] > 1 else 0
        return pl.BlockSpec((1, *x.shape[1:]), lambda i: (at, 0, 0))

    def out_spec(shape, dim):
        if dim is None:
            return spec(shape)
        block = shape[:dim] + (16,) + shape[dim + 1:]
        return pl.BlockSpec(block, lambda i: tuple(i if d == dim else 0 for d in range(len(shape))))

    return pl.pallas_call(
        model, grid=(TILES,),
        out_shape=[jax.ShapeDtypeStruct(s, F32) for s, _ in outs],
        in_specs=[pl.BlockSpec(memory_space=pltpu.SMEM)] + [piece_spec(x) for x in pieces] + [
            whole(factor),
            pl.BlockSpec((1, K, 2, 16, S), lambda i: (f, 0, 0, i, 0)),
            pl.BlockSpec((1, 2, 2, 2, 16, S), lambda i: (f, 0, 0, 0, i, 0)),
            pl.BlockSpec((1, *flags.shape[1:]), lambda i: (f, 0, 0)),
            whole(sels[0]), whole(sels[1]),
        ],
        out_specs=[out_spec(*o) for o in outs],
        scratch_shapes=[pltpu.VMEM((ROWS, S), F32), *sc["model"]],
        cost_estimate=pl.CostEstimate(flops=8_000_000_000, bytes_accessed=10_000_000, transcendentals=0),
    )(me, *pieces, factor, coh, vis, flags, sels[0], sels[1])


def call_grad(f, me, jall, coh, res, wgt, sels):
    G = jall.shape[0]
    sc = operand_scratch(G)
    outs = [(9 * K, ROWS)] * 5
    return pl.pallas_call(
        functools.partial(grad_kernel, f), grid=(1,),
        out_shape=[jax.ShapeDtypeStruct(s, F32) for s in outs],
        in_specs=[pl.BlockSpec(memory_space=pltpu.SMEM), whole(jall), pl.BlockSpec(memory_space=pl.ANY), pl.BlockSpec(memory_space=pl.ANY),
                  whole(wgt), whole(sels[0]), whole(sels[2])],
        out_specs=[spec(s) for s in outs],
        scratch_shapes=[pltpu.VMEM(coh.shape[1:], BF), pltpu.VMEM(res.shape, F32), pltpu.SemaphoreType.DMA((3,)),
                        pltpu.VMEM((G, 9 * K, ROWS), F32), *sc["grad"], *sc["bufs"]],
        cost_estimate=pl.CostEstimate(flops=20_000_000_000, bytes_accessed=10_000_000, transcendentals=0),
    )(me, jall, coh, res, wgt, sels[0], sels[2])


def beam_factor(beam, group_of):
    groups = beam.shape[0]
    onehot = (group_of[None, :] == jnp.arange(groups, dtype=jnp.int32)[:, None]).astype(F32)
    return jnp.sum(beam[:, :, None] * onehot[:, None, :], axis=0)


def hop_pairs(hop, count):
    return [(i, i ^ hop) for i in range(count)]


def on_device(gains, coherency, vis_data, flags, beam, group_of):
    chan_dev = gains.shape[0]
    row_count = gains.shape[5]
    stn_count = lax.axis_size(STN)
    chan_count = lax.axis_size(CHAN)
    me = lax.axis_index(STN).astype(jnp.int32)
    first_row = me * row_count
    all_channels = chan_dev * chan_count
    all_stations = row_count * stn_count

    raw = gains.reshape(chan_dev, 8 * K, row_count)
    over = [lax.ppermute(raw[f:f + 1], STN, hop_pairs(2, stn_count)) for f in range(chan_dev)]
    mate = lax.ppermute(raw, STN, hop_pairs(1, stn_count))
    far = [lax.ppermute(over[0], STN, hop_pairs(1, stn_count))]
    far.append(lax.ppermute(over[1], STN, hop_pairs(1, stn_count)))
    factor = beam_factor(beam, group_of).reshape(K, stn_count, row_count).swapaxes(0, 1)
    row_factor = lax.dynamic_index_in_dim(factor, me, 0, False)

    up = [(i, i + 1) for i in range(chan_count - 1)]
    down = [(i + 1, i) for i in range(chan_count - 1)]
    before, after = lax.ppermute(gains, CHAN, up), lax.ppermute(gains, CHAN, down)
    extended = jnp.concatenate([before, gains, after], axis=0)
    second = extended[2:] - 2.0 * extended[1:-1] + extended[:-2]
    positions = lax.axis_index(CHAN) * chan_dev - 1 + jnp.arange(chan_dev + 2, dtype=jnp.int32)
    inside = ((positions >= 1) & (positions <= all_channels - 2)).astype(F32)
    second = second * inside[:, None, None, None, None, None]
    smooth_grad = second[:-2] - 2.0 * second[1:-1] + second[2:]
    own_second = second[1:-1]
    smooth_local = jnp.sum(own_second * own_second)

    blocks = jnp.arange(flags.shape[1], dtype=jnp.int32) + first_row // BLK
    selves = blocks[:, None] == jnp.arange(flags.shape[2], dtype=jnp.int32)[None, :]
    local_count = jnp.sum(flags * jnp.where(selves, BLK * (BLK - 1), BLK * BLK)[None]).astype(F32)

    sels = tuple(jnp.asarray(x, BF) for x in selections())
    me1 = me[None]
    jall0, res0, wgt0, sq0 = call_model(0, me1, (raw, mate, over[0], far[0]), factor, coherency, vis_data, flags, sels)
    jall1, res1, wgt1, sq1 = call_model(1, me1, (raw, mate, over[1], far[1]), factor, coherency, vis_data, flags, sels)
    lane = jnp.arange(row_count)
    packed = jnp.where(lane == 0, local_count, jnp.where(lane == 1, jnp.sum(sq0 + sq1), jnp.where(lane == 2, smooth_local, 0.0)))

    arrived = lax.all_to_all(jnp.broadcast_to(packed, (lax.axis_size(NEAR), row_count)), NEAR, 0, 0, tiled=True)
    row0, *cols0 = call_grad(0, me1, jall0, coherency, res0, wgt0, sels)
    partial = jnp.sum(arrived, axis=0)
    arrived = lax.all_to_all(jnp.broadcast_to(partial, (lax.axis_size(OUTER), row_count)), OUTER, 0, 0, tiled=True)
    cols0 = cols0[:1] + [lax.ppermute(cols0[h], STN, hop_pairs(h, stn_count)) for h in range(1, stn_count)]
    row1, *cols1 = call_grad(1, me1, jall1, coherency, res1, wgt1, sels)
    cols1 = cols1[:1] + [lax.ppermute(cols1[h], STN, hop_pairs(h, stn_count)) for h in range(1, stn_count)]
    totals = jnp.sum(arrived, axis=0)

    norm_scale = all_channels * all_stations / totals[0]
    steps = []
    for f, (row, cols) in enumerate(((row0, cols0), (row1, cols1))):
        both = row + (cols[0] + cols[1]) + (cols[2] + cols[3])
        grad = both[:8 * K].reshape(2, 2, 2, K, row_count).swapaxes(0, 1)
        curv = both[8 * K:]
        gradient_f = norm_scale * row_factor * grad + smooth_weight * smooth_grad[f]
        curvature = norm_scale * row_factor * row_factor * curv + damping
        steps.append(gradient_f / curvature)
    gain_step = jnp.stack(steps)
    loss_value = (norm_scale * totals[1] + smooth_weight * totals[2]) / (all_channels * all_stations)
    return gain_step, loss_value


def solution(mesh):
    parts = Mesh(mesh.devices.reshape(4, 2, 8, 4), ("chan_x", "chan_y", "chan_z", "stn"))
    in_specs = (
        P(CHAN, None, None, None, None, STN),
        P(CHAN, None, None, STN, None),
        P(CHAN, None, None, None, STN, None),
        P(CHAN, STN, None),
        P(),
        P(),
    )
    out_specs = (P(CHAN, None, None, None, None, STN), P())

    return jax.shard_map(on_device, mesh=parts, in_specs=in_specs, out_specs=out_specs, check_vma=False)
```

time: 134 us -> 127 us (0.948)
  waiting for transfers between devices: 10.1 us -> 1.4 us
    all_to_all x3 -> x2, waiting for transfers between devices: 10.1 us -> 0.01 us  [the longest x1 0.01 us: on_device(): lax.all_to_all(jnp.broadcast_to(partial, (lax.axis_size(OUTER), row_count...]
    all_to_all x3 -> x2, starting transfers between devices: 25.4 us -> 17.8 us  [the longest x1 11.5 us: on_device(): lax.all_to_all(jnp.broadcast_to(packed, (lax.axis_size(NEAR), row_count))...]
    ppermute x3 -> x11, starting transfers between devices: 2.31 us -> 9.59 us  [the longest x1 2.85 us: on_device(): mate = lax.ppermute(raw, STN, hop_pairs(1, stn_count))]
    ppermute x3 -> x11, waiting for transfers between devices: 0.01 us -> 1.39 us  [the longest x3 1.37 us: on_device(): lax.ppermute(cols1[h], STN, hop_pairs(h, stn_count))]
    pallas_call x2 -> x4, Pallas kernels: 71.5 us -> 72.4 us  [the longest x2 46.2 us: call_grad(): pl.pallas_call(functools.partial(grad_kernel, f), grid=(1,), out_shape=[j...]
  transfers between devices with their start and end apart: 8 -> 15, of which waited for: 2 -> 2; matrix products, arithmetic and copies ran while one was open for 7% -> 6% of each run, Pallas kernels for 19% -> 47%
where the time goes in v2:
time: 127 us; the launch traced here: 126 us
  Pallas kernels  72.4 us (57%)
  starting transfers between devices  33.7 us (27%)
  other arithmetic  8.95 us (7%)
  between operations  4.71 us (4%)
  local copies, waits for them, and re-layouts  4.7 us (4%)
  waiting for transfers between devices  1.4 us (1%)
    pallas_call x2, Pallas kernels, call_grad(): pl.pallas_call(functools.partial(grad_kernel, f), grid=(1,), out_shape=[j...  46.2 us
    pallas_call x2, Pallas kernels, call_model(): pl.pallas_call(model, grid=(TILES,), out_shape=[jax.ShapeDtypeStruct(s, F...  26.3 us
    all_to_all x1, starting transfers between devices, on_device(): lax.all_to_all(jnp.broadcast_to(packed, (lax.axis_size(NEAR), row_count))...  11.5 us
    all_to_all x1, starting transfers between devices, on_device(): lax.all_to_all(jnp.broadcast_to(partial, (lax.axis_size(OUTER), row_count...  6.36 us
    ppermute x1, starting transfers between devices, on_device(): lax.ppermute(gains, CHAN, up)  5 us
    ppermute x1, starting transfers between devices, on_device(): mate = lax.ppermute(raw, STN, hop_pairs(1, stn_count))  2.85 us
  transfers between devices with their start and end apart: 15, of which 2 were waited for; matrix products, arithmetic and copies ran while one was open for 6% of the time, Pallas kernels for 47%

profile of v2, /device:TPU:1, one launch (start us, length us, event | category | flops | bytes accessed | tf_op | source)
XLA Modules:
  0.0 125.9 jit_solution(16947374440395329249)
XLA Ops:
  0.6 1.3 %collective-permute-start.5 = (f32[2,2,2,2,16,128]{5,4,3,2,1,0:T(8,128)}, f32[2,2,2,2,16,128]{5,4,3,2,1,0:T(8,128)S(1)}, u32[]{:S(2)}, u32[]{:S(2)}) collective-permute-start(f32[2,2,2,2,16,128]{5,4,3,2,1,0:T(8,128)} %param.9), channel_id=1, source_target_pairs={{4,0},{8,4},{12,8},{16,12},{20,16},{24,20},{28,24},{32,28},{36,32}... | collective-permute-start | bytes 393224 | tf_op jit(solution)/shard_map/ppermute | solution.py:374
  1.9 5.0 %collective-permute-start.6 = (f32[2,2,2,2,16,128]{5,4,3,2,1,0:T(8,128)}, f32[2,2,2,2,16,128]{5,4,3,2,1,0:T(8,128)S(1)}, u32[]{:S(2)}, u32[]{:S(2)}) collective-permute-start(f32[2,2,2,2,16,128]{5,4,3,2,1,0:T(8,128)} %param.9), channel_id=1, source_target_pairs={{0,4},{4,8},{8,12},{12,16},{16,20},{20,24},{24,28},{28,32},{32,36}... | collective-permute-start | bytes 393224 | tf_op jit(solution)/shard_map/ppermute | solution.py:374
  6.9 2.8 %collective-permute-start = (f32[2,128,128]{2,1,0:T(8,128)}, f32[2,128,128]{2,1,0:T(8,128)S(1)}, u32[]{:S(2)}, u32[]{:S(2)}) collective-permute-start(f32[2,128,128]{2,1,0:T(8,128)} %bitcast.43), channel_id=1, source_target_pairs={{0,1},{1,0},{2,3},{3,2},{4,5},{5,4},{6,7},{7,6},{8,9},{9,8},{10,11... | collective-permute-start | bytes 393224 | tf_op jit(solution)/shard_map/ppermute | solution.py:366
  9.8 0.9 fusion.16
  10.8 1.5 %collective-permute-start.3 = (f32[1,128,128]{2,1,0:T(8,128)S(1)}, f32[1,128,128]{2,1,0:T(8,128)S(1)}, u32[]{:S(2)}, u32[]{:S(2)}) collective-permute-start(f32[1,128,128]{2,1,0:T(8,128)S(1)} %bitcast.48), channel_id=1, source_target_pairs={{0,2},{1,3},{2,0},{3,1},{4,6},{5,7},{6,4},{7,5},{8,10},{9,11},{10,... | collective-permute-start | bytes 196616 | tf_op jit(solution)/shard_map/ppermute | solution.py:365
  12.2 0.7 fusion.12
  12.9 0.8 multiply_reduce_fusion
  13.7 0.6 bitcast_bitcast_fusion.factor
  14.4 1.3 %multiply_reduce_fusion.2 = s32[]{:T(128)} fusion(s32[2,8,32]{2,1,0:T(8,128)} %flags.3, s32[8,32]{1,0:T(8,128)S(1)} %fusion.15), kind=kLoop, calls=%fused_computation.32 | loop fusion | flops 1023 | bytes 3076 | tf_op jit(solution)/shard_map/reduce_sum | solution.py:386
  16.5 0.7 collective-permute-start.2
  17.2 1.1 fusion.3
  18.4 0.6 copy-done.3
  19.1 13.1 %shard_map.104 = (f32[4,128,128]{2,1,0:T(8,128)}, f32[2,2,2,128,512]{4,3,2,1,0:T(8,128)}, f32[128,512]{1,0:T(8,128)}, f32[8,128]{1,0:T(8,128)}) custom-call(s32[1]{0:T(128)} %bitcast.me_ref, f32[2,128,128]{2,1,0:T(8,128)} %bitcast.44, f32[2,128,128]{2,1,0:T(8,128)} %copy-done.3, f32[1,128,128]{2,1,0:T(8,128)} %copy-done.5, f32[1,128,128]{2,1,0:T(8,128)} %copy-done.7, ...), custom_call_target="tpu_custom_call" | custom-call | flops 8000000000 | bytes 10000000 | tf_op jit(solution)/shard_map/pallas_call | solution.py:312
  32.2 0.6 multiply_reduce_fusion.1
  32.9 0.6 copy-done.6
  33.5 13.1 %shard_map.105 = (f32[4,128,128]{2,1,0:T(8,128)}, f32[2,2,2,128,512]{4,3,2,1,0:T(8,128)}, f32[128,512]{1,0:T(8,128)}, f32[8,128]{1,0:T(8,128)}) custom-call(s32[1]{0:T(128)} %bitcast.me_ref, f32[2,128,128]{2,1,0:T(8,128)} %bitcast.45, f32[2,128,128]{2,1,0:T(8,128)} %copy-done.3, f32[1,128,128]{2,1,0:T(8,128)} %copy-done.4, f32[1,128,128]{2,1,0:T(8,128)} %copy-done.6, ...), custom_call_target="tpu_custom_call" | custom-call | flops 8000000000 | bytes 10000000 | tf_op jit(solution)/shard_map/pallas_call | solution.py:312
  46.6 1.3 %add_reduce_fusion = f32[]{:T(128)} fusion(f32[8,128]{1,0:T(8,128)S(1)} %copy-done.2, f32[8,128]{1,0:T(8,128)} %get-tuple-element.21), kind=kLoop, calls=%fused_computation.34 | loop fusion | flops 2047 | bytes 8196 | tf_op jit(solution)/shard_map/reduce_sum | solution.py:393
  47.9 1.3 %compare_select_fusion.2 = f32[128]{0:T(128)S(1)} fusion(f32[]{:T(128)} %get-tuple-element.38, f32[]{:T(128)} %add_reduce_fusion, f32[]{:T(128)S(6)} %convert_element_type.17), kind=kLoop, calls=%fused_computation.40 | loop fusion | flops 768 | bytes 524 | tf_op jit(solution)/shard_map/jit(_where)/select_n | solution.py:393
  49.2 0.6 broadcast_in_dim.51
  49.8 11.5 %all-to-all-start = ((f32[16,1,128]{2,1,0:T(1,128)}), f32[16,1,128]{2,1,0:T(1,128)S(1)}, u32[]{:S(2)}, u32[]{:S(2)}) async-start(f32[16,1,128]{2,1,0:T(1,128)} %broadcast_in_dim.51), calls=%async_computation | async-start | bytes 16384 | tf_op jit(solution)/shard_map/all_to_all | solution.py:395
  61.3 23.1 %shard_map.106 = (f32[144,128]{1,0:T(8,128)}, f32[144,128]{1,0:T(8,128)}, f32[144,128]{1,0:T(8,128)}, f32[144,128]{1,0:T(8,128)}, f32[144,128]{1,0:T(8,128)}) custom-call(s32[1]{0:T(128)} %bitcast.me_ref, f32[4,128,128]{2,1,0:T(8,128)} %get-tuple-element.22.jall, bf16[2,16,2,128,512]{4,3,2,1,0:T(8,128)(2,1)} %coh_hbm.3, ...), custom_call_target="tpu_custom_call" | custom-call | flops 20000000000 | bytes 10000000 | tf_op jit(solution)/shard_map/pallas_call | solution.py:332
  84.4 1.4 %collective-permute-start.8 = (f32[144,128]{1,0:T(8,128)}, f32[144,128]{1,0:T(8,128)S(1)}, u32[]{:S(2)}, u32[]{:S(2)}) collective-permute-start(f32[144,128]{1,0:T(8,128)} %get-tuple-element.28), channel_id=1, source_target_pairs={{0,2},{1,3},{2,0},{3,1},{4,6},{5,7},{6,4},{7,5},{8,10},{9,11},{10,... | collective-permute-start | bytes 221192 | tf_op jit(solution)/shard_map/ppermute | solution.py:399
  85.8 0.4 collective-permute-start.9
  86.5 0.6 broadcast_in_dim.52
  87.1 6.4 %all-to-all-start.1 = ((f32[16,1,128]{2,1,0:T(1,128)}), f32[16,1,128]{2,1,0:T(1,128)S(1)}, u32[]{:S(2)}, u32[]{:S(2)}) async-start(f32[16,1,128]{2,1,0:T(1,128)} %broadcast_in_dim.52), calls=%async_computation.1 | async-start | bytes 16384 | tf_op jit(solution)/shard_map/all_to_all | solution.py:398
  93.5 23.1 %shard_map.107 = (f32[144,128]{1,0:T(8,128)}, f32[144,128]{1,0:T(8,128)}, f32[144,128]{1,0:T(8,128)}, f32[144,128]{1,0:T(8,128)}, f32[144,128]{1,0:T(8,128)}) custom-call(s32[1]{0:T(128)} %bitcast.me_ref, f32[4,128,128]{2,1,0:T(8,128)} %get-tuple-element.30.jall, bf16[2,16,2,128,512]{4,3,2,1,0:T(8,128)(2,1)} %coh_hbm.3, ...), custom_call_target="tpu_custom_call" | custom-call | flops 20000000000 | bytes 10000000 | tf_op jit(solution)/shard_map/pallas_call | solution.py:332
  116.6 0.8 collective-permute-start.11
  117.5 1.4 %collective-permute-start.12 = (f32[144,128]{1,0:T(8,128)}, f32[144,128]{1,0:T(8,128)S(1)}, u32[]{:S(2)}, u32[]{:S(2)}) collective-permute-start(f32[144,128]{1,0:T(8,128)} %get-tuple-element.37), channel_id=1, source_target_pairs={{0,3},{1,2},{2,1},{3,0},{4,7},{5,6},{6,5},{7,4},{8,11},{9,10},{10,... | collective-permute-start | bytes 221192 | tf_op jit(solution)/shard_map/ppermute | solution.py:401
  118.9 0.7 fusion.17
  121.7 1.2 collective-permute-done.12
  123.1 0.9 add_add_fusion
  124.1 0.7 pad_maximum_fusion.2
  (44 shorter events, 1.1 us)
Async XLA Ops:
  0.6 16.6 %collective-permute-start.5 = (f32[2,2,2,2,16,128]{5,4,3,2,1,0:T(8,128)}, f32[2,2,2,2,16,128]{5,4,3,2,1,0:T(8,128)S(1)}, u32[]{:S(2)}, u32[]{:S(2)}) collective-permute-start(f32[2,2,2,2,16,128]{5,4,3,2,1,0:T(8,128)} %param.9), channel_id=1, source_target_pairs={{4,0},{8,4},{12,8},{16,12},{20,16},{24,20},{28,24},{32,28},{36,32}... | collective-permute-start | bytes 393224 | tf_op jit(solution)/shard_map/ppermute | solution.py:374
  1.9 15.3 %collective-permute-start.6 = (f32[2,2,2,2,16,128]{5,4,3,2,1,0:T(8,128)}, f32[2,2,2,2,16,128]{5,4,3,2,1,0:T(8,128)S(1)}, u32[]{:S(2)}, u32[]{:S(2)}) collective-permute-start(f32[2,2,2,2,16,128]{5,4,3,2,1,0:T(8,128)} %param.9), channel_id=1, source_target_pairs={{0,4},{4,8},{8,12},{12,16},{16,20},{20,24},{24,28},{28,32},{32,36}... | collective-permute-start | bytes 393224 | tf_op jit(solution)/shard_map/ppermute | solution.py:374
  6.9 11.5 %collective-permute-start = (f32[2,128,128]{2,1,0:T(8,128)}, f32[2,128,128]{2,1,0:T(8,128)S(1)}, u32[]{:S(2)}, u32[]{:S(2)}) collective-permute-start(f32[2,128,128]{2,1,0:T(8,128)} %bitcast.43), channel_id=1, source_target_pairs={{0,1},{1,0},{2,3},{3,2},{4,5},{5,4},{6,7},{7,6},{8,9},{9,8},{10,11... | collective-permute-start | bytes 393224 | tf_op jit(solution)/shard_map/ppermute | solution.py:366
  10.7 5.8 %collective-permute-start.1 = (f32[1,128,128]{2,1,0:T(8,128)S(1)}, f32[1,128,128]{2,1,0:T(8,128)S(1)}, u32[]{:S(2)}, u32[]{:S(2)}) collective-permute-start(f32[1,128,128]{2,1,0:T(8,128)S(1)} %bitcast.49), channel_id=1, source_target_pairs={{0,2},{1,3},{2,0},{3,1},{4,6},{5,7},{6,4},{7,5},{8,10},{9,11},{10,... | collective-permute-start | bytes 196616 | tf_op jit(solution)/shard_map/ppermute | solution.py:365
  10.8 6.4 %collective-permute-start.3 = (f32[1,128,128]{2,1,0:T(8,128)S(1)}, f32[1,128,128]{2,1,0:T(8,128)S(1)}, u32[]{:S(2)}, u32[]{:S(2)}) collective-permute-start(f32[1,128,128]{2,1,0:T(8,128)S(1)} %bitcast.48), channel_id=1, source_target_pairs={{0,2},{1,3},{2,0},{3,1},{4,6},{5,7},{6,4},{7,5},{8,10},{9,11},{10,... | collective-permute-start | bytes 196616 | tf_op jit(solution)/shard_map/ppermute | solution.py:365
  16.4 2.0 %copy-start.5 = (f32[1,128,128]{2,1,0:T(8,128)}, f32[1,128,128]{2,1,0:T(8,128)S(1)}, u32[]{:S(2)}) copy-start(f32[1,128,128]{2,1,0:T(8,128)S(1)} %collective-permute-done.1.over) | copy-start | bytes 196612
  16.5 2.0 %collective-permute-start.2 = (f32[1,128,128]{2,1,0:T(8,128)S(1)}, f32[1,128,128]{2,1,0:T(8,128)S(1)}, u32[]{:S(2)}, u32[]{:S(2)}) collective-permute-start(f32[1,128,128]{2,1,0:T(8,128)S(1)} %collective-permute-done.1.over), channel_id=1, source_target_pairs={{0,1},{1,0},{2,3},{3,2},{4,5},{5,4},{6,7},{7,6},{8,9},{9,8},{10,11... | collective-permute-start | bytes 196616 | tf_op jit(solution)/shard_map/ppermute | solution.py:367
  17.1 15.1 %copy-start.4 = (f32[1,128,128]{2,1,0:T(8,128)}, f32[1,128,128]{2,1,0:T(8,128)S(1)}, u32[]{:S(2)}) copy-start(f32[1,128,128]{2,1,0:T(8,128)S(1)} %collective-permute-done.3.over) | copy-start | bytes 196612
  17.1 15.7 %collective-permute-start.4 = (f32[1,128,128]{2,1,0:T(8,128)S(1)}, f32[1,128,128]{2,1,0:T(8,128)S(1)}, u32[]{:S(2)}, u32[]{:S(2)}) collective-permute-start(f32[1,128,128]{2,1,0:T(8,128)S(1)} %collective-permute-done.3.over), channel_id=1, source_target_pairs={{0,1},{1,0},{2,3},{3,2},{4,5},{5,4},{6,7},{7,6},{8,9},{9,8},{10,11... | collective-permute-start | bytes 196616 | tf_op jit(solution)/shard_map/ppermute | solution.py:368
  18.4 0.7 copy-start.3
  18.4 0.7 copy-start.7
  32.8 13.8 %copy-start.2 = (f32[8,128]{1,0:T(8,128)S(1)}, f32[8,128]{1,0:T(8,128)}, u32[]{:S(2)}) copy-start(f32[8,128]{1,0:T(8,128)} %get-tuple-element.20) | copy-start | bytes 12292
  32.9 0.6 copy-start.6
  49.8 36.6 %all-to-all-start = ((f32[16,1,128]{2,1,0:T(1,128)}), f32[16,1,128]{2,1,0:T(1,128)S(1)}, u32[]{:S(2)}, u32[]{:S(2)}) async-start(f32[16,1,128]{2,1,0:T(1,128)} %broadcast_in_dim.51), calls=%async_computation | async-start | bytes 16384 | tf_op jit(solution)/shard_map/all_to_all | solution.py:395
  84.4 37.2 %collective-permute-start.8 = (f32[144,128]{1,0:T(8,128)}, f32[144,128]{1,0:T(8,128)S(1)}, u32[]{:S(2)}, u32[]{:S(2)}) collective-permute-start(f32[144,128]{1,0:T(8,128)} %get-tuple-element.28), channel_id=1, source_target_pairs={{0,2},{1,3},{2,0},{3,1},{4,6},{5,7},{6,4},{7,5},{8,10},{9,11},{10,... | collective-permute-start | bytes 221192 | tf_op jit(solution)/shard_map/ppermute | solution.py:399
  85.8 35.8 %collective-permute-start.9 = (f32[144,128]{1,0:T(8,128)}, f32[144,128]{1,0:T(8,128)S(1)}, u32[]{:S(2)}, u32[]{:S(2)}) collective-permute-start(f32[144,128]{1,0:T(8,128)} %get-tuple-element.29), channel_id=1, source_target_pairs={{0,3},{1,2},{2,1},{3,0},{4,7},{5,6},{6,5},{7,4},{8,11},{9,10},{10,... | collective-permute-start | bytes 221192 | tf_op jit(solution)/shard_map/ppermute | solution.py:399
  86.2 35.5 %collective-permute-start.7 = (f32[144,128]{1,0:T(8,128)}, f32[144,128]{1,0:T(8,128)S(1)}, u32[]{:S(2)}, u32[]{:S(2)}) collective-permute-start(f32[144,128]{1,0:T(8,128)} %get-tuple-element.27), channel_id=1, source_target_pairs={{0,1},{1,0},{2,3},{3,2},{4,5},{5,4},{6,7},{7,6},{8,9},{9,8},{10,11... | collective-permute-start | bytes 221192 | tf_op jit(solution)/shard_map/ppermute | solution.py:399
  87.1 31.7 %all-to-all-start.1 = ((f32[16,1,128]{2,1,0:T(1,128)}), f32[16,1,128]{2,1,0:T(1,128)S(1)}, u32[]{:S(2)}, u32[]{:S(2)}) async-start(f32[16,1,128]{2,1,0:T(1,128)} %broadcast_in_dim.52), calls=%async_computation.1 | async-start | bytes 16384 | tf_op jit(solution)/shard_map/all_to_all | solution.py:398
  93.5 28.2 %copy-start = (f32[144,128]{1,0:T(8,128)S(1)}, f32[144,128]{1,0:T(8,128)}, u32[]{:S(2)}) copy-start(f32[144,128]{1,0:T(8,128)} %get-tuple-element.25) | copy-start | bytes 221188
  93.5 28.2 %copy-start.1 = (f32[144,128]{1,0:T(8,128)S(1)}, f32[144,128]{1,0:T(8,128)}, u32[]{:S(2)}) copy-start(f32[144,128]{1,0:T(8,128)} %get-tuple-element.26) | copy-start | bytes 221188
  116.6 5.1 %collective-permute-start.11 = (f32[144,128]{1,0:T(8,128)}, f32[144,128]{1,0:T(8,128)S(1)}, u32[]{:S(2)}, u32[]{:S(2)}) collective-permute-start(f32[144,128]{1,0:T(8,128)} %get-tuple-element.36), channel_id=1, source_target_pairs={{0,2},{1,3},{2,0},{3,1},{4,6},{5,7},{6,4},{7,5},{8,10},{9,11},{10,... | collective-permute-start | bytes 221192 | tf_op jit(solution)/shard_map/ppermute | solution.py:401
  117.5 5.4 %collective-permute-start.12 = (f32[144,128]{1,0:T(8,128)}, f32[144,128]{1,0:T(8,128)S(1)}, u32[]{:S(2)}, u32[]{:S(2)}) collective-permute-start(f32[144,128]{1,0:T(8,128)} %get-tuple-element.37), channel_id=1, source_target_pairs={{0,3},{1,2},{2,1},{3,0},{4,7},{5,6},{6,5},{7,4},{8,11},{9,10},{10,... | collective-permute-start | bytes 221192 | tf_op jit(solution)/shard_map/ppermute | solution.py:401
  121.5 1.6 %collective-permute-start.10 = (f32[144,128]{1,0:T(8,128)}, f32[144,128]{1,0:T(8,128)S(1)}, u32[]{:S(2)}, u32[]{:S(2)}) collective-permute-start(f32[144,128]{1,0:T(8,128)} %get-tuple-element.35), channel_id=1, source_target_pairs={{0,1},{1,0},{2,3},{3,2},{4,5},{5,4},{6,7},{7,6},{8,9},{9,8},{10,11... | collective-permute-start | bytes 221192 | tf_op jit(solution)/shard_map/ppermute | solution.py:401

commit v3 on v2

--- a/solution.py
+++ b/solution.py
@@ -12,11 +12,10 @@
 
 BF = jnp.bfloat16
 F32 = jnp.float32
-BLK = 16
 CHAN = ("chan_x", "chan_y", "chan_z")
 STN = "stn"
-NEAR = ("chan_x", "stn")
-OUTER = ("chan_y", "chan_z")
+OUTER = "chan_z"
+INNER = ("chan_x", "chan_y")
 smooth_weight = 0.05
 damping = 0.3
 
@@ -53,6 +52,10 @@
     return w2, sel_l, sel_c.reshape(32, 16)
 
 
+def operands():
+    return tuple(jnp.asarray(x, BF) for x in selections())
+
+
 def dot(a, b):
     return jnp.dot(a, b, preferred_element_type=F32)
 
@@ -79,6 +82,7 @@
 ROWS = 128
 LANES = 128
 TILES = ROWS // 16
+STEP = 2
 
 
 def weights_of(first, flags, wgt, groups):
@@ -94,10 +98,19 @@
         wgt[:, g * LANES:(g + 1) * LANES] = jnp.where(row_id == col_id, 0.0, full)
 
 
+def in_fours(turn):
+    def four(i, _):
+        for n in range(4):
+            turn(i * 4 + n)
+        return 0
+
+    lax.fori_loop(0, K // 4, four, 0)
+
+
 def model_operands(jall, me, w2, sell, wr, wi, lr):
     groups = jall.shape[0]
 
-    def turn(k, _):
+    def turn(k):
         for g in range(groups):
             w = dot(w2[0:64], parts_of(jall[g, pl.ds(k, 8, stride=16), :])).astype(BF)
             for b in range(2):
@@ -108,12 +121,11 @@
             l = dot_l(hm, sell[a]).astype(BF)
             for t in range(TILES):
                 lr[k, t, a * 16:(a + 1) * 16, :] = l[t * 16:(t + 1) * 16]
-        return 0
-
-    lax.fori_loop(0, K, turn, 0)
-
-
-def model(me_ref, own, mate, over, far, factor, coh, vis, flags, w2, sell, jall, res, wgt, sq, w_all, wr, wi, lr):
+
+    in_fours(turn)
+
+
+def model(me_ref, own, mate, over, far, factor, coh, vis, flags, w2, sell, smooth, earlier, jall, res, wgt, stats, w_all, wr, wi, lr):
     groups = jall.shape[0]
     t = pl.program_id(0)
     me = me_ref[0]
@@ -128,33 +140,43 @@
                 jall[g, at, :] = piece[0, at, :] * scale
         weights_of(me * ROWS, flags[0], w_all, groups)
         model_operands(jall, me, w2, sell, wr, wi, lr)
-        sq[...] = jnp.zeros_like(sq)
-
-    w_rows = w_all[pl.ds(pl.multiple_of(t * 16, 16), 16), :]
-    wgt[...] = w_rows
-    total = jnp.zeros((16, 128), F32)
-    for g in range(groups):
-        cols = slice(g * 128, (g + 1) * 128)
-        acc = [[[jnp.zeros((16, 128), F32)] * 2 for _ in range(2)] for _ in range(2)]
-        for k in range(K):
-            o_re = dot(lr[k, t], wr[k, g])
-            o_im = dot(lr[k, t], wi[k, g])
-            c_re = coh[0, k, 0, :, cols].astype(F32)
-            c_im = coh[0, k, 1, :, cols].astype(F32)
+        stats[...] = earlier[...]
+        stats[16:32] += smooth[...]
+
+    def tile(n, _):
+        rows = pl.ds(pl.multiple_of(n * 16, 16), 16)
+        at = t * STEP + n
+        w_rows = w_all[pl.ds(pl.multiple_of(at * 16, 16), 16), :]
+        wgt[rows, :] = w_rows
+        total = jnp.zeros((16, 128), F32)
+        used = jnp.zeros((16, 128), F32)
+        for g in range(groups):
+            cols = slice(g * 128, (g + 1) * 128)
+            acc = [[[jnp.zeros((16, 128), F32)] * 2 for _ in range(2)] for _ in range(2)]
+            for k in range(K):
+                o_re = dot(lr[k, at], wr[k, g])
+                o_im = dot(lr[k, at], wi[k, g])
+                c_re = coh[0, k, 0, rows, cols].astype(F32)
+                c_im = coh[0, k, 1, rows, cols].astype(F32)
+                for a in range(2):
+                    for b in range(2):
+                        re = o_re[a * 16:(a + 1) * 16, b * 128:(b + 1) * 128]
+                        im = o_im[a * 16:(a + 1) * 16, b * 128:(b + 1) * 128]
+                        acc[a][b] = [acc[a][b][0] + c_re * re - c_im * im,
+                                     acc[a][b][1] + c_re * im + c_im * re]
+            w = w_rows[:, cols]
+            used = used + w
             for a in range(2):
                 for b in range(2):
-                    re = o_re[a * 16:(a + 1) * 16, b * 128:(b + 1) * 128]
-                    im = o_im[a * 16:(a + 1) * 16, b * 128:(b + 1) * 128]
-                    acc[a][b] = [acc[a][b][0] + c_re * re - c_im * im,
-                                 acc[a][b][1] + c_re * im + c_im * re]
-        w = w_rows[:, cols]
-        for a in range(2):
-            for b in range(2):
-                for r in range(2):
-                    v = w * (vis[0, r, a, b, :, cols].astype(F32) - acc[a][b][r])
-                    res[b, r, a, :, cols] = v
-                    total = total + v * v
-    sq[...] += total[:8] + total[8:]
+                    for r in range(2):
+                        v = w * (vis[0, r, a, b, rows, cols].astype(F32) - acc[a][b][r])
+                        res[b, r, a, rows, cols] = v
+                        total = total + v * v
+        stats[0:8] += total[:8] + total[8:]
+        stats[8:16] += used[:8] + used[8:]
+        return 0
+
+    lax.fori_loop(0, STEP, tile, 0)
 
 
 def norms(x):
@@ -165,7 +187,7 @@
     groups = jall.shape[0]
     span = groups * LANES
 
-    def turn(k, _):
+    def turn(k):
         for g in range(groups):
             x = jall[g, pl.ds(k, 8, stride=16), :]
             w = dot(w2[64:128], parts_of(x)).astype(BF)
@@ -177,9 +199,8 @@
         for a in range(2):
             lc[k, :, a * 128:(a + 1) * 128] = c[a * 16:(a + 1) * 16]
         nr[k] = norms(x)
-        return 0
-
-    lax.fori_loop(0, K, turn, 0)
+
+    in_fours(turn)
 
 
 def gradient(coh, wgt, res, lq, lc, nq, nr, bufs, row, col, groups, rest):
@@ -293,11 +314,14 @@
     return pl.BlockSpec(shape, lambda i: (0,) * len(shape))
 
 
-def call_model(f, me, pieces, factor, coh, vis, flags, sels):
+def call_model(f, me, pieces, factor, coh, vis, flags, sels, smooth, earlier):
     G = factor.shape[0]
     S = G * LANES
     sc = operand_scratch(G)
-    outs = [((G, 8 * K, LANES), None), ((2, 2, 2, ROWS, S), 3), ((ROWS, S), 0), ((8, 128), None)]
+    outs = [((G, 8 * K, LANES), None), ((2, 2, 2, ROWS, S), 3), ((ROWS, S), 0), ((32, LANES), None)]
+
+    if earlier is None:
+        earlier, smooth = jnp.zeros((32, LANES), F32), jnp.zeros((16, LANES), F32)
 
     def piece_spec(x):
         at = f if x.shape[0] > 1 else 0
@@ -306,23 +330,24 @@
     def out_spec(shape, dim):
         if dim is None:
             return spec(shape)
-        block = shape[:dim] + (16,) + shape[dim + 1:]
+        block = shape[:dim] + (16 * STEP,) + shape[dim + 1:]
         return pl.BlockSpec(block, lambda i: tuple(i if d == dim else 0 for d in range(len(shape))))
 
     return pl.pallas_call(
-        model, grid=(TILES,),
+        model, grid=(TILES // STEP,),
         out_shape=[jax.ShapeDtypeStruct(s, F32) for s, _ in outs],
         in_specs=[pl.BlockSpec(memory_space=pltpu.SMEM)] + [piece_spec(x) for x in pieces] + [
             whole(factor),
-            pl.BlockSpec((1, K, 2, 16, S), lambda i: (f, 0, 0, i, 0)),
-            pl.BlockSpec((1, 2, 2, 2, 16, S), lambda i: (f, 0, 0, 0, i, 0)),
+            pl.BlockSpec((1, K, 2, 16 * STEP, S), lambda i: (f, 0, 0, i, 0)),
+            pl.BlockSpec((1, 2, 2, 2, 16 * STEP, S), lambda i: (f, 0, 0, 0, i, 0)),
             pl.BlockSpec((1, *flags.shape[1:]), lambda i: (f, 0, 0)),
-            whole(sels[0]), whole(sels[1]),
+            whole(sels[0]), whole(sels[1]), whole(smooth), whole(earlier),
         ],
         out_specs=[out_spec(*o) for o in outs],
         scratch_shapes=[pltpu.VMEM((ROWS, S), F32), *sc["model"]],
         cost_estimate=pl.CostEstimate(flops=8_000_000_000, bytes_accessed=10_000_000, transcendentals=0),
-    )(me, *pieces, factor, coh, vis, flags, sels[0], sels[1])
+        compiler_params=pltpu.CompilerParams(vmem_limit_bytes=24 << 20),
+    )(me, *pieces, factor, coh, vis, flags, sels[0], sels[1], smooth, earlier)
 
 
 def call_grad(f, me, jall, coh, res, wgt, sels):
@@ -338,6 +363,7 @@
         scratch_shapes=[pltpu.VMEM(coh.shape[1:], BF), pltpu.VMEM(res.shape, F32), pltpu.SemaphoreType.DMA((3,)),
                         pltpu.VMEM((G, 9 * K, ROWS), F32), *sc["grad"], *sc["bufs"]],
         cost_estimate=pl.CostEstimate(flops=20_000_000_000, bytes_accessed=10_000_000, transcendentals=0),
+        compiler_params=pltpu.CompilerParams(vmem_limit_bytes=36 << 20),
     )(me, jall, coh, res, wgt, sels[0], sels[2])
 
 
@@ -349,6 +375,14 @@
 
 def hop_pairs(hop, count):
     return [(i, i ^ hop) for i in range(count)]
+
+
+def summed(values, axes):
+    count = lax.axis_size(axes)
+    parts = [values] + [lax.ppermute(values, axes, hop_pairs(hop, count)) for hop in range(1, count)]
+    while len(parts) > 1:
+        parts = [parts[i] + parts[i + 1] for i in range(0, len(parts), 2)]
+    return parts[0]
 
 
 def on_device(gains, coherency, vis_data, flags, beam, group_of):
@@ -357,7 +391,6 @@
     stn_count = lax.axis_size(STN)
     chan_count = lax.axis_size(CHAN)
     me = lax.axis_index(STN).astype(jnp.int32)
-    first_row = me * row_count
     all_channels = chan_dev * chan_count
     all_stations = row_count * stn_count
 
@@ -379,29 +412,23 @@
     second = second * inside[:, None, None, None, None, None]
     smooth_grad = second[:-2] - 2.0 * second[1:-1] + second[2:]
     own_second = second[1:-1]
-    smooth_local = jnp.sum(own_second * own_second)
-
-    blocks = jnp.arange(flags.shape[1], dtype=jnp.int32) + first_row // BLK
-    selves = blocks[:, None] == jnp.arange(flags.shape[2], dtype=jnp.int32)[None, :]
-    local_count = jnp.sum(flags * jnp.where(selves, BLK * (BLK - 1), BLK * BLK)[None]).astype(F32)
-
-    sels = tuple(jnp.asarray(x, BF) for x in selections())
+    smooth_local = jnp.sum(own_second * own_second, axis=(0, 1, 2, 3))
+
+    sels = operands()
     me1 = me[None]
-    jall0, res0, wgt0, sq0 = call_model(0, me1, (raw, mate, over[0], far[0]), factor, coherency, vis_data, flags, sels)
-    jall1, res1, wgt1, sq1 = call_model(1, me1, (raw, mate, over[1], far[1]), factor, coherency, vis_data, flags, sels)
-    lane = jnp.arange(row_count)
-    packed = jnp.where(lane == 0, local_count, jnp.where(lane == 1, jnp.sum(sq0 + sq1), jnp.where(lane == 2, smooth_local, 0.0)))
-
-    arrived = lax.all_to_all(jnp.broadcast_to(packed, (lax.axis_size(NEAR), row_count)), NEAR, 0, 0, tiled=True)
+    jall0, res0, wgt0, stats = call_model(0, me1, (raw, mate, over[0], far[0]), factor, coherency, vis_data, flags, sels, None, None)
+    jall1, res1, wgt1, stats = call_model(1, me1, (raw, mate, over[1], far[1]), factor, coherency, vis_data, flags, sels, smooth_local, stats)
+
+    stats = summed(stats, OUTER)
     row0, *cols0 = call_grad(0, me1, jall0, coherency, res0, wgt0, sels)
-    partial = jnp.sum(arrived, axis=0)
-    arrived = lax.all_to_all(jnp.broadcast_to(partial, (lax.axis_size(OUTER), row_count)), OUTER, 0, 0, tiled=True)
+    stats = summed(stats, INNER)
     cols0 = cols0[:1] + [lax.ppermute(cols0[h], STN, hop_pairs(h, stn_count)) for h in range(1, stn_count)]
     row1, *cols1 = call_grad(1, me1, jall1, coherency, res1, wgt1, sels)
     cols1 = cols1[:1] + [lax.ppermute(cols1[h], STN, hop_pairs(h, stn_count)) for h in range(1, stn_count)]
-    totals = jnp.sum(arrived, axis=0)
-
-    norm_scale = all_channels * all_stations / totals[0]
+    stats = summed(stats, STN)
+    sq, count, smooth = jnp.sum(stats[:8]), jnp.sum(stats[8:16]), jnp.sum(stats[16:])
+
+    norm_scale = all_channels * all_stations / count
     steps = []
     for f, (row, cols) in enumerate(((row0, cols0), (row1, cols1))):
         both = row + (cols[0] + cols[1]) + (cols[2] + cols[3])
@@ -411,7 +438,7 @@
         curvature = norm_scale * row_factor * row_factor * curv + damping
         steps.append(gradient_f / curvature)
     gain_step = jnp.stack(steps)
-    loss_value = (norm_scale * totals[1] + smooth_weight * totals[2]) / (all_channels * all_stations)
+    loss_value = (norm_scale * sq + smooth_weight * smooth) / (all_channels * all_stations)
     return gain_step, loss_value
 
 

time: 127 us -> 141 us (1.11)
  starting transfers between devices: 33.7 us -> 53.4 us
  Pallas kernels: 72.4 us -> 57.7 us
  local copies, waits for them, and re-layouts: 4.7 us -> 15.9 us
  other arithmetic: 8.95 us -> 5.56 us
  waiting for transfers between devices: 1.4 us -> 3.92 us
    ppermute x0 -> x17, starting transfers between devices: none -> 32.4 us  [summed(): lax.ppermute(values, axes, hop_pairs(hop, count))]
    all_to_all x2 -> x0, starting transfers between devices: 17.8 us -> none  [the longest x1 11.5 us: on_device(): lax.all_to_all(jnp.broadcast_to(packed, (lax.axis_size(NEAR), row_count))...]
    unnamed x16 -> x38, local copies, waits for them, and re-layouts: 1.3 us -> 14.9 us
    pallas_call x2, Pallas kernels: 26.3 us -> 16.9 us  [call_model(): pl.pallas_call(model, grid=(TILES // STEP,), out_shape=[jax.ShapeDtypeStr...]
    pallas_call x2, Pallas kernels: 46.2 us -> 40.7 us  [call_grad(): pl.pallas_call(functools.partial(grad_kernel, f), grid=(1,), out_shape=[j...]
    ppermute x3, starting transfers between devices: 2.11 us -> 5.86 us  [on_device(): lax.ppermute(cols0[h], STN, hop_pairs(h, stn_count))]
    ppermute x0 -> x17, waiting for transfers between devices: none -> 2.92 us  [summed(): lax.ppermute(values, axes, hop_pairs(hop, count))]
    reduce_sum x5 -> x3, other arithmetic: 3.29 us -> 1.23 us  [the longest x1 0.6 us: on_device(): jnp.sum(stats[:8])]
  transfers between devices with their start and end apart: 15 -> 30, of which waited for: 2 -> 5; matrix products, arithmetic and copies ran while one was open for 6% -> 4% of each run, Pallas kernels for 47% -> 35%
where the time goes in v3:
time: 141 us
  Pallas kernels  57.7 us (41%)
  starting transfers between devices  53.4 us (38%)
  local copies, waits for them, and re-layouts  15.9 us (11%)
  other arithmetic  5.56 us (4%)
  between operations  4.18 us (3%)
  waiting for transfers between devices  3.92 us (3%)
    pallas_call x2, Pallas kernels, call_grad(): pl.pallas_call(functools.partial(grad_kernel, f), grid=(1,), out_shape=[j...  40.7 us
    ppermute x17, starting transfers between devices, summed(): lax.ppermute(values, axes, hop_pairs(hop, count))  32.4 us
    pallas_call x2, Pallas kernels, call_model(): pl.pallas_call(model, grid=(TILES // STEP,), out_shape=[jax.ShapeDtypeStr...  16.9 us
    unnamed x38, local copies, waits for them, and re-layouts  14.9 us
    ppermute x3, starting transfers between devices, on_device(): lax.ppermute(cols0[h], STN, hop_pairs(h, stn_count))  5.86 us
    ppermute x1, starting transfers between devices, on_device(): lax.ppermute(gains, CHAN, up)  5 us
    ppermute x17, waiting for transfers between devices, summed(): lax.ppermute(values, axes, hop_pairs(hop, count))  2.92 us
    ppermute x1, starting transfers between devices, on_device(): mate = lax.ppermute(raw, STN, hop_pairs(1, stn_count))  2.85 us
  transfers between devices with their start and end apart: 30, of which 5 were waited for; matrix products, arithmetic and copies ran while one was open for 4% of the time, Pallas kernels for 35%

profile of v3, /device:TPU:1, one launch (start us, length us, event | category | flops | bytes accessed | tf_op | source)
XLA Modules:
  0.0 140.6 jit_solution(15993815915005702931)
XLA Ops:
  0.6 1.3 collective-permute-start.3
  1.9 5.0 %collective-permute-start.4 = (f32[2,2,2,2,16,128]{5,4,3,2,1,0:T(8,128)}, f32[2,2,2,2,16,128]{5,4,3,2,1,0:T(8,128)S(1)}, u32[]{:S(2)}, u32[]{:S(2)}) collective-permute-start(f32[2,2,2,2,16,128]{5,4,3,2,1,0:T(8,128)} %param.9), channel_id=1, source_target_pairs={{0,4},{4,8},{8,12},{12,16},{16,20},{20,24},{24,28},{28,32},{32,36}... | collective-permute-start | bytes 393224 | tf_op jit(solution)/shard_map/ppermute | solution.py:407
  6.9 2.8 %collective-permute-start = (f32[2,128,128]{2,1,0:T(8,128)}, f32[2,128,128]{2,1,0:T(8,128)S(1)}, u32[]{:S(2)}, u32[]{:S(2)}) collective-permute-start(f32[2,128,128]{2,1,0:T(8,128)} %bitcast.38), channel_id=1, source_target_pairs={{0,1},{1,0},{2,3},{3,2},{4,5},{5,4},{6,7},{7,6},{8,9},{9,8},{10,11... | collective-permute-start | bytes 393224 | tf_op jit(solution)/shard_map/ppermute | solution.py:399
  10.8 1.5 %collective-permute-start.1 = (f32[1,128,128]{2,1,0:T(8,128)S(1)}, f32[1,128,128]{2,1,0:T(8,128)S(1)}, u32[]{:S(2)}, u32[]{:S(2)}) collective-permute-start(f32[1,128,128]{2,1,0:T(8,128)S(1)} %bitcast.43), channel_id=1, source_target_pairs={{0,2},{1,3},{2,0},{3,1},{4,6},{5,7},{6,4},{7,5},{8,10},{9,11},{10,... | collective-permute-start | bytes 196616 | tf_op jit(solution)/shard_map/ppermute | solution.py:398
  14.4 1.3 collective-permute-start.6
  16.7 1.1 fusion.3
  18.8 3.4 %copy-done.1 = bf16[2,16,2,128,512]{4,3,2,1,0:T(8,128)(2,1)S(1)} copy-done((bf16[2,16,2,128,512]{4,3,2,1,0:T(8,128)(2,1)S(1)}, bf16[2,16,2,128,512]{4,3,2,1,0:T(8,128)(2,1)}, u32[]{:S(2)}) %copy-start.1) | copy-done | bytes 8388632
  22.2 1.6 %copy-done.4 = bf16[2,2,2,2,128,512]{5,4,3,2,1,0:T(8,128)(2,1)S(1)} copy-done((bf16[2,2,2,2,128,512]{5,4,3,2,1,0:T(8,128)(2,1)S(1)}, bf16[2,2,2,2,128,512]{5,4,3,2,1,0:T(8,128)(2,1)}, u32[]{:S(2)}) %copy-start.4) | copy-done | bytes 2097176
  25.9 8.5 %shard_map.104 = (f32[4,128,128]{2,1,0:T(8,128)S(1)}, f32[2,2,2,128,512]{4,3,2,1,0:T(8,128)S(1)}, f32[128,512]{1,0:T(8,128)S(1)}, f32[32,128]{1,0:T(8,128)S(1)}) custom-call(s32[1]{0:T(128)} %bitcast.me_ref, f32[2,128,128]{2,1,0:T(8,128)S(1)} %bitcast.39, f32[2,128,128]{2,1,0:T(8,128)S(1)} %collective-permute-done.mate, ...), custom_call_target="tpu_custom_call" | custom-call | flops 8000000000 | bytes 10000000 | tf_op jit(solution)/shard_map/pallas_call | solution.py:336
  34.5 8.5 %shard_map.105 = (f32[4,128,128]{2,1,0:T(8,128)S(1)}, f32[2,2,2,128,512]{4,3,2,1,0:T(8,128)S(1)}, f32[128,512]{1,0:T(8,128)S(1)}, f32[32,128]{1,0:T(8,128)S(1)}) custom-call(s32[1]{0:T(128)} %bitcast.me_ref, f32[2,128,128]{2,1,0:T(8,128)S(1)} %bitcast.40, f32[2,128,128]{2,1,0:T(8,128)S(1)} %collective-permute-done.mate, ...), custom_call_target="tpu_custom_call" | custom-call | flops 8000000000 | bytes 10000000 | tf_op jit(solution)/shard_map/pallas_call | solution.py:336
  43.0 4.4 %collective-permute-start.12 = (f32[32,128]{1,0:T(8,128)S(1)}, f32[32,128]{1,0:T(8,128)S(1)}, u32[]{:S(2)}, u32[]{:S(2)}) collective-permute-start(f32[32,128]{1,0:T(8,128)S(1)} %get-tuple-element.21), channel_id=1, source_target_pairs={{0,24},{4,28},{8,16},{12,20},{16,8},{20,12},{24,0},{28,4},{1,25},{... | collective-permute-start | bytes 49160 | tf_op jit(solution)/shard_map/ppermute | solution.py:382
  47.4 3.3 %collective-permute-start.13 = (f32[32,128]{1,0:T(8,128)S(1)}, f32[32,128]{1,0:T(8,128)S(1)}, u32[]{:S(2)}, u32[]{:S(2)}) collective-permute-start(f32[32,128]{1,0:T(8,128)S(1)} %get-tuple-element.21), channel_id=1, source_target_pairs={{0,28},{4,24},{8,20},{12,16},{16,12},{20,8},{24,4},{28,0},{1,29},{... | collective-permute-start | bytes 49160 | tf_op jit(solution)/shard_map/ppermute | solution.py:382
  51.4 4.5 %collective-permute-start.11 = (f32[32,128]{1,0:T(8,128)S(1)}, f32[32,128]{1,0:T(8,128)S(1)}, u32[]{:S(2)}, u32[]{:S(2)}) collective-permute-start(f32[32,128]{1,0:T(8,128)S(1)} %get-tuple-element.21), channel_id=1, source_target_pairs={{0,20},{4,16},{8,28},{12,24},{16,4},{20,0},{24,12},{28,8},{1,21},{... | collective-permute-start | bytes 49160 | tf_op jit(solution)/shard_map/ppermute | solution.py:382
  55.9 1.2 collective-permute-start.8
  57.1 1.3 collective-permute-start.9
  58.6 1.2 collective-permute-done.8
  59.9 1.7 %collective-permute-done.9 = f32[32,128]{1,0:T(8,128)S(1)} collective-permute-done((f32[32,128]{1,0:T(8,128)S(1)}, f32[32,128]{1,0:T(8,128)S(1)}, u32[]{:S(2)}, u32[]{:S(2)}) %collective-permute-start.9) | collective-permute-done | bytes 16416 | tf_op jit(solution)/shard_map/ppermute | solution.py:382
  61.5 5.2 %collective-permute-start.19 = (f32[32,128]{1,0:T(8,128)S(1)}, f32[32,128]{1,0:T(8,128)S(1)}, u32[]{:S(2)}, u32[]{:S(2)}) collective-permute-start(f32[32,128]{1,0:T(8,128)S(1)} %add_add_fusion.4), channel_id=1, source_target_pairs={{0,192},{32,224},{64,128},{96,160},{128,64},{160,96},{192,0},{224,... | collective-permute-start | bytes 49160 | tf_op jit(solution)/shard_map/ppermute | solution.py:382
  66.7 1.1 collective-permute-start.20
  67.8 1.6 %collective-permute-start.17 = (f32[32,128]{1,0:T(8,128)S(1)}, f32[32,128]{1,0:T(8,128)S(1)}, u32[]{:S(2)}, u32[]{:S(2)}) collective-permute-start(f32[32,128]{1,0:T(8,128)S(1)} %add_add_fusion.4), channel_id=1, source_target_pairs={{0,128},{32,160},{64,192},{96,224},{128,0},{160,32},{192,64},{224,... | collective-permute-start | bytes 49160 | tf_op jit(solution)/shard_map/ppermute | solution.py:382
  69.5 2.9 %collective-permute-start.18 = (f32[32,128]{1,0:T(8,128)S(1)}, f32[32,128]{1,0:T(8,128)S(1)}, u32[]{:S(2)}, u32[]{:S(2)}) collective-permute-start(f32[32,128]{1,0:T(8,128)S(1)} %add_add_fusion.4), channel_id=1, source_target_pairs={{0,160},{32,128},{64,224},{96,192},{128,32},{160,0},{192,96},{224,... | collective-permute-start | bytes 49160 | tf_op jit(solution)/shard_map/ppermute | solution.py:382
  72.6 2.2 %collective-permute-start.16 = (f32[32,128]{1,0:T(8,128)S(1)}, f32[32,128]{1,0:T(8,128)S(1)}, u32[]{:S(2)}, u32[]{:S(2)}) collective-permute-start(f32[32,128]{1,0:T(8,128)S(1)} %add_add_fusion.4), channel_id=1, source_target_pairs={{0,96},{32,64},{64,32},{96,0},{128,224},{160,192},{192,160},{224,1... | collective-permute-start | bytes 49160 | tf_op jit(solution)/shard_map/ppermute | solution.py:382
  74.8 1.7 %collective-permute-start.14 = (f32[32,128]{1,0:T(8,128)S(1)}, f32[32,128]{1,0:T(8,128)S(1)}, u32[]{:S(2)}, u32[]{:S(2)}) collective-permute-start(f32[32,128]{1,0:T(8,128)S(1)} %add_add_fusion.4), channel_id=1, source_target_pairs={{0,32},{32,0},{64,96},{96,64},{128,160},{160,128},{192,224},{224,1... | collective-permute-start | bytes 49160 | tf_op jit(solution)/shard_map/ppermute | solution.py:382
  76.5 3.4 %copy-done.3 = bf16[2,16,2,128,512]{4,3,2,1,0:T(8,128)(2,1)S(1)} copy-done((bf16[2,16,2,128,512]{4,3,2,1,0:T(8,128)(2,1)S(1)}, bf16[2,16,2,128,512]{4,3,2,1,0:T(8,128)(2,1)}, u32[]{:S(2)}) %copy-start.3) | copy-done | bytes 8388632
  79.9 1.6 %copy-done.14 = f32[2,2,2,128,512]{4,3,2,1,0:T(8,128)S(1)} copy-done((f32[2,2,2,128,512]{4,3,2,1,0:T(8,128)S(1)}, f32[2,2,2,128,512]{4,3,2,1,0:T(8,128)}, u32[]{:S(2)}) %copy-start.14) | copy-done | bytes 2097176
  81.5 0.9 copy-done.16
  83.4 20.4 %shard_map.106 = (f32[144,128]{1,0:T(8,128)S(1)}, f32[144,128]{1,0:T(8,128)S(1)}, f32[144,128]{1,0:T(8,128)S(1)}, f32[144,128]{1,0:T(8,128)S(1)}, f32[144,128]{1,0:T(8,128)S(1)}) custom-call(s32[1]{0:T(128)} %bitcast.me_ref, f32[4,128,128]{2,1,0:T(8,128)S(1)} %copy-done.16, bf16[2,16,2,128,512]{4,3,2,1,0:T(8,128)(2,1)S(1)} %copy-done.3, ...), custom_call_target="tpu_custom_call" | custom-call | flops 20000000000 | bytes 10000000 | tf_op jit(solution)/shard_map/pallas_call | solution.py:357
  104.0 5.5 %collective-permute-start.26 = (f32[144,128]{1,0:T(8,128)S(1)}, f32[144,128]{1,0:T(8,128)}, u32[]{:S(2)}, u32[]{:S(2)}) collective-permute-start(f32[144,128]{1,0:T(8,128)S(1)} %get-tuple-element.29), channel_id=1, source_target_pairs={{0,3},{1,2},{2,1},{3,0},{4,7},{5,6},{6,5},{7,4},{8,11},{9,10},{10,... | collective-permute-start | bytes 221192 | tf_op jit(solution)/shard_map/ppermute | solution.py:425
  110.2 1.3 collective-permute-start.21
  111.5 20.4 %shard_map.107 = (f32[144,128]{1,0:T(8,128)S(1)}, f32[144,128]{1,0:T(8,128)S(1)}, f32[144,128]{1,0:T(8,128)S(1)}, f32[144,128]{1,0:T(8,128)S(1)}, f32[144,128]{1,0:T(8,128)S(1)}) custom-call(s32[1]{0:T(128)} %bitcast.me_ref, f32[4,128,128]{2,1,0:T(8,128)S(1)} %get-tuple-element.30.jall, bf16[2,16,2,128,512]{4,3,2,1,0:T(8,128)(2,1)S(1)} %copy-done.3, ...), custom_call_target="tpu_custom_call" | custom-call | flops 20000000000 | bytes 10000000 | tf_op jit(solution)/shard_map/pallas_call | solution.py:357
  132.4 1.7 %collective-permute-start.29 = (f32[144,128]{1,0:T(8,128)S(1)}, f32[144,128]{1,0:T(8,128)S(1)}, u32[]{:S(2)}, u32[]{:S(2)}) collective-permute-start(f32[144,128]{1,0:T(8,128)S(1)} %get-tuple-element.37), channel_id=1, source_target_pairs={{0,3},{1,2},{2,1},{3,0},{4,7},{5,6},{6,5},{7,4},{8,11},{9,10},{10,... | collective-permute-start | bytes 221192 | tf_op jit(solution)/shard_map/ppermute | solution.py:427
  137.5 1.0 add_add_fusion.1
  (93 shorter events, 13.2 us)
Async XLA Ops:
  0.6 16.0 %collective-permute-start.3 = (f32[2,2,2,2,16,128]{5,4,3,2,1,0:T(8,128)}, f32[2,2,2,2,16,128]{5,4,3,2,1,0:T(8,128)S(1)}, u32[]{:S(2)}, u32[]{:S(2)}) collective-permute-start(f32[2,2,2,2,16,128]{5,4,3,2,1,0:T(8,128)} %param.9), channel_id=1, source_target_pairs={{4,0},{8,4},{12,8},{16,12},{20,16},{24,20},{28,24},{32,28},{36,32}... | collective-permute-start | bytes 393224 | tf_op jit(solution)/shard_map/ppermute | solution.py:407
  1.9 14.7 %collective-permute-start.4 = (f32[2,2,2,2,16,128]{5,4,3,2,1,0:T(8,128)}, f32[2,2,2,2,16,128]{5,4,3,2,1,0:T(8,128)S(1)}, u32[]{:S(2)}, u32[]{:S(2)}) collective-permute-start(f32[2,2,2,2,16,128]{5,4,3,2,1,0:T(8,128)} %param.9), channel_id=1, source_target_pairs={{0,4},{4,8},{8,12},{12,16},{16,20},{20,24},{24,28},{28,32},{32,36}... | collective-permute-start | bytes 393224 | tf_op jit(solution)/shard_map/ppermute | solution.py:407
  6.9 10.9 %collective-permute-start = (f32[2,128,128]{2,1,0:T(8,128)}, f32[2,128,128]{2,1,0:T(8,128)S(1)}, u32[]{:S(2)}, u32[]{:S(2)}) collective-permute-start(f32[2,128,128]{2,1,0:T(8,128)} %bitcast.38), channel_id=1, source_target_pairs={{0,1},{1,0},{2,3},{3,2},{4,5},{5,4},{6,7},{7,6},{8,9},{9,8},{10,11... | collective-permute-start | bytes 393224 | tf_op jit(solution)/shard_map/ppermute | solution.py:399
  10.7 3.7 %collective-permute-start.5 = (f32[1,128,128]{2,1,0:T(8,128)S(1)}, f32[1,128,128]{2,1,0:T(8,128)S(1)}, u32[]{:S(2)}, u32[]{:S(2)}) collective-permute-start(f32[1,128,128]{2,1,0:T(8,128)S(1)} %bitcast.44), channel_id=1, source_target_pairs={{0,2},{1,3},{2,0},{3,1},{4,6},{5,7},{6,4},{7,5},{8,10},{9,11},{10,... | collective-permute-start | bytes 196616 | tf_op jit(solution)/shard_map/ppermute | solution.py:398
  10.8 5.0 %collective-permute-start.1 = (f32[1,128,128]{2,1,0:T(8,128)S(1)}, f32[1,128,128]{2,1,0:T(8,128)S(1)}, u32[]{:S(2)}, u32[]{:S(2)}) collective-permute-start(f32[1,128,128]{2,1,0:T(8,128)S(1)} %bitcast.43), channel_id=1, source_target_pairs={{0,2},{1,3},{2,0},{3,1},{4,6},{5,7},{6,4},{7,5},{8,10},{9,11},{10,... | collective-permute-start | bytes 196616 | tf_op jit(solution)/shard_map/ppermute | solution.py:398
  14.4 3.4 %collective-permute-start.6 = (f32[1,128,128]{2,1,0:T(8,128)S(1)}, f32[1,128,128]{2,1,0:T(8,128)S(1)}, u32[]{:S(2)}, u32[]{:S(2)}) collective-permute-start(f32[1,128,128]{2,1,0:T(8,128)S(1)} %collective-permute-done.5.over), channel_id=1, source_target_pairs={{0,1},{1,0},{2,3},{3,2},{4,5},{5,4},{6,7},{7,6},{8,9},{9,8},{10,11... | collective-permute-start | bytes 196616 | tf_op jit(solution)/shard_map/ppermute | solution.py:400
  15.8 18.7 %collective-permute-start.2 = (f32[1,128,128]{2,1,0:T(8,128)S(1)}, f32[1,128,128]{2,1,0:T(8,128)S(1)}, u32[]{:S(2)}, u32[]{:S(2)}) collective-permute-start(f32[1,128,128]{2,1,0:T(8,128)S(1)} %collective-permute-done.1.over), channel_id=1, source_target_pairs={{0,1},{1,0},{2,3},{3,2},{4,5},{5,4},{6,7},{7,6},{8,9},{9,8},{10,11... | collective-permute-start | bytes 196616 | tf_op jit(solution)/shard_map/ppermute | solution.py:401
  34.5 42.0 %copy-start.9 = (bf16[128,16]{1,0:T(8,128)(2,1)S(1)}, bf16[128,16]{1,0:T(8,128)(2,1)}, u32[]{:S(2)}) copy-start(bf16[128,16]{1,0:T(8,128)(2,1)} %constant.60.clone.w2) | copy-start | bytes 12292
  34.5 42.0 %copy-start.10 = (bf16[32,16]{1,0:T(8,128)(2,1)S(1)}, bf16[32,16]{1,0:T(8,128)(2,1)}, u32[]{:S(2)}) copy-start(bf16[32,16]{1,0:T(8,128)(2,1)} %constant.62.clone.selc) | copy-start | bytes 3076
  43.0 14.1 %collective-permute-start.12 = (f32[32,128]{1,0:T(8,128)S(1)}, f32[32,128]{1,0:T(8,128)S(1)}, u32[]{:S(2)}, u32[]{:S(2)}) collective-permute-start(f32[32,128]{1,0:T(8,128)S(1)} %get-tuple-element.21), channel_id=1, source_target_pairs={{0,24},{4,28},{8,16},{12,20},{16,8},{20,12},{24,0},{28,4},{1,25},{... | collective-permute-start | bytes 49160 | tf_op jit(solution)/shard_map/ppermute | solution.py:382
  47.4 11.0 %collective-permute-start.13 = (f32[32,128]{1,0:T(8,128)S(1)}, f32[32,128]{1,0:T(8,128)S(1)}, u32[]{:S(2)}, u32[]{:S(2)}) collective-permute-start(f32[32,128]{1,0:T(8,128)S(1)} %get-tuple-element.21), channel_id=1, source_target_pairs={{0,28},{4,24},{8,20},{12,16},{16,12},{20,8},{24,4},{28,0},{1,29},{... | collective-permute-start | bytes 49160 | tf_op jit(solution)/shard_map/ppermute | solution.py:382
  50.7 8.0 %collective-permute-start.10 = (f32[32,128]{1,0:T(8,128)S(1)}, f32[32,128]{1,0:T(8,128)S(1)}, u32[]{:S(2)}, u32[]{:S(2)}) collective-permute-start(f32[32,128]{1,0:T(8,128)S(1)} %get-tuple-element.21), channel_id=1, source_target_pairs={{0,16},{4,20},{8,24},{12,28},{16,0},{20,4},{24,8},{28,12},{1,17},{... | collective-permute-start | bytes 49160 | tf_op jit(solution)/shard_map/ppermute | solution.py:382
  51.4 7.2 %collective-permute-start.11 = (f32[32,128]{1,0:T(8,128)S(1)}, f32[32,128]{1,0:T(8,128)S(1)}, u32[]{:S(2)}, u32[]{:S(2)}) collective-permute-start(f32[32,128]{1,0:T(8,128)S(1)} %get-tuple-element.21), channel_id=1, source_target_pairs={{0,20},{4,16},{8,28},{12,24},{16,4},{20,0},{24,12},{28,8},{1,21},{... | collective-permute-start | bytes 49160 | tf_op jit(solution)/shard_map/ppermute | solution.py:382
  55.9 3.9 %collective-permute-start.8 = (f32[32,128]{1,0:T(8,128)S(1)}, f32[32,128]{1,0:T(8,128)S(1)}, u32[]{:S(2)}, u32[]{:S(2)}) collective-permute-start(f32[32,128]{1,0:T(8,128)S(1)} %get-tuple-element.21), channel_id=1, source_target_pairs={{0,8},{4,12},{8,0},{12,4},{16,24},{20,28},{24,16},{28,20},{1,9},{5... | collective-permute-start | bytes 49160 | tf_op jit(solution)/shard_map/ppermute | solution.py:382
  57.1 4.4 %collective-permute-start.9 = (f32[32,128]{1,0:T(8,128)S(1)}, f32[32,128]{1,0:T(8,128)S(1)}, u32[]{:S(2)}, u32[]{:S(2)}) collective-permute-start(f32[32,128]{1,0:T(8,128)S(1)} %get-tuple-element.21), channel_id=1, source_target_pairs={{0,12},{4,8},{8,4},{12,0},{16,28},{20,24},{24,20},{28,16},{1,13},{... | collective-permute-start | bytes 49160 | tf_op jit(solution)/shard_map/ppermute | solution.py:382
  58.4 3.1 %collective-permute-start.7 = (f32[32,128]{1,0:T(8,128)S(1)}, f32[32,128]{1,0:T(8,128)S(1)}, u32[]{:S(2)}, u32[]{:S(2)}) collective-permute-start(f32[32,128]{1,0:T(8,128)S(1)} %get-tuple-element.21), channel_id=1, source_target_pairs={{0,4},{4,0},{8,12},{12,8},{16,20},{20,16},{24,28},{28,24},{1,5},{5... | collective-permute-start | bytes 49160 | tf_op jit(solution)/shard_map/ppermute | solution.py:382
  61.5 11.1 %collective-permute-start.19 = (f32[32,128]{1,0:T(8,128)S(1)}, f32[32,128]{1,0:T(8,128)S(1)}, u32[]{:S(2)}, u32[]{:S(2)}) collective-permute-start(f32[32,128]{1,0:T(8,128)S(1)} %add_add_fusion.4), channel_id=1, source_target_pairs={{0,192},{32,224},{64,128},{96,160},{128,64},{160,96},{192,0},{224,... | collective-permute-start | bytes 49160 | tf_op jit(solution)/shard_map/ppermute | solution.py:382
  66.7 8.0 %collective-permute-start.20 = (f32[32,128]{1,0:T(8,128)S(1)}, f32[32,128]{1,0:T(8,128)S(1)}, u32[]{:S(2)}, u32[]{:S(2)}) collective-permute-start(f32[32,128]{1,0:T(8,128)S(1)} %add_add_fusion.4), channel_id=1, source_target_pairs={{0,224},{32,192},{64,160},{96,128},{128,96},{160,64},{192,32},{224... | collective-permute-start | bytes 49160 | tf_op jit(solution)/shard_map/ppermute | solution.py:382
  67.8 35.9 %collective-permute-start.17 = (f32[32,128]{1,0:T(8,128)S(1)}, f32[32,128]{1,0:T(8,128)S(1)}, u32[]{:S(2)}, u32[]{:S(2)}) collective-permute-start(f32[32,128]{1,0:T(8,128)S(1)} %add_add_fusion.4), channel_id=1, source_target_pairs={{0,128},{32,160},{64,192},{96,224},{128,0},{160,32},{192,64},{224,... | collective-permute-start | bytes 49160 | tf_op jit(solution)/shard_map/ppermute | solution.py:382
  69.5 34.6 %collective-permute-start.18 = (f32[32,128]{1,0:T(8,128)S(1)}, f32[32,128]{1,0:T(8,128)S(1)}, u32[]{:S(2)}, u32[]{:S(2)}) collective-permute-start(f32[32,128]{1,0:T(8,128)S(1)} %add_add_fusion.4), channel_id=1, source_target_pairs={{0,160},{32,128},{64,224},{96,192},{128,32},{160,0},{192,96},{224,... | collective-permute-start | bytes 49160 | tf_op jit(solution)/shard_map/ppermute | solution.py:382
  72.3 37.2 %collective-permute-start.15 = (f32[32,128]{1,0:T(8,128)S(1)}, f32[32,128]{1,0:T(8,128)S(1)}, u32[]{:S(2)}, u32[]{:S(2)}) collective-permute-start(f32[32,128]{1,0:T(8,128)S(1)} %add_add_fusion.4), channel_id=1, source_target_pairs={{0,64},{32,96},{64,0},{96,32},{128,192},{160,224},{192,128},{224,1... | collective-permute-start | bytes 49160 | tf_op jit(solution)/shard_map/ppermute | solution.py:382
  72.6 36.9 %collective-permute-start.16 = (f32[32,128]{1,0:T(8,128)S(1)}, f32[32,128]{1,0:T(8,128)S(1)}, u32[]{:S(2)}, u32[]{:S(2)}) collective-permute-start(f32[32,128]{1,0:T(8,128)S(1)} %add_add_fusion.4), channel_id=1, source_target_pairs={{0,96},{32,64},{64,32},{96,0},{128,224},{160,192},{192,160},{224,1... | collective-permute-start | bytes 49160 | tf_op jit(solution)/shard_map/ppermute | solution.py:382
  74.8 34.8 %collective-permute-start.14 = (f32[32,128]{1,0:T(8,128)S(1)}, f32[32,128]{1,0:T(8,128)S(1)}, u32[]{:S(2)}, u32[]{:S(2)}) collective-permute-start(f32[32,128]{1,0:T(8,128)S(1)} %add_add_fusion.4), channel_id=1, source_target_pairs={{0,32},{32,0},{64,96},{96,64},{128,160},{160,128},{192,224},{224,1... | collective-permute-start | bytes 49160 | tf_op jit(solution)/shard_map/ppermute | solution.py:382
  103.7 33.6 %collective-permute-start.25 = (f32[144,128]{1,0:T(8,128)S(1)}, f32[144,128]{1,0:T(8,128)}, u32[]{:S(2)}, u32[]{:S(2)}) collective-permute-start(f32[144,128]{1,0:T(8,128)S(1)} %get-tuple-element.28), channel_id=1, source_target_pairs={{0,2},{1,3},{2,0},{3,1},{4,6},{5,7},{6,4},{7,5},{8,10},{9,11},{10,... | collective-permute-start | bytes 221192 | tf_op jit(solution)/shard_map/ppermute | solution.py:425
  104.0 33.4 %collective-permute-start.26 = (f32[144,128]{1,0:T(8,128)S(1)}, f32[144,128]{1,0:T(8,128)}, u32[]{:S(2)}, u32[]{:S(2)}) collective-permute-start(f32[144,128]{1,0:T(8,128)S(1)} %get-tuple-element.29), channel_id=1, source_target_pairs={{0,3},{1,2},{2,1},{3,0},{4,7},{5,6},{6,5},{7,4},{8,11},{9,10},{10,... | collective-permute-start | bytes 221192 | tf_op jit(solution)/shard_map/ppermute | solution.py:425
  109.6 22.3 %collective-permute-start.22 = (f32[32,128]{1,0:T(8,128)S(1)}, f32[32,128]{1,0:T(8,128)S(1)}, u32[]{:S(2)}, u32[]{:S(2)}) collective-permute-start(f32[32,128]{1,0:T(8,128)S(1)} %add_add_fusion.3), channel_id=1, source_target_pairs={{0,2},{1,3},{2,0},{3,1},{4,6},{5,7},{6,4},{7,5},{8,10},{9,11},{10,... | collective-permute-start | bytes 49160 | tf_op jit(solution)/shard_map/ppermute | solution.py:382
  109.9 22.1 %collective-permute-start.23 = (f32[32,128]{1,0:T(8,128)S(1)}, f32[32,128]{1,0:T(8,128)S(1)}, u32[]{:S(2)}, u32[]{:S(2)}) collective-permute-start(f32[32,128]{1,0:T(8,128)S(1)} %add_add_fusion.3), channel_id=1, source_target_pairs={{0,3},{1,2},{2,1},{3,0},{4,7},{5,6},{6,5},{7,4},{8,11},{9,10},{10,... | collective-permute-start | bytes 49160 | tf_op jit(solution)/shard_map/ppermute | solution.py:382
  110.2 22.2 %collective-permute-start.21 = (f32[32,128]{1,0:T(8,128)S(1)}, f32[32,128]{1,0:T(8,128)S(1)}, u32[]{:S(2)}, u32[]{:S(2)}) collective-permute-start(f32[32,128]{1,0:T(8,128)S(1)} %add_add_fusion.3), channel_id=1, source_target_pairs={{0,1},{1,0},{2,3},{3,2},{4,5},{5,4},{6,7},{7,6},{8,9},{9,8},{10,11... | collective-permute-start | bytes 49160 | tf_op jit(solution)/shard_map/ppermute | solution.py:382
  131.9 5.6 %collective-permute-start.24 = (f32[144,128]{1,0:T(8,128)S(1)}, f32[144,128]{1,0:T(8,128)S(1)}, u32[]{:S(2)}, u32[]{:S(2)}) collective-permute-start(f32[144,128]{1,0:T(8,128)S(1)} %get-tuple-element.27), channel_id=1, source_target_pairs={{0,1},{1,0},{2,3},{3,2},{4,5},{5,4},{6,7},{7,6},{8,9},{9,8},{10,11... | collective-permute-start | bytes 221192 | tf_op jit(solution)/shard_map/ppermute | solution.py:425
  132.0 6.4 %collective-permute-start.28 = (f32[144,128]{1,0:T(8,128)S(1)}, f32[144,128]{1,0:T(8,128)S(1)}, u32[]{:S(2)}, u32[]{:S(2)}) collective-permute-start(f32[144,128]{1,0:T(8,128)S(1)} %get-tuple-element.36), channel_id=1, source_target_pairs={{0,2},{1,3},{2,0},{3,1},{4,6},{5,7},{6,4},{7,5},{8,10},{9,11},{10,... | collective-permute-start | bytes 221192 | tf_op jit(solution)/shard_map/ppermute | solution.py:427
  132.4 6.0 %collective-permute-start.29 = (f32[144,128]{1,0:T(8,128)S(1)}, f32[144,128]{1,0:T(8,128)S(1)}, u32[]{:S(2)}, u32[]{:S(2)}) collective-permute-start(f32[144,128]{1,0:T(8,128)S(1)} %get-tuple-element.37), channel_id=1, source_target_pairs={{0,3},{1,2},{2,1},{3,0},{4,7},{5,6},{6,5},{7,4},{8,11},{9,10},{10,... | collective-permute-start | bytes 221192 | tf_op jit(solution)/shard_map/ppermute | solution.py:427
  137.3 1.4 collective-permute-start.27
  (17 other events, 75.0 us)

commit v4 on v3

--- a/solution.py
+++ b/solution.py
@@ -14,8 +14,7 @@
 F32 = jnp.float32
 CHAN = ("chan_x", "chan_y", "chan_z")
 STN = "stn"
-OUTER = "chan_z"
-INNER = ("chan_x", "chan_y")
+ALL = ("chan_x", "chan_y", "chan_z", "stn")
 smooth_weight = 0.05
 damping = 0.3
 
@@ -125,7 +124,9 @@
     in_fours(turn)
 
 
-def model(me_ref, own, mate, over, far, factor, coh, vis, flags, w2, sell, smooth, earlier, jall, res, wgt, stats, w_all, wr, wi, lr):
+def model(me_ref, own, mate, over, far, factor, coh, vis, flags, w2, sell, smooth, earlier, jall, res, wgt, stats, *rest):
+    *spread, w_all, wr, wi, lr = rest
+    spread = spread[0] if spread else None
     groups = jall.shape[0]
     t = pl.program_id(0)
     me = me_ref[0]
@@ -177,6 +178,12 @@
         return 0
 
     lax.fori_loop(0, STEP, tile, 0)
+    if spread is not None:
+        @pl.when(t == pl.num_programs(0) - 1)
+        def _():
+            lane = lax.broadcasted_iota(jnp.int32, spread.shape, 1)
+            sums = [jnp.sum(stats[lo:hi]) for lo, hi in ((0, 8), (8, 16), (16, 32))]
+            spread[...] = jnp.where(lane == 0, sums[0], jnp.where(lane == 1, sums[1], jnp.where(lane == 2, sums[2], 0.0)))
 
 
 def norms(x):
@@ -314,14 +321,21 @@
     return pl.BlockSpec(shape, lambda i: (0,) * len(shape))
 
 
-def call_model(f, me, pieces, factor, coh, vis, flags, sels, smooth, earlier):
+def call_model(f, me, pieces, factor, coh, vis, flags, sels, smooth, earlier, devices=0):
     G = factor.shape[0]
     S = G * LANES
     sc = operand_scratch(G)
     outs = [((G, 8 * K, LANES), None), ((2, 2, 2, ROWS, S), 3), ((ROWS, S), 0), ((32, LANES), None)]
+    if devices:
+        outs.append(((devices, LANES), None))
 
     if earlier is None:
         earlier, smooth = jnp.zeros((32, LANES), F32), jnp.zeros((16, LANES), F32)
+
+    operands_in = (coh, vis, flags, sels[0], sels[1])
+    if f == 0:
+        operands_in = tuple(pltpu.with_memory_space_constraint(x, pltpu.HBM) for x in operands_in)
+        pieces = (pltpu.with_memory_space_constraint(pieces[0], pltpu.HBM), *pieces[1:])
 
     def piece_spec(x):
         at = f if x.shape[0] > 1 else 0
@@ -347,7 +361,7 @@
         scratch_shapes=[pltpu.VMEM((ROWS, S), F32), *sc["model"]],
         cost_estimate=pl.CostEstimate(flops=8_000_000_000, bytes_accessed=10_000_000, transcendentals=0),
         compiler_params=pltpu.CompilerParams(vmem_limit_bytes=24 << 20),
-    )(me, *pieces, factor, coh, vis, flags, sels[0], sels[1], smooth, earlier)
+    )(me, *pieces, factor, *operands_in, smooth, earlier)
 
 
 def call_grad(f, me, jall, coh, res, wgt, sels):
@@ -364,7 +378,7 @@
                         pltpu.VMEM((G, 9 * K, ROWS), F32), *sc["grad"], *sc["bufs"]],
         cost_estimate=pl.CostEstimate(flops=20_000_000_000, bytes_accessed=10_000_000, transcendentals=0),
         compiler_params=pltpu.CompilerParams(vmem_limit_bytes=36 << 20),
-    )(me, jall, coh, res, wgt, sels[0], sels[2])
+    )(me, jall, pltpu.with_memory_space_constraint(coh, pltpu.HBM), res, wgt, sels[0], sels[2])
 
 
 def beam_factor(beam, group_of):
@@ -375,14 +389,6 @@
 
 def hop_pairs(hop, count):
     return [(i, i ^ hop) for i in range(count)]
-
-
-def summed(values, axes):
-    count = lax.axis_size(axes)
-    parts = [values] + [lax.ppermute(values, axes, hop_pairs(hop, count)) for hop in range(1, count)]
-    while len(parts) > 1:
-        parts = [parts[i] + parts[i + 1] for i in range(0, len(parts), 2)]
-    return parts[0]
 
 
 def on_device(gains, coherency, vis_data, flags, beam, group_of):
@@ -417,16 +423,15 @@
     sels = operands()
     me1 = me[None]
     jall0, res0, wgt0, stats = call_model(0, me1, (raw, mate, over[0], far[0]), factor, coherency, vis_data, flags, sels, None, None)
-    jall1, res1, wgt1, stats = call_model(1, me1, (raw, mate, over[1], far[1]), factor, coherency, vis_data, flags, sels, smooth_local, stats)
-
-    stats = summed(stats, OUTER)
+    jall1, res1, wgt1, _, spread = call_model(1, me1, (raw, mate, over[1], far[1]), factor, coherency, vis_data, flags, sels, smooth_local, stats, chan_count * stn_count)
+
+    arrived = lax.all_to_all(spread, ALL, 0, 0, tiled=True)
     row0, *cols0 = call_grad(0, me1, jall0, coherency, res0, wgt0, sels)
-    stats = summed(stats, INNER)
     cols0 = cols0[:1] + [lax.ppermute(cols0[h], STN, hop_pairs(h, stn_count)) for h in range(1, stn_count)]
     row1, *cols1 = call_grad(1, me1, jall1, coherency, res1, wgt1, sels)
     cols1 = cols1[:1] + [lax.ppermute(cols1[h], STN, hop_pairs(h, stn_count)) for h in range(1, stn_count)]
-    stats = summed(stats, STN)
-    sq, count, smooth = jnp.sum(stats[:8]), jnp.sum(stats[8:16]), jnp.sum(stats[16:])
+    totals = jnp.sum(arrived, axis=0)
+    sq, count, smooth = totals[0], totals[1], totals[2]
 
     norm_scale = all_channels * all_stations / count
     steps = []

time: 141 us -> 108 us (0.77)
  starting transfers between devices: 53.4 us -> 35 us
  local copies, waits for them, and re-layouts: 15.9 us -> 1.65 us
  Pallas kernels: 57.7 us -> 60.5 us
  other arithmetic: 5.56 us -> 3.59 us
    ppermute x17 -> x0, starting transfers between devices: 32.4 us -> none  [summed(): lax.ppermute(values, axes, hop_pairs(hop, count))]
    all_to_all x0 -> x1, starting transfers between devices: none -> 16.1 us  [on_device(): arrived = lax.all_to_all(spread, ALL, 0, 0, tiled=True)]
    unnamed x38 -> x16, local copies, waits for them, and re-layouts: 14.9 us -> 0.05 us
    ppermute x3, starting transfers between devices: 5.86 us -> 2.04 us  [on_device(): lax.ppermute(cols0[h], STN, hop_pairs(h, stn_count))]
    ppermute x17 -> x0, waiting for transfers between devices: 2.92 us -> none  [summed(): lax.ppermute(values, axes, hop_pairs(hop, count))]
    pallas_call x2, Pallas kernels: 16.9 us -> 18.9 us  [call_model(): pl.pallas_call(model, grid=(TILES // STEP,), out_shape=[jax.ShapeDtypeStr...]
    ppermute x3, waiting for transfers between devices: 0.25 us -> 2.11 us  [on_device(): lax.ppermute(cols1[h], STN, hop_pairs(h, stn_count))]
    ppermute x3, starting transfers between devices: 2.21 us -> 4.04 us  [on_device(): lax.ppermute(cols1[h], STN, hop_pairs(h, stn_count))]
  transfers between devices with their start and end apart: 30 -> 14, of which waited for: 5 -> 3; matrix products, arithmetic and copies ran while one was open for 4% -> 3% of each run, Pallas kernels for 35% -> 56%
where the time goes in v4:
time: 108 us
  Pallas kernels  60.5 us (56%)
  starting transfers between devices  35 us (32%)
  between operations  4.13 us (4%)
  other arithmetic  3.59 us (3%)
  waiting for transfers between devices  2.82 us (3%)
  local copies, waits for them, and re-layouts  1.65 us (2%)
    pallas_call x2, Pallas kernels, call_grad(): pl.pallas_call(functools.partial(grad_kernel, f), grid=(1,), out_shape=[j...  41.6 us
    pallas_call x2, Pallas kernels, call_model(): pl.pallas_call(model, grid=(TILES // STEP,), out_shape=[jax.ShapeDtypeStr...  18.9 us
    all_to_all x1, starting transfers between devices, on_device(): arrived = lax.all_to_all(spread, ALL, 0, 0, tiled=True)  16.1 us
    ppermute x1, starting transfers between devices, on_device(): lax.ppermute(gains, CHAN, up)  5 us
    ppermute x3, starting transfers between devices, on_device(): lax.ppermute(cols1[h], STN, hop_pairs(h, stn_count))  4.04 us
    ppermute x1, starting transfers between devices, on_device(): mate = lax.ppermute(raw, STN, hop_pairs(1, stn_count))  2.85 us
  transfers between devices with their start and end apart: 14, of which 3 were waited for; matrix products, arithmetic and copies ran while one was open for 3% of the time, Pallas kernels for 56%

profile of v4, /device:TPU:1, one launch (start us, length us, event | category | flops | bytes accessed | tf_op | source)
XLA Modules:
  0.0 107.8 jit_solution(6947862509717816774)
XLA Ops:
  0.6 1.3 %collective-permute-start.3 = (f32[2,2,2,2,16,128]{5,4,3,2,1,0:T(8,128)}, f32[2,2,2,2,16,128]{5,4,3,2,1,0:T(8,128)S(1)}, u32[]{:S(2)}, u32[]{:S(2)}) collective-permute-start(f32[2,2,2,2,16,128]{5,4,3,2,1,0:T(8,128)} %param.9), channel_id=1, source_target_pairs={{4,0},{8,4},{12,8},{16,12},{20,16},{24,20},{28,24},{32,28},{36,32}... | collective-permute-start | bytes 393224 | tf_op jit(solution)/shard_map/ppermute | solution.py:413
  1.9 5.0 %collective-permute-start.4 = (f32[2,2,2,2,16,128]{5,4,3,2,1,0:T(8,128)}, f32[2,2,2,2,16,128]{5,4,3,2,1,0:T(8,128)S(1)}, u32[]{:S(2)}, u32[]{:S(2)}) collective-permute-start(f32[2,2,2,2,16,128]{5,4,3,2,1,0:T(8,128)} %param.9), channel_id=1, source_target_pairs={{0,4},{4,8},{8,12},{12,16},{16,20},{20,24},{24,28},{28,32},{32,36}... | collective-permute-start | bytes 393224 | tf_op jit(solution)/shard_map/ppermute | solution.py:413
  6.9 2.8 %collective-permute-start = (f32[2,128,128]{2,1,0:T(8,128)}, f32[2,128,128]{2,1,0:T(8,128)S(1)}, u32[]{:S(2)}, u32[]{:S(2)}) collective-permute-start(f32[2,128,128]{2,1,0:T(8,128)} %bitcast.44), channel_id=1, source_target_pairs={{0,1},{1,0},{2,3},{3,2},{4,5},{5,4},{6,7},{7,6},{8,9},{9,8},{10,11... | collective-permute-start | bytes 393224 | tf_op jit(solution)/shard_map/ppermute | solution.py:405
  9.8 0.9 fusion.15
  10.7 0.1 collective-permute-start.5
  10.8 1.5 %collective-permute-start.1 = (f32[1,128,128]{2,1,0:T(8,128)S(1)}, f32[1,128,128]{2,1,0:T(8,128)S(1)}, u32[]{:S(2)}, u32[]{:S(2)}) collective-permute-start(f32[1,128,128]{2,1,0:T(8,128)S(1)} %bitcast.51), channel_id=1, source_target_pairs={{0,2},{1,3},{2,0},{3,1},{4,6},{5,7},{6,4},{7,5},{8,10},{9,11},{10,... | collective-permute-start | bytes 196616 | tf_op jit(solution)/shard_map/ppermute | solution.py:404
  12.2 0.7 fusion.12
  12.9 0.8 multiply_reduce_fusion
  13.8 0.6 collective-permute-done.5.over
  14.4 1.3 %collective-permute-start.6 = (f32[1,128,128]{2,1,0:T(8,128)S(1)}, f32[1,128,128]{2,1,0:T(8,128)S(1)}, u32[]{:S(2)}, u32[]{:S(2)}) collective-permute-start(f32[1,128,128]{2,1,0:T(8,128)S(1)} %collective-permute-done.5.over), channel_id=1, source_target_pairs={{0,1},{1,0},{2,3},{3,2},{4,5},{5,4},{6,7},{7,6},{8,9},{9,8},{10,11... | collective-permute-start | bytes 196616 | tf_op jit(solution)/shard_map/ppermute | solution.py:406
  15.7 0.1 collective-permute-done.1.over
  15.8 0.9 collective-permute-start.2
  16.7 0.0 copy-start.3
  16.7 0.0 copy-start.4
  16.7 0.0 slice-start
  16.7 9.6 %shard_map.104 = (f32[4,128,128]{2,1,0:T(8,128)S(1)}, f32[2,2,2,128,512]{4,3,2,1,0:T(8,128)S(1)}, f32[128,512]{1,0:T(8,128)S(1)}, f32[32,128]{1,0:T(8,128)S(1)}) custom-call(s32[1]{0:T(128)} %bitcast.me_ref, f32[2,128,128]{2,1,0:T(8,128)} %bitcast.45, f32[2,128,128]{2,1,0:T(8,128)S(1)} %collective-permute-done.mate, ...), custom_call_target="tpu_custom_call" | custom-call | flops 8000000000 | bytes 10000000 | tf_op jit(solution)/shard_map/pallas_call | solution.py:350
  26.4 0.0 slice-start.1
  26.4 0.0 copy-start.5
  26.4 21.0 %shard_map.106 = (f32[144,128]{1,0:T(8,128)S(1)}, f32[144,128]{1,0:T(8,128)S(1)}, f32[144,128]{1,0:T(8,128)S(1)}, f32[144,128]{1,0:T(8,128)S(1)}, f32[144,128]{1,0:T(8,128)S(1)}) custom-call(s32[1]{0:T(128)} %bitcast.me_ref, f32[4,128,128]{2,1,0:T(8,128)S(1)} %get-tuple-element.22.jall, bf16[2,16,2,128,512]{4,3,2,1,0:T(8,128)(2,1)} %coh_hbm.3, ...), custom_call_target="tpu_custom_call" | custom-call | flops 20000000000 | bytes 10000000 | tf_op jit(solution)/shard_map/pallas_call | solution.py:371
  47.5 0.1 fusion.3
  47.6 0.2 collective-permute-start.8
  47.8 1.8 %collective-permute-start.9 = (f32[144,128]{1,0:T(8,128)S(1)}, f32[144,128]{1,0:T(8,128)}, u32[]{:S(2)}, u32[]{:S(2)}) collective-permute-start(f32[144,128]{1,0:T(8,128)S(1)} %get-tuple-element.29), channel_id=1, source_target_pairs={{0,3},{1,2},{2,1},{3,0},{4,7},{5,6},{6,5},{7,4},{8,11},{9,10},{10,... | collective-permute-start | bytes 221192 | tf_op jit(solution)/shard_map/ppermute | solution.py:430
  49.7 9.2 %shard_map.105 = (f32[4,128,128]{2,1,0:T(8,128)S(1)}, f32[2,2,2,128,512]{4,3,2,1,0:T(8,128)S(1)}, f32[128,512]{1,0:T(8,128)S(1)}, f32[32,128]{1,0:T(8,128)}, f32[256,128]{1,0:T(8,128)}) custom-call(s32[1]{0:T(128)} %bitcast.me_ref, f32[2,128,128]{2,1,0:T(8,128)S(1)} %bitcast.46, f32[2,128,128]{2,1,0:T(8,128)S(1)} %collective-permute-done.mate, ...), custom_call_target="tpu_custom_call" | custom-call | flops 8000000000 | bytes 10000000 | tf_op jit(solution)/shard_map/pallas_call | solution.py:350
  58.9 16.1 %all-to-all-start = ((f32[256,1,128]{2,1,0:T(1,128)}), f32[256,1,128]{2,1,0:T(1,128)S(1)}, u32[]{:S(2)}, u32[]{:S(2)}) async-start(f32[256,1,128]{2,1,0:T(1,128)} %bitcast.6), calls=%async_computation | async-start | bytes 262144 | tf_op jit(solution)/shard_map/all_to_all | solution.py:428
  75.0 20.7 %shard_map.107 = (f32[144,128]{1,0:T(8,128)S(1)}, f32[144,128]{1,0:T(8,128)S(1)}, f32[144,128]{1,0:T(8,128)S(1)}, f32[144,128]{1,0:T(8,128)S(1)}, f32[144,128]{1,0:T(8,128)S(1)}) custom-call(s32[1]{0:T(128)} %bitcast.me_ref, f32[4,128,128]{2,1,0:T(8,128)S(1)} %get-tuple-element.30.jall, bf16[2,16,2,128,512]{4,3,2,1,0:T(8,128)(2,1)} %coh_hbm.3, ...), custom_call_target="tpu_custom_call" | custom-call | flops 20000000000 | bytes 10000000 | tf_op jit(solution)/shard_map/pallas_call | solution.py:371
  95.7 1.4 %collective-permute-start.11 = (f32[144,128]{1,0:T(8,128)S(1)}, f32[144,128]{1,0:T(8,128)S(1)}, u32[]{:S(2)}, u32[]{:S(2)}) collective-permute-start(f32[144,128]{1,0:T(8,128)S(1)} %get-tuple-element.36), channel_id=1, source_target_pairs={{0,2},{1,3},{2,0},{3,1},{4,6},{5,7},{6,4},{7,5},{8,10},{9,11},{10,... | collective-permute-start | bytes 221192 | tf_op jit(solution)/shard_map/ppermute | solution.py:432
  97.1 2.6 %collective-permute-start.12 = (f32[144,128]{1,0:T(8,128)S(1)}, f32[144,128]{1,0:T(8,128)S(1)}, u32[]{:S(2)}, u32[]{:S(2)}) collective-permute-start(f32[144,128]{1,0:T(8,128)S(1)} %get-tuple-element.37), channel_id=1, source_target_pairs={{0,3},{1,2},{2,1},{3,0},{4,7},{5,6},{6,5},{7,4},{8,11},{9,10},{10,... | collective-permute-start | bytes 221192 | tf_op jit(solution)/shard_map/ppermute | solution.py:432
  99.7 1.0 add_add_fusion.1
  100.8 2.1 %collective-permute-done.12 = f32[144,128]{1,0:T(8,128)S(1)} collective-permute-done((f32[144,128]{1,0:T(8,128)S(1)}, f32[144,128]{1,0:T(8,128)S(1)}, u32[]{:S(2)}, u32[]{:S(2)}) %collective-permute-start.12) | collective-permute-done | bytes 73760 | tf_op jit(solution)/shard_map/ppermute | solution.py:432
  102.9 0.3 reduce_sum.29
  103.2 0.7 fusion.16
  105.3 0.7 pad_maximum_fusion.2
  (37 shorter events, 0.2 us)
Async XLA Ops:
  0.6 46.8 %collective-permute-start.3 = (f32[2,2,2,2,16,128]{5,4,3,2,1,0:T(8,128)}, f32[2,2,2,2,16,128]{5,4,3,2,1,0:T(8,128)S(1)}, u32[]{:S(2)}, u32[]{:S(2)}) collective-permute-start(f32[2,2,2,2,16,128]{5,4,3,2,1,0:T(8,128)} %param.9), channel_id=1, source_target_pairs={{4,0},{8,4},{12,8},{16,12},{20,16},{24,20},{28,24},{32,28},{36,32}... | collective-permute-start | bytes 393224 | tf_op jit(solution)/shard_map/ppermute | solution.py:413
  1.9 45.5 %collective-permute-start.4 = (f32[2,2,2,2,16,128]{5,4,3,2,1,0:T(8,128)}, f32[2,2,2,2,16,128]{5,4,3,2,1,0:T(8,128)S(1)}, u32[]{:S(2)}, u32[]{:S(2)}) collective-permute-start(f32[2,2,2,2,16,128]{5,4,3,2,1,0:T(8,128)} %param.9), channel_id=1, source_target_pairs={{0,4},{4,8},{8,12},{12,16},{16,20},{20,24},{24,28},{28,32},{32,36}... | collective-permute-start | bytes 393224 | tf_op jit(solution)/shard_map/ppermute | solution.py:413
  6.9 9.7 %collective-permute-start = (f32[2,128,128]{2,1,0:T(8,128)}, f32[2,128,128]{2,1,0:T(8,128)S(1)}, u32[]{:S(2)}, u32[]{:S(2)}) collective-permute-start(f32[2,128,128]{2,1,0:T(8,128)} %bitcast.44), channel_id=1, source_target_pairs={{0,1},{1,0},{2,3},{3,2},{4,5},{5,4},{6,7},{7,6},{8,9},{9,8},{10,11... | collective-permute-start | bytes 393224 | tf_op jit(solution)/shard_map/ppermute | solution.py:405
  10.7 3.7 %collective-permute-start.5 = (f32[1,128,128]{2,1,0:T(8,128)S(1)}, f32[1,128,128]{2,1,0:T(8,128)S(1)}, u32[]{:S(2)}, u32[]{:S(2)}) collective-permute-start(f32[1,128,128]{2,1,0:T(8,128)S(1)} %bitcast.52), channel_id=1, source_target_pairs={{0,2},{1,3},{2,0},{3,1},{4,6},{5,7},{6,4},{7,5},{8,10},{9,11},{10,... | collective-permute-start | bytes 196616 | tf_op jit(solution)/shard_map/ppermute | solution.py:404
  10.8 5.0 %collective-permute-start.1 = (f32[1,128,128]{2,1,0:T(8,128)S(1)}, f32[1,128,128]{2,1,0:T(8,128)S(1)}, u32[]{:S(2)}, u32[]{:S(2)}) collective-permute-start(f32[1,128,128]{2,1,0:T(8,128)S(1)} %bitcast.51), channel_id=1, source_target_pairs={{0,2},{1,3},{2,0},{3,1},{4,6},{5,7},{6,4},{7,5},{8,10},{9,11},{10,... | collective-permute-start | bytes 196616 | tf_op jit(solution)/shard_map/ppermute | solution.py:404
  14.4 2.3 %collective-permute-start.6 = (f32[1,128,128]{2,1,0:T(8,128)S(1)}, f32[1,128,128]{2,1,0:T(8,128)S(1)}, u32[]{:S(2)}, u32[]{:S(2)}) collective-permute-start(f32[1,128,128]{2,1,0:T(8,128)S(1)} %collective-permute-done.5.over), channel_id=1, source_target_pairs={{0,1},{1,0},{2,3},{3,2},{4,5},{5,4},{6,7},{7,6},{8,9},{9,8},{10,11... | collective-permute-start | bytes 196616 | tf_op jit(solution)/shard_map/ppermute | solution.py:406
  15.8 33.8 %collective-permute-start.2 = (f32[1,128,128]{2,1,0:T(8,128)S(1)}, f32[1,128,128]{2,1,0:T(8,128)S(1)}, u32[]{:S(2)}, u32[]{:S(2)}) collective-permute-start(f32[1,128,128]{2,1,0:T(8,128)S(1)} %collective-permute-done.1.over), channel_id=1, source_target_pairs={{0,1},{1,0},{2,3},{3,2},{4,5},{5,4},{6,7},{7,6},{8,9},{9,8},{10,11... | collective-permute-start | bytes 196616 | tf_op jit(solution)/shard_map/ppermute | solution.py:407
  16.7 9.7 %copy-start.3 = (bf16[128,16]{1,0:T(8,128)(2,1)S(1)}, bf16[128,16]{1,0:T(8,128)(2,1)}, u32[]{:S(2)}) copy-start(bf16[128,16]{1,0:T(8,128)(2,1)} %constant.63.clone.w2) | copy-start | bytes 12292
  16.7 9.7 %copy-start.4 = (bf16[32,16]{1,0:T(8,128)(2,1)S(1)}, bf16[32,16]{1,0:T(8,128)(2,1)}, u32[]{:S(2)}) copy-start(bf16[32,16]{1,0:T(8,128)(2,1)} %constant.65.clone.selc) | copy-start | bytes 3076
  16.7 32.9 %slice-start = ((s8[8388608]{0:T(1024)(128)(4,1)}), s8[4194304]{0:T(1024)(128)(4,1)S(1)}, s32[]{:S(2)}) async-start(s8[8388608]{0:T(1024)(128)(4,1)} %bitcast.47), calls=%async_computation.1 | async-start | bytes 8388608
  26.4 21.1 %copy-start = (f32[2,2,2,2,16,128]{5,4,3,2,1,0:T(8,128)S(1)}, f32[2,2,2,2,16,128]{5,4,3,2,1,0:T(8,128)}, u32[]{:S(2)}) copy-start(f32[2,2,2,2,16,128]{5,4,3,2,1,0:T(8,128)} %param.9) | copy-start | bytes 393220
  26.4 23.3 %slice-start.1 = ((s8[8388608]{0:T(1024)(128)(4,1)}), s8[4194304]{0:T(1024)(128)(4,1)S(1)}, s32[]{:S(2)}) async-start(s8[8388608]{0:T(1024)(128)(4,1)} %bitcast.47), calls=%async_computation.2 | async-start | bytes 8388608
  26.4 23.2 %copy-start.1 = (bf16[2,2,2,2,128,512]{5,4,3,2,1,0:T(8,128)(2,1)S(1)}, bf16[2,2,2,2,128,512]{5,4,3,2,1,0:T(8,128)(2,1)}, u32[]{:S(2)}) copy-start(bf16[2,2,2,2,128,512]{5,4,3,2,1,0:T(8,128)(2,1)} %vis.3) | copy-start | bytes 6291460
  26.4 23.2 %copy-start.2 = (s32[2,8,32]{2,1,0:T(8,128)S(1)}, s32[2,8,32]{2,1,0:T(8,128)}, u32[]{:S(2)}) copy-start(s32[2,8,32]{2,1,0:T(8,128)} %flags.3) | copy-start | bytes 6148
  26.4 23.2 %copy-start.5 = (bf16[2,16,16]{2,1,0:T(8,128)(2,1)S(1)}, bf16[2,16,16]{2,1,0:T(8,128)(2,1)}, u32[]{:S(2)}) copy-start(bf16[2,16,16]{2,1,0:T(8,128)(2,1)} %constant.64.clone.sell) | copy-start | bytes 3076
  47.6 52.1 %collective-permute-start.8 = (f32[144,128]{1,0:T(8,128)S(1)}, f32[144,128]{1,0:T(8,128)}, u32[]{:S(2)}, u32[]{:S(2)}) collective-permute-start(f32[144,128]{1,0:T(8,128)S(1)} %get-tuple-element.28), channel_id=1, source_target_pairs={{0,2},{1,3},{2,0},{3,1},{4,6},{5,7},{6,4},{7,5},{8,10},{9,11},{10,... | collective-permute-start | bytes 221192 | tf_op jit(solution)/shard_map/ppermute | solution.py:430
  47.8 51.9 %collective-permute-start.9 = (f32[144,128]{1,0:T(8,128)S(1)}, f32[144,128]{1,0:T(8,128)}, u32[]{:S(2)}, u32[]{:S(2)}) collective-permute-start(f32[144,128]{1,0:T(8,128)S(1)} %get-tuple-element.29), channel_id=1, source_target_pairs={{0,3},{1,2},{2,1},{3,0},{4,7},{5,6},{6,5},{7,4},{8,11},{9,10},{10,... | collective-permute-start | bytes 221192 | tf_op jit(solution)/shard_map/ppermute | solution.py:430
  49.6 50.1 %collective-permute-start.7 = (f32[144,128]{1,0:T(8,128)S(1)}, f32[144,128]{1,0:T(8,128)}, u32[]{:S(2)}, u32[]{:S(2)}) collective-permute-start(f32[144,128]{1,0:T(8,128)S(1)} %get-tuple-element.27), channel_id=1, source_target_pairs={{0,1},{1,0},{2,3},{3,2},{4,5},{5,4},{6,7},{7,6},{8,9},{9,8},{10,11... | collective-permute-start | bytes 221192 | tf_op jit(solution)/shard_map/ppermute | solution.py:430
  58.9 44.0 %all-to-all-start = ((f32[256,1,128]{2,1,0:T(1,128)}), f32[256,1,128]{2,1,0:T(1,128)S(1)}, u32[]{:S(2)}, u32[]{:S(2)}) async-start(f32[256,1,128]{2,1,0:T(1,128)} %bitcast.6), calls=%async_computation | async-start | bytes 262144 | tf_op jit(solution)/shard_map/all_to_all | solution.py:428
  95.7 5.1 %collective-permute-start.11 = (f32[144,128]{1,0:T(8,128)S(1)}, f32[144,128]{1,0:T(8,128)S(1)}, u32[]{:S(2)}, u32[]{:S(2)}) collective-permute-start(f32[144,128]{1,0:T(8,128)S(1)} %get-tuple-element.36), channel_id=1, source_target_pairs={{0,2},{1,3},{2,0},{3,1},{4,6},{5,7},{6,4},{7,5},{8,10},{9,11},{10,... | collective-permute-start | bytes 221192 | tf_op jit(solution)/shard_map/ppermute | solution.py:432
  97.1 5.7 %collective-permute-start.12 = (f32[144,128]{1,0:T(8,128)S(1)}, f32[144,128]{1,0:T(8,128)S(1)}, u32[]{:S(2)}, u32[]{:S(2)}) collective-permute-start(f32[144,128]{1,0:T(8,128)S(1)} %get-tuple-element.37), channel_id=1, source_target_pairs={{0,3},{1,2},{2,1},{3,0},{4,7},{5,6},{6,5},{7,4},{8,11},{9,10},{10,... | collective-permute-start | bytes 221192 | tf_op jit(solution)/shard_map/ppermute | solution.py:432
  99.7 3.1 %collective-permute-start.10 = (f32[144,128]{1,0:T(8,128)S(1)}, f32[144,128]{1,0:T(8,128)S(1)}, u32[]{:S(2)}, u32[]{:S(2)}) collective-permute-start(f32[144,128]{1,0:T(8,128)S(1)} %get-tuple-element.35), channel_id=1, source_target_pairs={{0,1},{1,0},{2,3},{3,2},{4,5},{5,4},{6,7},{7,6},{8,9},{9,8},{10,11... | collective-permute-start | bytes 221192 | tf_op jit(solution)/shard_map/ppermute | solution.py:432

commit v5 on v4

--- a/solution.py
+++ b/solution.py
@@ -295,7 +295,7 @@
     )
 
 
-def grad_kernel(f, me_ref, jall, coh_hbm, res_hbm, wgt, w2, selc, row, col0, col1, col2, col3,
+def grad_kernel(f, me_ref, jall, coh_hbm, res_hbm, wgt, w2, selc, arrived, row, col0, col1, col2, col3, sums,
                 coh, res, sems, col, lq, lc, nq, nr, y0, a0, y1, a1):
     groups = jall.shape[0]
     me = me_ref[0]
@@ -309,6 +309,11 @@
     load_res.wait()
     load_first.wait()
     gradient(coh, wgt, res, lq, lc, nq, nr, ((y0, a0), (y1, a1)), row, col, groups, load_rest.wait)
+    total = jnp.sum(arrived[...], axis=0, keepdims=True)
+    lane = lax.broadcasted_iota(jnp.int32, total.shape, 1)
+    line = lax.broadcasted_iota(jnp.int32, sums.shape, 0)
+    picked = [jnp.sum(jnp.where(lane == n, total, 0.0)) for n in range(3)]
+    sums[...] = jnp.where(line == 0, picked[0], jnp.where(line == 1, picked[1], picked[2]))
     for hop, out in enumerate((col0, col1, col2, col3)):
         out[...] = col[me ^ hop]
 
@@ -364,21 +369,23 @@
     )(me, *pieces, factor, *operands_in, smooth, earlier)
 
 
-def call_grad(f, me, jall, coh, res, wgt, sels):
+def call_grad(f, me, jall, coh, res, wgt, sels, arrived):
+    if f == 0:
+        res, wgt = (pltpu.with_memory_space_constraint(x, pltpu.HBM) for x in (res, wgt))
     G = jall.shape[0]
     sc = operand_scratch(G)
-    outs = [(9 * K, ROWS)] * 5
+    outs = [(9 * K, ROWS)] * 5 + [(8, LANES)]
     return pl.pallas_call(
         functools.partial(grad_kernel, f), grid=(1,),
         out_shape=[jax.ShapeDtypeStruct(s, F32) for s in outs],
         in_specs=[pl.BlockSpec(memory_space=pltpu.SMEM), whole(jall), pl.BlockSpec(memory_space=pl.ANY), pl.BlockSpec(memory_space=pl.ANY),
-                  whole(wgt), whole(sels[0]), whole(sels[2])],
+                  whole(wgt), whole(sels[0]), whole(sels[2]), whole(arrived)],
         out_specs=[spec(s) for s in outs],
         scratch_shapes=[pltpu.VMEM(coh.shape[1:], BF), pltpu.VMEM(res.shape, F32), pltpu.SemaphoreType.DMA((3,)),
                         pltpu.VMEM((G, 9 * K, ROWS), F32), *sc["grad"], *sc["bufs"]],
         cost_estimate=pl.CostEstimate(flops=20_000_000_000, bytes_accessed=10_000_000, transcendentals=0),
         compiler_params=pltpu.CompilerParams(vmem_limit_bytes=36 << 20),
-    )(me, jall, pltpu.with_memory_space_constraint(coh, pltpu.HBM), res, wgt, sels[0], sels[2])
+    )(me, jall, pltpu.with_memory_space_constraint(coh, pltpu.HBM), res, wgt, sels[0], sels[2], arrived)
 
 
 def beam_factor(beam, group_of):
@@ -401,12 +408,10 @@
     all_stations = row_count * stn_count
 
     raw = gains.reshape(chan_dev, 8 * K, row_count)
-    over = [lax.ppermute(raw[f:f + 1], STN, hop_pairs(2, stn_count)) for f in range(chan_dev)]
+    over = lax.ppermute(raw, STN, hop_pairs(2, stn_count))
     mate = lax.ppermute(raw, STN, hop_pairs(1, stn_count))
-    far = [lax.ppermute(over[0], STN, hop_pairs(1, stn_count))]
-    far.append(lax.ppermute(over[1], STN, hop_pairs(1, stn_count)))
+    far = lax.ppermute(over, STN, hop_pairs(1, stn_count))
     factor = beam_factor(beam, group_of).reshape(K, stn_count, row_count).swapaxes(0, 1)
-    row_factor = lax.dynamic_index_in_dim(factor, me, 0, False)
 
     up = [(i, i + 1) for i in range(chan_count - 1)]
     down = [(i + 1, i) for i in range(chan_count - 1)]
@@ -422,18 +427,17 @@
 
     sels = operands()
     me1 = me[None]
-    jall0, res0, wgt0, stats = call_model(0, me1, (raw, mate, over[0], far[0]), factor, coherency, vis_data, flags, sels, None, None)
-    jall1, res1, wgt1, _, spread = call_model(1, me1, (raw, mate, over[1], far[1]), factor, coherency, vis_data, flags, sels, smooth_local, stats, chan_count * stn_count)
+    jall0, res0, wgt0, stats = call_model(0, me1, (raw, mate, over, far), factor, coherency, vis_data, flags, sels, None, None)
+    jall1, res1, wgt1, _, spread = call_model(1, me1, (raw, mate, over, far), factor, coherency, vis_data, flags, sels, smooth_local, stats, chan_count * stn_count)
 
     arrived = lax.all_to_all(spread, ALL, 0, 0, tiled=True)
-    row0, *cols0 = call_grad(0, me1, jall0, coherency, res0, wgt0, sels)
+    row0, *cols0, _ = call_grad(0, me1, jall0, coherency, res0, wgt0, sels, jnp.zeros((8, row_count), F32))
     cols0 = cols0[:1] + [lax.ppermute(cols0[h], STN, hop_pairs(h, stn_count)) for h in range(1, stn_count)]
-    row1, *cols1 = call_grad(1, me1, jall1, coherency, res1, wgt1, sels)
+    row1, *cols1, totals = call_grad(1, me1, jall1, coherency, res1, wgt1, sels, arrived)
     cols1 = cols1[:1] + [lax.ppermute(cols1[h], STN, hop_pairs(h, stn_count)) for h in range(1, stn_count)]
-    totals = jnp.sum(arrived, axis=0)
-    sq, count, smooth = totals[0], totals[1], totals[2]
-
-    norm_scale = all_channels * all_stations / count
+    late, row1 = lax.optimization_barrier((factor, row1))
+    row_factor = lax.dynamic_index_in_dim(late, me, 0, False)
+    norm_scale = all_channels * all_stations / totals[1]
     steps = []
     for f, (row, cols) in enumerate(((row0, cols0), (row1, cols1))):
         both = row + (cols[0] + cols[1]) + (cols[2] + cols[3])
@@ -443,7 +447,7 @@
         curvature = norm_scale * row_factor * row_factor * curv + damping
         steps.append(gradient_f / curvature)
     gain_step = jnp.stack(steps)
-    loss_value = (norm_scale * sq + smooth_weight * smooth) / (all_channels * all_stations)
+    loss_value = (norm_scale[0] * totals[0, 0] + smooth_weight * totals[2, 0]) / (all_channels * all_stations)
     return gain_step, loss_value
 
 

time: 108 us -> 122 us (1.13)
  waiting for transfers between devices: 2.82 us -> 17.3 us
  starting transfers between devices: 35 us -> 30.4 us
  Pallas kernels: 60.5 us -> 63.4 us
    all_to_all x1, waiting for transfers between devices: 0.01 us -> 11.8 us  [on_device(): arrived = lax.all_to_all(spread, ALL, 0, 0, tiled=True)]
    ppermute x4 -> x2, waiting for transfers between devices: 0.7 us -> 3.66 us  [the longest x1 3.66 us: on_device(): over = lax.ppermute(raw, STN, hop_pairs(2, stn_count))]
    pallas_call x2, Pallas kernels: 41.6 us -> 44.5 us  [call_grad(): pl.pallas_call(functools.partial(grad_kernel, f), grid=(1,), out_shape=[j...]
    ppermute x4 -> x2, starting transfers between devices: 3.76 us -> 0.96 us  [the longest x1 0.96 us: on_device(): far = lax.ppermute(over, STN, hop_pairs(1, stn_count))]
    unnamed x16 -> x20, local copies, waits for them, and re-layouts: 0.05 us -> 2.07 us
    ppermute x3, starting transfers between devices: 4.04 us -> 2.37 us  [on_device(): lax.ppermute(cols1[h], STN, hop_pairs(h, stn_count))]
  transfers between devices with their start and end apart: 14 -> 12, of which waited for: 3 -> 3; matrix products, arithmetic and copies ran while one was open for 3% -> 3% of each run, Pallas kernels for 56% -> 8%
where the time goes in v5:
time: 122 us; the launch traced here: 121 us
  Pallas kernels  63.4 us (52%)
  starting transfers between devices  30.4 us (25%)
  waiting for transfers between devices  17.3 us (14%)
  other arithmetic  4.35 us (4%)
  between operations  3.41 us (3%)
  local copies, waits for them, and re-layouts  2.61 us (2%)
    pallas_call x2, Pallas kernels, call_grad(): pl.pallas_call(functools.partial(grad_kernel, f), grid=(1,), out_shape=[j...  44.5 us
    pallas_call x2, Pallas kernels, call_model(): pl.pallas_call(model, grid=(TILES // STEP,), out_shape=[jax.ShapeDtypeStr...  19 us
    all_to_all x1, starting transfers between devices, on_device(): arrived = lax.all_to_all(spread, ALL, 0, 0, tiled=True)  16 us
    all_to_all x1, waiting for transfers between devices, on_device(): arrived = lax.all_to_all(spread, ALL, 0, 0, tiled=True)  11.8 us
    ppermute x1, starting transfers between devices, on_device(): lax.ppermute(gains, CHAN, up)  5 us
    ppermute x1, waiting for transfers between devices, on_device(): over = lax.ppermute(raw, STN, hop_pairs(2, stn_count))  3.66 us
    ppermute x1, starting transfers between devices, on_device(): mate = lax.ppermute(raw, STN, hop_pairs(1, stn_count))  2.85 us
  transfers between devices with their start and end apart: 12, of which 3 were waited for; matrix products, arithmetic and copies ran while one was open for 3% of the time, Pallas kernels for 8%

profile of v5, /device:TPU:1, one launch (start us, length us, event | category | flops | bytes accessed | tf_op | source)
XLA Modules:
  0.0 121.5 jit_solution(11135965410036745567)
XLA Ops:
  0.6 1.3 %collective-permute-start.3 = (f32[2,2,2,2,16,128]{5,4,3,2,1,0:T(8,128)}, f32[2,2,2,2,16,128]{5,4,3,2,1,0:T(8,128)S(1)}, u32[]{:S(2)}, u32[]{:S(2)}) collective-permute-start(f32[2,2,2,2,16,128]{5,4,3,2,1,0:T(8,128)} %param.9), channel_id=1, source_target_pairs={{4,0},{8,4},{12,8},{16,12},{20,16},{24,20},{28,24},{32,28},{36,32}... | collective-permute-start | bytes 393224 | tf_op jit(solution)/shard_map/ppermute | solution.py:418
  1.9 5.0 %collective-permute-start.4 = (f32[2,2,2,2,16,128]{5,4,3,2,1,0:T(8,128)}, f32[2,2,2,2,16,128]{5,4,3,2,1,0:T(8,128)S(1)}, u32[]{:S(2)}, u32[]{:S(2)}) collective-permute-start(f32[2,2,2,2,16,128]{5,4,3,2,1,0:T(8,128)} %param.9), channel_id=1, source_target_pairs={{0,4},{4,8},{8,12},{12,16},{16,20},{20,24},{24,28},{28,32},{32,36}... | collective-permute-start | bytes 393224 | tf_op jit(solution)/shard_map/ppermute | solution.py:418
  6.9 2.8 %collective-permute-start = (f32[2,128,128]{2,1,0:T(8,128)}, f32[2,128,128]{2,1,0:T(8,128)S(1)}, u32[]{:S(2)}, u32[]{:S(2)}) collective-permute-start(f32[2,128,128]{2,1,0:T(8,128)} %bitcast.52), channel_id=1, source_target_pairs={{0,1},{1,0},{2,3},{3,2},{4,5},{5,4},{6,7},{7,6},{8,9},{9,8},{10,11... | collective-permute-start | bytes 393224 | tf_op jit(solution)/shard_map/ppermute | solution.py:412
  9.8 0.7 fusion.12
  10.5 0.8 multiply_reduce_fusion
  11.3 3.7 %collective-permute-done.1.over = f32[2,128,128]{2,1,0:T(8,128)S(1)} collective-permute-done((f32[2,128,128]{2,1,0:T(8,128)}, f32[2,128,128]{2,1,0:T(8,128)S(1)}, u32[]{:S(2)}, u32[]{:S(2)}) %collective-permute-start.1) | collective-permute-done | bytes 131104 | tf_op jit(solution)/shard_map/ppermute | solution.py:411
  14.9 1.0 collective-permute-start.2
  15.9 1.1 fusion.3
  17.1 0.0 copy-start.3
  17.1 0.0 copy-start.4
  17.2 0.0 slice-start
  17.2 9.7 %shard_map.104 = (f32[4,128,128]{2,1,0:T(8,128)S(1)}, f32[2,2,2,128,512]{4,3,2,1,0:T(8,128)S(1)}, f32[128,512]{1,0:T(8,128)S(1)}, f32[32,128]{1,0:T(8,128)S(1)}) custom-call(s32[1]{0:T(128)} %bitcast.me_ref, f32[2,128,128]{2,1,0:T(8,128)} %bitcast.54, f32[2,128,128]{2,1,0:T(8,128)S(1)} %collective-permute-done.mate, ...), custom_call_target="tpu_custom_call" | custom-call | flops 8000000000 | bytes 10000000 | tf_op jit(solution)/shard_map/pallas_call | solution.py:355
  26.9 1.3 %copy-done.6 = f32[2,2,2,128,512]{4,3,2,1,0:T(8,128)} copy-done((f32[2,2,2,128,512]{4,3,2,1,0:T(8,128)}, f32[2,2,2,128,512]{4,3,2,1,0:T(8,128)S(1)}, u32[]{:S(2)}) %copy-start.6) | copy-done | bytes 2097176
  28.2 0.7 copy-done.7
  28.9 0.0 slice-start.1
  28.9 0.0 copy-start.1
  29.0 0.0 copy-start.2
  29.0 0.0 copy-start.5
  29.0 23.5 %shard_map.107 = (f32[144,128]{1,0:T(8,128)S(1)}, f32[144,128]{1,0:T(8,128)S(1)}, f32[144,128]{1,0:T(8,128)S(1)}, f32[144,128]{1,0:T(8,128)S(1)}, f32[144,128]{1,0:T(8,128)S(1)}, /*index=5*/f32[8,128]{1,0:T(8,128)}) custom-call(s32[1]{0:T(128)} %bitcast.me_ref, f32[4,128,128]{2,1,0:T(8,128)S(1)} %get-tuple-element.31.jall, ...), custom_call_target="tpu_custom_call" | custom-call | flops 20000000000 | bytes 10000000 | tf_op jit(solution)/shard_map/pallas_call | solution.py:378
  52.5 0.1 collective-permute-start.6
  52.6 1.7 %collective-permute-start.7 = (f32[144,128]{1,0:T(8,128)S(1)}, f32[144,128]{1,0:T(8,128)}, u32[]{:S(2)}, u32[]{:S(2)}) collective-permute-start(f32[144,128]{1,0:T(8,128)S(1)} %get-tuple-element.38), channel_id=1, source_target_pairs={{0,3},{1,2},{2,1},{3,0},{4,7},{5,6},{6,5},{7,4},{8,11},{9,10},{10,... | collective-permute-start | bytes 221192 | tf_op jit(solution)/shard_map/ppermute | solution.py:435
  54.4 0.1 collective-permute-start.5
  54.5 9.3 %shard_map.105 = (f32[4,128,128]{2,1,0:T(8,128)S(1)}, f32[2,2,2,128,512]{4,3,2,1,0:T(8,128)S(1)}, f32[128,512]{1,0:T(8,128)S(1)}, f32[32,128]{1,0:T(8,128)}, f32[256,128]{1,0:T(8,128)}) custom-call(s32[1]{0:T(128)} %bitcast.me_ref, f32[2,128,128]{2,1,0:T(8,128)S(1)} %bitcast.55, f32[2,128,128]{2,1,0:T(8,128)S(1)} %collective-permute-done.mate, ...), custom_call_target="tpu_custom_call" | custom-call | flops 8000000000 | bytes 10000000 | tf_op jit(solution)/shard_map/pallas_call | solution.py:355
  63.8 16.0 %all-to-all-start = ((f32[256,1,128]{2,1,0:T(1,128)}), f32[256,1,128]{2,1,0:T(1,128)S(1)}, u32[]{:S(2)}, u32[]{:S(2)}) async-start(f32[256,1,128]{2,1,0:T(1,128)} %bitcast.4), calls=%async_computation | async-start | bytes 262144 | tf_op jit(solution)/shard_map/all_to_all | solution.py:433
  79.8 1.0 add_add_fusion.1
  80.8 11.8 %all-to-all-done = f32[256,1,128]{2,1,0:T(1,128)S(1)} async-done(((f32[256,1,128]{2,1,0:T(1,128)}), f32[256,1,128]{2,1,0:T(1,128)S(1)}, u32[]{:S(2)}, u32[]{:S(2)}) %all-to-all-start) | async-done | bytes 131104 | tf_op jit(solution)/shard_map/all_to_all | solution.py:433
  92.6 20.9 %shard_map.106 = (f32[144,128]{1,0:T(8,128)S(1)}, f32[144,128]{1,0:T(8,128)S(1)}, f32[144,128]{1,0:T(8,128)S(1)}, f32[144,128]{1,0:T(8,128)S(1)}, f32[144,128]{1,0:T(8,128)S(1)}, /*index=5*/f32[8,128]{1,0:T(8,128)S(1)}) custom-call(s32[1]{0:T(128)} %bitcast.me_ref, f32[4,128,128]{2,1,0:T(8,128)S(1)} %get-tuple-element.24.jall, ...), custom_call_target="tpu_custom_call" | custom-call | flops 20000000000 | bytes 10000000 | tf_op jit(solution)/shard_map/pallas_call | solution.py:378
  113.6 0.4 collective-permute-start.9
  113.9 2.0 %collective-permute-start.10 = (f32[144,128]{1,0:T(8,128)S(1)}, f32[144,128]{1,0:T(8,128)S(1)}, u32[]{:S(2)}, u32[]{:S(2)}) collective-permute-start(f32[144,128]{1,0:T(8,128)S(1)} %get-tuple-element.43), channel_id=1, source_target_pairs={{0,3},{1,2},{2,1},{3,0},{4,7},{5,6},{6,5},{7,4},{8,11},{9,10},{10,... | collective-permute-start | bytes 221192 | tf_op jit(solution)/shard_map/ppermute | solution.py:437
  116.0 0.5 fusion.15
  117.8 1.7 %collective-permute-done.10 = f32[144,128]{1,0:T(8,128)S(1)} collective-permute-done((f32[144,128]{1,0:T(8,128)S(1)}, f32[144,128]{1,0:T(8,128)S(1)}, u32[]{:S(2)}, u32[]{:S(2)}) %collective-permute-start.10) | collective-permute-done | bytes 73760 | tf_op jit(solution)/shard_map/ppermute | solution.py:437
  119.7 0.7 pad_maximum_fusion.2
  (37 shorter events, 0.2 us)
Async XLA Ops:
  0.6 15.3 %collective-permute-start.3 = (f32[2,2,2,2,16,128]{5,4,3,2,1,0:T(8,128)}, f32[2,2,2,2,16,128]{5,4,3,2,1,0:T(8,128)S(1)}, u32[]{:S(2)}, u32[]{:S(2)}) collective-permute-start(f32[2,2,2,2,16,128]{5,4,3,2,1,0:T(8,128)} %param.9), channel_id=1, source_target_pairs={{4,0},{8,4},{12,8},{16,12},{20,16},{24,20},{28,24},{32,28},{36,32}... | collective-permute-start | bytes 393224 | tf_op jit(solution)/shard_map/ppermute | solution.py:418
  1.9 14.0 %collective-permute-start.4 = (f32[2,2,2,2,16,128]{5,4,3,2,1,0:T(8,128)}, f32[2,2,2,2,16,128]{5,4,3,2,1,0:T(8,128)S(1)}, u32[]{:S(2)}, u32[]{:S(2)}) collective-permute-start(f32[2,2,2,2,16,128]{5,4,3,2,1,0:T(8,128)} %param.9), channel_id=1, source_target_pairs={{0,4},{4,8},{8,12},{12,16},{16,20},{20,24},{24,28},{28,32},{32,36}... | collective-permute-start | bytes 393224 | tf_op jit(solution)/shard_map/ppermute | solution.py:418
  6.9 10.2 %collective-permute-start = (f32[2,128,128]{2,1,0:T(8,128)}, f32[2,128,128]{2,1,0:T(8,128)S(1)}, u32[]{:S(2)}, u32[]{:S(2)}) collective-permute-start(f32[2,128,128]{2,1,0:T(8,128)} %bitcast.52), channel_id=1, source_target_pairs={{0,1},{1,0},{2,3},{3,2},{4,5},{5,4},{6,7},{7,6},{8,9},{9,8},{10,11... | collective-permute-start | bytes 393224 | tf_op jit(solution)/shard_map/ppermute | solution.py:412
  9.8 5.2 %collective-permute-start.1 = (f32[2,128,128]{2,1,0:T(8,128)}, f32[2,128,128]{2,1,0:T(8,128)S(1)}, u32[]{:S(2)}, u32[]{:S(2)}) collective-permute-start(f32[2,128,128]{2,1,0:T(8,128)} %bitcast.53), channel_id=1, source_target_pairs={{0,2},{1,3},{2,0},{3,1},{4,6},{5,7},{6,4},{7,5},{8,10},{9,11},{10,... | collective-permute-start | bytes 393224 | tf_op jit(solution)/shard_map/ppermute | solution.py:411
  14.9 2.2 %collective-permute-start.2 = (f32[2,128,128]{2,1,0:T(8,128)S(1)}, f32[2,128,128]{2,1,0:T(8,128)S(1)}, u32[]{:S(2)}, u32[]{:S(2)}) collective-permute-start(f32[2,128,128]{2,1,0:T(8,128)S(1)} %collective-permute-done.1.over), channel_id=1, source_target_pairs={{0,1},{1,0},{2,3},{3,2},{4,5},{5,4},{6,7},{7,6},{8,9},{9,8},{10,11... | collective-permute-start | bytes 393224 | tf_op jit(solution)/shard_map/ppermute | solution.py:413
  17.1 11.8 %copy-start.3 = (bf16[128,16]{1,0:T(8,128)(2,1)S(1)}, bf16[128,16]{1,0:T(8,128)(2,1)}, u32[]{:S(2)}) copy-start(bf16[128,16]{1,0:T(8,128)(2,1)} %constant.65.clone.w2) | copy-start | bytes 12292
  17.1 11.8 %copy-start.4 = (bf16[32,16]{1,0:T(8,128)(2,1)S(1)}, bf16[32,16]{1,0:T(8,128)(2,1)}, u32[]{:S(2)}) copy-start(bf16[32,16]{1,0:T(8,128)(2,1)} %constant.67.clone.selc) | copy-start | bytes 3076
  17.2 37.3 %slice-start = ((s8[8388608]{0:T(1024)(128)(4,1)}), s8[4194304]{0:T(1024)(128)(4,1)S(1)}, s32[]{:S(2)}) async-start(s8[8388608]{0:T(1024)(128)(4,1)} %bitcast.56), calls=%async_computation.1 | async-start | bytes 8388608
  26.9 1.3 %copy-start.6 = (f32[2,2,2,128,512]{4,3,2,1,0:T(8,128)}, f32[2,2,2,128,512]{4,3,2,1,0:T(8,128)S(1)}, u32[]{:S(2)}) copy-start(f32[2,2,2,128,512]{4,3,2,1,0:T(8,128)S(1)} %get-tuple-element.32.res_hbm) | copy-start | bytes 6291460
  28.2 0.7 copy-start.7
  28.9 25.6 %copy-start = (f32[2,2,2,2,16,128]{5,4,3,2,1,0:T(8,128)S(1)}, f32[2,2,2,2,16,128]{5,4,3,2,1,0:T(8,128)}, u32[]{:S(2)}) copy-start(f32[2,2,2,2,16,128]{5,4,3,2,1,0:T(8,128)} %param.9) | copy-start | bytes 393220
  28.9 25.6 %slice-start.1 = ((s8[8388608]{0:T(1024)(128)(4,1)}), s8[4194304]{0:T(1024)(128)(4,1)S(1)}, s32[]{:S(2)}) async-start(s8[8388608]{0:T(1024)(128)(4,1)} %bitcast.56), calls=%async_computation.2 | async-start | bytes 8388608
  28.9 25.5 %copy-start.1 = (bf16[2,2,2,2,128,512]{5,4,3,2,1,0:T(8,128)(2,1)S(1)}, bf16[2,2,2,2,128,512]{5,4,3,2,1,0:T(8,128)(2,1)}, u32[]{:S(2)}) copy-start(bf16[2,2,2,2,128,512]{5,4,3,2,1,0:T(8,128)(2,1)} %vis.3) | copy-start | bytes 6291460
  29.0 25.5 %copy-start.2 = (s32[2,8,32]{2,1,0:T(8,128)S(1)}, s32[2,8,32]{2,1,0:T(8,128)}, u32[]{:S(2)}) copy-start(s32[2,8,32]{2,1,0:T(8,128)} %flags.3) | copy-start | bytes 6148
  29.0 25.5 %copy-start.5 = (bf16[2,16,16]{2,1,0:T(8,128)(2,1)S(1)}, bf16[2,16,16]{2,1,0:T(8,128)(2,1)}, u32[]{:S(2)}) copy-start(bf16[2,16,16]{2,1,0:T(8,128)(2,1)} %constant.66.clone.sell) | copy-start | bytes 3076
  52.5 27.3 %collective-permute-start.6 = (f32[144,128]{1,0:T(8,128)S(1)}, f32[144,128]{1,0:T(8,128)S(1)}, u32[]{:S(2)}, u32[]{:S(2)}) collective-permute-start(f32[144,128]{1,0:T(8,128)S(1)} %get-tuple-element.37), channel_id=1, source_target_pairs={{0,2},{1,3},{2,0},{3,1},{4,6},{5,7},{6,4},{7,5},{8,10},{9,11},{10,... | collective-permute-start | bytes 221192 | tf_op jit(solution)/shard_map/ppermute | solution.py:435
  52.6 27.2 %collective-permute-start.7 = (f32[144,128]{1,0:T(8,128)S(1)}, f32[144,128]{1,0:T(8,128)}, u32[]{:S(2)}, u32[]{:S(2)}) collective-permute-start(f32[144,128]{1,0:T(8,128)S(1)} %get-tuple-element.38), channel_id=1, source_target_pairs={{0,3},{1,2},{2,1},{3,0},{4,7},{5,6},{6,5},{7,4},{8,11},{9,10},{10,... | collective-permute-start | bytes 221192 | tf_op jit(solution)/shard_map/ppermute | solution.py:435
  54.4 25.4 %collective-permute-start.5 = (f32[144,128]{1,0:T(8,128)S(1)}, f32[144,128]{1,0:T(8,128)}, u32[]{:S(2)}, u32[]{:S(2)}) collective-permute-start(f32[144,128]{1,0:T(8,128)S(1)} %get-tuple-element.36), channel_id=1, source_target_pairs={{0,1},{1,0},{2,3},{3,2},{4,5},{5,4},{6,7},{7,6},{8,9},{9,8},{10,11... | collective-permute-start | bytes 221192 | tf_op jit(solution)/shard_map/ppermute | solution.py:435
  63.8 28.9 %all-to-all-start = ((f32[256,1,128]{2,1,0:T(1,128)}), f32[256,1,128]{2,1,0:T(1,128)S(1)}, u32[]{:S(2)}, u32[]{:S(2)}) async-start(f32[256,1,128]{2,1,0:T(1,128)} %bitcast.4), calls=%async_computation | async-start | bytes 262144 | tf_op jit(solution)/shard_map/all_to_all | solution.py:433
  113.6 4.2 %collective-permute-start.9 = (f32[144,128]{1,0:T(8,128)S(1)}, f32[144,128]{1,0:T(8,128)S(1)}, u32[]{:S(2)}, u32[]{:S(2)}) collective-permute-start(f32[144,128]{1,0:T(8,128)S(1)} %get-tuple-element.42), channel_id=1, source_target_pairs={{0,2},{1,3},{2,0},{3,1},{4,6},{5,7},{6,4},{7,5},{8,10},{9,11},{10,... | collective-permute-start | bytes 221192 | tf_op jit(solution)/shard_map/ppermute | solution.py:437
  113.9 5.6 %collective-permute-start.10 = (f32[144,128]{1,0:T(8,128)S(1)}, f32[144,128]{1,0:T(8,128)S(1)}, u32[]{:S(2)}, u32[]{:S(2)}) collective-permute-start(f32[144,128]{1,0:T(8,128)S(1)} %get-tuple-element.43), channel_id=1, source_target_pairs={{0,3},{1,2},{2,1},{3,0},{4,7},{5,6},{6,5},{7,4},{8,11},{9,10},{10,... | collective-permute-start | bytes 221192 | tf_op jit(solution)/shard_map/ppermute | solution.py:437
  115.9 3.6 %collective-permute-start.8 = (f32[144,128]{1,0:T(8,128)S(1)}, f32[144,128]{1,0:T(8,128)S(1)}, u32[]{:S(2)}, u32[]{:S(2)}) collective-permute-start(f32[144,128]{1,0:T(8,128)S(1)} %get-tuple-element.41), channel_id=1, source_target_pairs={{0,1},{1,0},{2,3},{3,2},{4,5},{5,4},{6,7},{7,6},{8,9},{9,8},{10,11... | collective-permute-start | bytes 221192 | tf_op jit(solution)/shard_map/ppermute | solution.py:437
